TPU v7x, 32 devices: a whole 2x2x4 slice. The times are simulated.
32 devices in a mesh: fsdp: 32 (over z, y, x, core).
Axes of the slice: x: 2, y: 2, z: 4, core: 2. Of those that a mesh axis runs over, the one named last changes fastest.
Arguments:
- block_input: bfloat16 [32768, 768], P('fsdp'), may hold values from -6 to 6
- seg_ids: int32 [64, 512], P('fsdp'), may hold values from 0 to 3, never falling along the last dimension, each value on 1 to 256 neighbouring positions
- masked: int32 [64, 512], P('fsdp'), may hold values 0 or 1
- out_grad: bfloat16 [32768, 768], P('fsdp'), may hold values from -6 to 6
- att_master: float32 [18496, 128], P('fsdp'), may hold values from -3 to 3, as said below
- att_moment: float32 [18496, 128], P('fsdp'), as said below
- att_average: float32 [18496, 128], P('fsdp'), may hold values from -3 to 3, as said below
- ffn_master: float32 [36928, 128], P('fsdp'), may hold values from -1 to 2, as said below
- ffn_moment: float32 [36928, 128], P('fsdp'), as said below
- ffn_average: float32 [36928, 128], P('fsdp'), may hold values from -1 to 2, as said below
Outputs:
- block_output: bfloat16 [32768, 768], P('fsdp')
- input_grad: float32 [32768, 768], P('fsdp')
- att_master_new: float32 [18496, 128], P('fsdp')
- att_moment_new: float32 [18496, 128], P('fsdp')
- att_average_new: float32 [18496, 128], P('fsdp')
- att_master_low: bfloat16 [18496, 128], P('fsdp')
- ffn_master_new: float32 [36928, 128], P('fsdp')
- ffn_moment_new: float32 [36928, 128], P('fsdp')
- ffn_average_new: float32 [36928, 128], P('fsdp')
- ffn_master_low: bfloat16 [36928, 128], P('fsdp')
Inputs may be any that keep to these rules, and one draw needn't show every extreme that they name: `att_master`: entries after the first 2363904 of the vector are zero. `att_average`: entries after the first 2363904 of the vector are zero. `att_moment`: entries after the first 2363904 of the vector are zero; the others have a spread of the order of the root of 32768. `ffn_master`: entries after the first 4723968 of the vector are zero. `ffn_average`: entries after the first 4723968 of the vector are zero. `ffn_moment`: entries after the first 4723968 of the vector are zero; the others have a spread of the order of the root of 32768.
All inputs are finite; a program needn't handle non-finite values. No bound on the sum of `masked` on one device may be relied on, other than what follows from the above.
Results may differ from a plain program's by a relative error of at most 0.012.
The roundings to bfloat16 on the way count: a program that leaves them out, or rounds other values in their place, can miss the bound.
Values may be sent and summed in bfloat16 or wider, within the bound.
No kernel may reach another device: no remote copies, remote signals or barrier semaphores. Data moves between devices by JAX's collectives and lax.ppermute only.
A program may use at most 192 MiB of HBM per device.

v0:
```python
import functools
import math

import jax
import jax.numpy as jnp
from jax import lax
from jax.experimental import pallas as pl
from jax.experimental.pallas import tpu as pltpu
from jax.sharding import PartitionSpec as P

HEAD_DIM = 64
FF = 3072


EPSILON = 1e-05
MASKED_SCORE = -1e30


def layer_norm(pre_norm, gain, shift):
    center = pre_norm - jnp.mean(pre_norm, axis=-1, keepdims=True)
    spread = jnp.mean(center * center, axis=-1, keepdims=True)
    return center * lax.rsqrt(spread + EPSILON) * gain + shift


def gelu_exact(inputs):
    return jax.nn.gelu(inputs, approximate=False)


def unpack_attention(flat_att, model_width):
    square = model_width * model_width
    att_mats = flat_att[: 4 * square].reshape(4, model_width, model_width)
    small_params = flat_att[4 * square : 4 * square + 6 * model_width].reshape(6, model_width)
    return (att_mats, small_params)


def unpack_ffn(flat_ffn, model_width, hidden):
    size_in = model_width * hidden
    weight_in = flat_ffn[:size_in].reshape(model_width, hidden)
    weight_out = flat_ffn[size_in : 2 * size_in].reshape(hidden, model_width)
    offset = 2 * size_in
    bias_in = flat_ffn[offset : offset + hidden]
    small_params = flat_ffn[offset + hidden : offset + hidden + 3 * model_width].reshape(
        3, model_width
    )
    return (weight_in, weight_out, bias_in, small_params)


def pack_rows(pieces, row_count):
    filled = sum((piece.shape[0] for piece in pieces))
    padding = jnp.zeros((row_count * 128 - filled,), jnp.float32)
    return jnp.concatenate(list(pieces) + [padding]).reshape(row_count, 128)


def attend_forward(block_items):
    query_block, key_block, value_block, doc_block = block_items
    scores = jnp.einsum("qhd,khd->hqk", query_block, key_block, preferred_element_type=jnp.float32)
    same_doc = doc_block[:, None] == doc_block[None, :]
    scores = jnp.where(same_doc[None], scores, MASKED_SCORE)
    row_max = jnp.max(scores, axis=-1, keepdims=True)
    exponent = jnp.exp(scores - row_max)
    row_total = jnp.sum(exponent, axis=-1, keepdims=True)
    attn_probs = (exponent / row_total).astype(jnp.bfloat16)
    context = jnp.einsum(
        "hqk,khd->qhd", attn_probs, value_block, preferred_element_type=jnp.float32
    )
    return (context.astype(jnp.bfloat16), (row_max + jnp.log(row_total))[..., 0])


def attend_backward(block_items):
    query_block, key_block, value_block, doc_block, log_total, grad_context = block_items
    scores = jnp.einsum("qhd,khd->hqk", query_block, key_block, preferred_element_type=jnp.float32)
    same_doc = doc_block[:, None] == doc_block[None, :]
    scores = jnp.where(same_doc[None], scores, MASKED_SCORE)
    attn_probs = jnp.exp(scores - log_total[..., None])
    probs_low = attn_probs.astype(jnp.bfloat16)
    grad_probs = jnp.einsum(
        "qhd,khd->hqk", grad_context, value_block, preferred_element_type=jnp.float32
    )
    row_inner = jnp.sum(grad_probs * attn_probs, axis=-1, keepdims=True)
    grad_scores = (attn_probs * (grad_probs - row_inner)).astype(jnp.bfloat16)
    grad_query = jnp.einsum(
        "hqk,khd->qhd", grad_scores, key_block, preferred_element_type=jnp.float32
    ).astype(jnp.bfloat16)
    grad_key = jnp.einsum(
        "hqk,qhd->khd", grad_scores, query_block, preferred_element_type=jnp.float32
    ).astype(jnp.bfloat16)
    grad_value = jnp.einsum(
        "hqk,qhd->khd", probs_low, grad_context, preferred_element_type=jnp.float32
    ).astype(jnp.bfloat16)
    return (grad_query, grad_key, grad_value)


def nesterov(master, moment, average, gradient, step_rate):
    moment_new = 0.5 * moment + gradient
    master_new = master - step_rate * (gradient + 0.5 * moment_new)
    average_new = 0.5 * average + 0.5 * master_new
    return (master_new, moment_new, average_new, master_new.astype(jnp.bfloat16))


def local(
    block_input,
    seg_ids,
    masked,
    out_grad,
    att_master,
    att_moment,
    att_average,
    ffn_master,
    ffn_moment,
    ffn_average,
):
    tok_rows, model_width = block_input.shape
    seq_count, seq_length = seg_ids.shape
    head_count = model_width // HEAD_DIM
    devices = lax.axis_size("fsdp")
    att_rows = att_master.shape[0] * devices
    ffn_rows = ffn_master.shape[0] * devices
    head_shape = (seq_count, seq_length, head_count, HEAD_DIM)
    att_whole = lax.all_gather(att_master.astype(jnp.bfloat16), "fsdp", axis=0, tiled=True)
    att_mats, att_small_low = unpack_attention(att_whole.reshape(-1), model_width)
    att_small = att_small_low.astype(jnp.float32)
    masked_rows = masked.reshape(tok_rows, 1) == 1
    stream_in = jnp.where(masked_rows, att_small[5][None, :], block_input.astype(jnp.float32))
    stream_low = stream_in.astype(jnp.bfloat16)
    projected = jnp.einsum(
        "td,cde->cte", stream_low, att_mats[:3], preferred_element_type=jnp.float32
    )
    queries = ((projected[0] + att_small[0]) * 0.125).astype(jnp.bfloat16).reshape(head_shape)
    key_rows = projected[1].astype(jnp.bfloat16).reshape(head_shape)
    values = (projected[2] + att_small[1]).astype(jnp.bfloat16).reshape(head_shape)
    context, log_total = lax.map(attend_forward, (queries, key_rows, values, seg_ids))
    context_flat = context.reshape(tok_rows, model_width)
    pre_one = (
        stream_in
        + jnp.dot(context_flat, att_mats[3], preferred_element_type=jnp.float32)
        + att_small[2]
    )
    normed_one = layer_norm(pre_one, att_small[3], att_small[4])
    normed_low = normed_one.astype(jnp.bfloat16)
    ffn_whole = lax.all_gather(ffn_master.astype(jnp.bfloat16), "fsdp", axis=0, tiled=True)
    weight_in, weight_out, bias_in_low, ffn_small_low = unpack_ffn(
        ffn_whole.reshape(-1), model_width, FF
    )
    bias_in = bias_in_low.astype(jnp.float32)
    ffn_small = ffn_small_low.astype(jnp.float32)
    hid_pre = jnp.dot(normed_low, weight_in, preferred_element_type=jnp.float32) + bias_in
    hid_act = gelu_exact(hid_pre).astype(jnp.bfloat16)
    pre_two = (
        normed_one + jnp.dot(hid_act, weight_out, preferred_element_type=jnp.float32) + ffn_small[0]
    )
    normed_two, norm_two_pull = jax.vjp(layer_norm, pre_two, ffn_small[1], ffn_small[2])
    block_output = normed_two.astype(jnp.bfloat16)
    ffn_back = lax.all_gather(ffn_master.astype(jnp.bfloat16), "fsdp", axis=0, tiled=True)
    back_in, back_out, bias_unused, small_unused = unpack_ffn(ffn_back.reshape(-1), model_width, FF)
    grad_pre_two, grad_gain_two, grad_shift_two = norm_two_pull(out_grad.astype(jnp.float32))
    grad_branch_two = grad_pre_two.astype(jnp.bfloat16)
    grad_w_out = jnp.einsum(
        "tf,td->fd", hid_act, grad_branch_two, preferred_element_type=jnp.float32
    )
    grad_b_out = jnp.sum(grad_branch_two, axis=0, dtype=jnp.float32)
    grad_act = jnp.einsum(
        "td,fd->tf", grad_branch_two, back_out, preferred_element_type=jnp.float32
    )
    hid_unused, gelu_pull = jax.vjp(gelu_exact, hid_pre)
    grad_hidden = gelu_pull(grad_act)[0].astype(jnp.bfloat16)
    grad_w_in = jnp.einsum("td,tf->df", normed_low, grad_hidden, preferred_element_type=jnp.float32)
    grad_b_in = jnp.sum(grad_hidden, axis=0, dtype=jnp.float32)
    grad_normed_one = grad_pre_two + jnp.einsum(
        "tf,df->td", grad_hidden, back_in, preferred_element_type=jnp.float32
    )
    ffn_flat_grad = pack_rows(
        (
            grad_w_in.reshape(-1),
            grad_w_out.reshape(-1),
            grad_b_in,
            grad_b_out,
            grad_gain_two,
            grad_shift_two,
        ),
        ffn_rows,
    )
    ffn_grad = lax.psum_scatter(ffn_flat_grad, "fsdp", scatter_dimension=0, tiled=True)
    att_back = lax.all_gather(att_master.astype(jnp.bfloat16), "fsdp", axis=0, tiled=True)
    back_mats, small_back = unpack_attention(att_back.reshape(-1), model_width)
    pre_unused, norm_one_pull = jax.vjp(layer_norm, pre_one, att_small[3], att_small[4])
    grad_pre_one, grad_gain_one, grad_shift_one = norm_one_pull(grad_normed_one)
    grad_branch_one = grad_pre_one.astype(jnp.bfloat16)
    grad_w_o = jnp.einsum(
        "td,te->de", context_flat, grad_branch_one, preferred_element_type=jnp.float32
    )
    grad_b_o = jnp.sum(grad_branch_one, axis=0, dtype=jnp.float32)
    grad_context = jnp.einsum(
        "te,de->td", grad_branch_one, back_mats[3], preferred_element_type=jnp.float32
    ).astype(jnp.bfloat16)
    grad_q4, grad_k4, grad_v4 = lax.map(
        attend_backward,
        (queries, key_rows, values, seg_ids, log_total, grad_context.reshape(head_shape)),
    )
    grad_queries = grad_q4.reshape(tok_rows, model_width) * 0.125
    grad_keys = grad_k4.reshape(tok_rows, model_width)
    grad_values = grad_v4.reshape(tok_rows, model_width)
    grad_projected = jnp.stack([grad_queries, grad_keys, grad_values])
    grad_w_qkv = jnp.einsum(
        "td,cte->cde", stream_low, grad_projected, preferred_element_type=jnp.float32
    )
    grad_b_q = jnp.sum(grad_queries, axis=0, dtype=jnp.float32)
    grad_b_v = jnp.sum(grad_values, axis=0, dtype=jnp.float32)
    grad_stream = grad_pre_one + jnp.einsum(
        "cte,cde->td", grad_projected, back_mats[:3], preferred_element_type=jnp.float32
    )
    grad_mask_vector = jnp.sum(jnp.where(masked_rows, grad_stream, 0.0), axis=0)
    input_grad = jnp.where(masked_rows, 0.0, grad_stream)
    att_flat_grad = pack_rows(
        (
            grad_w_qkv.reshape(-1),
            grad_w_o.reshape(-1),
            grad_b_q,
            grad_b_v,
            grad_b_o,
            grad_gain_one,
            grad_shift_one,
            grad_mask_vector,
        ),
        att_rows,
    )
    att_grad = lax.psum_scatter(att_flat_grad, "fsdp", scatter_dimension=0, tiled=True)
    step_rate = 0.05 / math.sqrt(tok_rows * devices)
    att_new = nesterov(att_master, att_moment, att_average, att_grad, step_rate)
    ffn_new = nesterov(ffn_master, ffn_moment, ffn_average, ffn_grad, step_rate)
    return (
        block_output,
        input_grad,
        att_new[0],
        att_new[1],
        att_new[2],
        att_new[3],
        ffn_new[0],
        ffn_new[1],
        ffn_new[2],
        ffn_new[3],
    )


BF = jnp.bfloat16
F32 = jnp.float32
LANES = 128
SLOT = 96
TILE = 256
FFN_TILE = 512
FFN_SPLIT = 2
FWD_PAIRS = 1
BWD_PAIRS = 2
EXTRA = 16
MIB = 1 << 20
BIG = 58


def params(limit):
    return pltpu.CompilerParams(vmem_limit_bytes=limit * MIB)


def spec_any():
    return pl.BlockSpec(memory_space=pl.ANY)


def spec_vmem():
    return pl.BlockSpec(memory_space=pltpu.VMEM)


def spec_whole(shape):
    return pl.BlockSpec(shape, lambda *ids: (0,) * len(shape))


def dot_nn(left, right):
    return lax.dot_general(left, right, (((1,), (0,)), ((), ())), preferred_element_type=F32)


def dot_nt(left, right):
    return lax.dot_general(left, right, (((1,), (1,)), ((), ())), preferred_element_type=F32)


def dot_tn(left, right):
    return lax.dot_general(left, right, (((0,), (0,)), ((), ())), preferred_element_type=F32)


def slot_of(chunk, me, late=False):
    diff = lax.bitwise_xor(me, chunk)
    far_core = lax.bitwise_and(diff, 1)
    x_bit = lax.bitwise_and(lax.shift_right_logical(diff, 1), 1)
    y_bit = lax.bitwise_and(lax.shift_right_logical(diff, 2), 1)
    z_low = lax.bitwise_and(lax.shift_right_logical(diff, 3), 1)
    z_high = lax.shift_right_logical(diff, 4)
    core = lax.bitwise_xor(lax.bitwise_and(me, 1), far_core)
    third = x_bit + core * (y_bit - x_bit)
    fourth = y_bit + core * (x_bit - y_bit)
    if late:
        return far_core, z_high + 2 * third + 4 * z_low + 8 * fourth
    return far_core, z_high + 2 * z_low + 4 * third + 8 * fourth


def bit(value, place):
    return lax.bitwise_and(lax.shift_right_logical(value, place), 1)


def chunk_of(part, slot, me, late=False):
    third, z_low = (bit(slot, 1), bit(slot, 2)) if late else (bit(slot, 2), bit(slot, 1))
    far_core, fourth = part >> 1, part & 1
    rest = far_core + 8 * z_low + 16 * bit(slot, 0)
    first_core = rest + 2 * third + 4 * fourth
    other_core = rest + 4 * third + 2 * fourth
    core = lax.bitwise_xor(bit(me, 0), far_core)
    return lax.bitwise_xor(me, first_core + core * (other_core - first_core))


def stage_perm(stage):
    if stage == 0:
        return [(i, i ^ 16) for i in range(32)]
    if stage == 1:
        return [(i, i ^ 8) for i in range(32)]
    if stage == 2:
        return [(i, i ^ (4 if i & 1 else 2)) for i in range(32)]
    if stage == 3:
        return [(i, i ^ (2 if i & 1 else 4)) for i in range(32)]
    return [(i, i ^ 1) for i in range(32)]


def exchange(array, stage):
    return lax.ppermute(array, "fsdp", stage_perm(stage))


def widen(held, got):
    return jnp.concatenate([held, got])


def widen_small(held, got):
    low = held.shape[0] - EXTRA
    small = held[low:] + got[low:]
    return jnp.concatenate([held[:low], got[:low], small])


def total_of(arrays, first, last):
    total = arrays[0][first:last].astype(F32)
    for array in arrays[1:]:
        total = total + array[first:last].astype(F32)
    return total


def halve(*arrays):
    rows = arrays[0].shape[0]
    low = total_of(arrays, 0, rows // 2).astype(BF)
    return low, total_of(arrays, rows // 2, rows).astype(BF)


def add_small(values, small):
    return jnp.concatenate([values, small.astype(BF)])


def phase(*values):
    return lax.optimization_barrier(values)


def tail_kernel(att_ref, ffn_ref, out_ref, buf, sems):
    refs = (att_ref, ffn_ref)
    starts = [(ref.shape[0] - 64) // 8 * 8 for ref in refs]
    copies = []
    for number in range(2):
        rows = refs[number].shape[0] - starts[number]
        src = refs[number].at[starts[number] :, :]
        copies.append(pltpu.make_async_copy(src, buf.at[number, 0:rows, :], sems.at[number]))
        copies[number].start()
    for number in range(2):
        rows = refs[number].shape[0] - starts[number]
        copies[number].wait()
        out_ref[number * 64 : number * 64 + 64, :] = buf[number, rows - 64 : rows, :]


def row_tails(att_master, ffn_master):
    return pl.pallas_call(
        tail_kernel,
        out_shape=jax.ShapeDtypeStruct((128, LANES), F32),
        in_specs=[spec_any()] * 2,
        out_specs=spec_vmem(),
        scratch_shapes=[pltpu.VMEM((2, 72, LANES), F32), pltpu.SemaphoreType.DMA((2,))],
        compiler_params=params(BIG),
        name="row_tails",
    )(att_master, ffn_master)


def prep_kernel(last, att_mats, ffn_mats, att_ref, ffn_ref, tail_ref, *refs):
    att_out, ffn_a, ffn_b, att_buf, ffn_buf = refs
    me = lax.axis_index("fsdp")
    att_rows = att_ref.shape[0]
    ffn_rows = ffn_ref.shape[0]
    att_buf[0:64, :] = tail_ref[0:64, :]
    att_buf[64 : 64 + att_rows, :] = att_ref[...]
    ffn_buf[0:64, :] = tail_ref[64:128, :]
    ffn_buf[64 : 64 + ffn_rows, :] = ffn_ref[...]
    start = 64 - 2 * me
    for part in range(6):
        cols = slice(part * LANES, (part + 1) * LANES)
        att_out[0:SLOT, cols] = att_buf[pl.ds(start + part, SLOT, stride=6), :].astype(BF)
    att_out[SLOT:, :] = jnp.zeros((EXTRA, att_out.shape[1]), BF)
    first = me < 16

    @pl.when(first)
    def _():
        for block in range(4):
            out = ffn_a if block < 2 else ffn_b
            rows = slice((block % 2) * 48, (block % 2) * 48 + 48)
            for part in range(6):
                cols = slice(part * LANES, (part + 1) * LANES)
                piece = ffn_buf[pl.ds(start + 6 * block + part, 48, stride=24), :]
                out[rows, cols] = piece.astype(BF)

    @pl.when(jnp.logical_not(first))
    def _():
        for part in range(6):
            cols = slice(part * LANES, (part + 1) * LANES)
            ffn_a[:, cols] = ffn_buf[pl.ds(start + part, SLOT, stride=6), :].astype(BF)
            ffn_b[:, cols] = ffn_buf[pl.ds(start + 6 * SLOT + part, SLOT, stride=6), :].astype(BF)

    @pl.when(me == last)
    def _():
        att_at = 64 + att_mats - last * att_rows
        ffn_at = 64 + ffn_mats - last * ffn_rows
        for part in range(6):
            cols = slice(part * LANES, (part + 1) * LANES)
            upper = att_buf[pl.ds(att_at + part, 6, stride=6), :]
            lower = ffn_buf[pl.ds(ffn_at + part, 7, stride=6), :]
            both = jnp.concatenate([upper, lower, jnp.zeros((3, LANES), F32)])
            att_out[SLOT:, cols] = both.astype(BF)


def prepare(att_master, ffn_master, tails, devices, width):
    att_mats = 4 * width * width // LANES
    ffn_mats = 2 * width * FF // LANES
    att_rows, ffn_rows = att_master.shape[0], ffn_master.shape[0]
    body = functools.partial(prep_kernel, devices - 1, att_mats, ffn_mats)
    return pl.pallas_call(
        body,
        out_shape=(
            jax.ShapeDtypeStruct((SLOT + EXTRA, width), BF),
            jax.ShapeDtypeStruct((SLOT, width), BF),
            jax.ShapeDtypeStruct((SLOT, width), BF),
        ),
        in_specs=[spec_vmem()] * 3,
        out_specs=(spec_vmem(),) * 3,
        scratch_shapes=[
            pltpu.VMEM((64 + att_rows + 6, LANES), F32),
            pltpu.VMEM((64 + ffn_rows + 6, LANES), F32),
        ],
        compiler_params=params(16),
        name="prep",
    )(att_master, ffn_master, tails)


def pick(index, refs, use):
    for number in range(len(refs)):

        @pl.when(index == number)
        def _():
            use(refs[number])


def each_slot(body):
    def step(slot, carry):
        for part in range(4):
            body(part, slot)
        return carry

    lax.fori_loop(0, 8, step, 0)


def load_projections(quad, dst, sems):
    me = lax.axis_index("fsdp")

    def body(part, slot):
        chunk = chunk_of(part, slot, me)

        @pl.when(chunk < 24)
        def _():
            at = pl.multiple_of(chunk * SLOT, 32)
            src = quad[part].at[pl.ds(pl.multiple_of(slot * SLOT, 32), SLOT), :]
            sem = sems.at[lax.shift_right_logical(chunk, 3)]
            pltpu.make_async_copy(src, dst.at[pl.ds(at, SLOT), :], sem).start()

    each_slot(body)


def load_output(quad, dst, sem):
    me = lax.axis_index("fsdp")
    planes = (1 - bit(me, 4)) + 2 * (1 - bit(me, 3))

    def step(third, carry):
        slot = planes + 4 * third
        for part in range(4):
            at = pl.multiple_of((chunk_of(part, slot, me) - 24) * SLOT, 32)
            src = quad[part].at[pl.ds(pl.multiple_of(slot * SLOT, 32), SLOT), :]
            pltpu.make_async_copy(src, dst.at[pl.ds(at, SLOT), :], sem).start()
        return carry

    lax.fori_loop(0, 2, step, 0)


def load_ffn(quads, w_in, w_out, sem_in, sem_out):
    me = lax.axis_index("fsdp")
    for unit in range(2):

        def body(part, slot):
            chunk = chunk_of(part, slot, me, unit == 1)
            src = quads[unit][part].at[slot]

            @pl.when(chunk < 16)
            def _():
                at = pl.multiple_of(chunk * 48, 16)
                dst = w_in.at[2 * unit : 2 * unit + 2, pl.ds(at, 48), :]
                pltpu.make_async_copy(src, dst, sem_in.at[unit]).start()

            @pl.when(chunk >= 16)
            def _():
                dst = w_out.at[2 * (chunk - 16) + unit]
                pltpu.make_async_copy(src, dst, sem_out).start()

        each_slot(body)


def wait_whole(ref, sem):
    pltpu.make_async_copy(ref, ref, sem).wait()


def as_column(row):
    return jnp.broadcast_to(row.astype(F32), (8, row.shape[1])).T[:, 0:1]


def head_mask(rows):
    lane = lax.broadcasted_iota(jnp.int32, (rows, LANES), 1)
    return lane < HEAD_DIM


def project_kernel(x_ref, masked_ref, *refs):
    quad = refs[0:4]
    stream_ref, qkv_ref, small_ref, weights, smalls, sems, small_sem = refs[4:]
    width = x_ref.shape[1]

    @pl.when(pl.program_id(0) == 0)
    def _():
        for part in range(4):
            src = quad[part].at[pl.ds(8 * SLOT, EXTRA), :]
            pltpu.make_async_copy(src, smalls.at[part], small_sem).start()
        load_projections(quad, weights, sems)
        wait_whole(smalls, small_sem)
        total = smalls[0].astype(F32)
        for part in range(1, 4):
            total = total + smalls[part].astype(F32)
        small_ref[...] = total

    small = small_ref[...]
    stream = jnp.where(as_column(masked_ref[0]) == 1.0, small[5:6], x_ref[...].astype(F32)).astype(BF)
    stream_ref[...] = stream

    def body(matrix, carry):
        rows = pl.ds(pl.multiple_of(matrix * width, width), width)

        @pl.when(pl.program_id(0) == 0)
        def _():
            wait_whole(weights.at[rows], sems.at[matrix])

        odd = lax.rem(matrix, 2)
        bias = small_ref[pl.ds(lax.div(matrix, 2), 1), :] * (1.0 - odd.astype(F32))
        scale = jnp.where(matrix == 0, 0.125, 1.0)
        product = dot_nn(stream_ref[...], weights[rows])
        qkv_ref[matrix] = ((product + bias) * scale).astype(BF)
        return carry

    lax.fori_loop(0, 3, body, 0)


def project(block_input, masked_row, quad):
    tok, width = block_input.shape
    rows = masked_row.shape[2]
    tile = lambda cols: pl.BlockSpec((rows, cols), lambda s: (s, 0))
    bf = jax.ShapeDtypeStruct((tok, width), BF)
    return pl.pallas_call(
        project_kernel,
        grid=(tok // rows,),
        out_shape=(
            bf,
            jax.ShapeDtypeStruct((3, tok, width), BF),
            jax.ShapeDtypeStruct((EXTRA, width), F32),
        ),
        in_specs=[tile(width), pl.BlockSpec((1, 1, rows), lambda s: (s, 0, 0))] + [spec_any()] * 4,
        out_specs=(
            tile(width),
            pl.BlockSpec((3, rows, width), lambda s: (0, s, 0)),
            spec_whole((EXTRA, width)),
        ),
        scratch_shapes=[
            pltpu.VMEM((3 * width, width), BF),
            pltpu.VMEM((4, EXTRA, width), BF),
            pltpu.SemaphoreType.DMA((3,)),
            pltpu.SemaphoreType.DMA,
        ],
        compiler_params=params(BIG),
        cost_estimate=pl.CostEstimate(
            flops=6 * tok * width * width, bytes_accessed=16 * MIB, transcendentals=0
        ),
        name="project",
    )(block_input, masked_row, *quad)


def forward_kernel(held, q_ref, k_ref, v_ref, seg_row_ref, *refs):
    ctx_ref, lse_ref = refs[held:]
    left = head_mask(q_ref.shape[0])
    same = as_column(seg_row_ref[0]) == seg_row_ref[0].astype(F32)
    for pair in range(FWD_PAIRS):
        cols = slice(pair * LANES, (pair + 1) * LANES)
        queries = q_ref[:, cols]
        keys = k_ref[:, cols]
        values_t = v_ref[:, cols].T
        outs = []
        for head in range(2):
            keep = left if head == 0 else jnp.logical_not(left)
            own = jnp.where(keep, queries, jnp.zeros_like(queries))
            scores = jnp.where(same, dot_nt(keys, own), MASKED_SCORE)
            top = jnp.max(scores, axis=0, keepdims=True)
            exponent = jnp.exp(scores - top)
            total = jnp.sum(exponent, axis=0, keepdims=True)
            probs = (exponent * (1.0 / total)).astype(BF)
            lse_ref[0, pair, head : head + 1, :] = top + jnp.log(total)
            outs.append(dot_nn(values_t[head * HEAD_DIM : (head + 1) * HEAD_DIM], probs))
        ctx_ref[:, cols] = jnp.concatenate(outs).T.astype(BF)


def sequence_specs(at, seq, pairs):
    tile = lambda: pl.BlockSpec((seq, pairs * LANES), lambda i: (at, i))
    row = lambda: pl.BlockSpec((1, 1, seq), lambda i: (at, 0, 0))
    part = lambda which: pl.BlockSpec((None, seq, pairs * LANES), lambda i: (which, at, i))
    stat = lambda: pl.BlockSpec((1, pairs, 2, seq), lambda i: (at, i, 0, 0))
    return tile, row, stat, [part(0), part(1), part(2)]


def attention_forward(at, qkv, seg_row, held=()):
    tok, width = qkv.shape[1:]
    seq_count, seq = seg_row.shape[0], seg_row.shape[2]
    pairs = width // LANES
    tile, row, stat, parts = sequence_specs(at, seq, FWD_PAIRS)
    return pl.pallas_call(
        functools.partial(forward_kernel, len(held)),
        grid=(pairs // FWD_PAIRS,),
        out_shape=(
            jax.ShapeDtypeStruct((tok, width), BF),
            jax.ShapeDtypeStruct((seq_count, pairs, 2, seq), F32),
        ),
        in_specs=parts + [row()] + [spec_any() for _ in held],
        out_specs=(tile(), stat()),
        input_output_aliases={4 + i: i for i in range(len(held))},
        compiler_params=params(BIG),
        cost_estimate=pl.CostEstimate(
            flops=16 * seq * seq * width,
            bytes_accessed=4 * MIB,
            transcendentals=seq * seq * width // HEAD_DIM,
        ),
        name="attention_forward",
    )(qkv, qkv, qkv, seg_row, *held)


def norm_stats(pre_norm):
    center = pre_norm - jnp.mean(pre_norm, axis=-1, keepdims=True)
    scale = lax.rsqrt(jnp.mean(center * center, axis=-1, keepdims=True) + EPSILON)
    return center * scale, scale


def norm_back(grad, gain, normed, scale):
    scaled = grad * gain
    mean_one = jnp.mean(scaled, axis=-1, keepdims=True)
    mean_two = jnp.mean(scaled * normed, axis=-1, keepdims=True)
    return scale * (scaled - mean_one - normed * mean_two)


def column_sum(array):
    return jnp.sum(array, axis=0, keepdims=True)


def gelu_pair(inputs):
    phi_cdf = 0.5 + 0.5 * lax.erf(inputs * math.sqrt(0.5))
    density = jnp.exp(inputs * inputs * -0.5) * (1.0 / math.sqrt(2.0 * math.pi))
    return inputs * phi_cdf, phi_cdf + inputs * density


def ffn_kernel(
    stream_ref,
    ctx_ref,
    grad_ref,
    small_ref,
    *refs,
):
    att_quad, quad_a, quad_b = refs[0:4], refs[4:8], refs[8:12]
    y_ref, x1_ref, hid_ref, dhid_ref, dfb_ref, dob_ref, dctx_ref, sums_ref = refs[12:20]
    w_in, w_out, w_o, slope, sem_in, sem_out, sem_o = refs[20:]
    width = ctx_ref.shape[1]
    step = pl.program_id(0)

    @pl.when(step == 0)
    def _():
        load_output(att_quad, w_o, sem_o)
        load_ffn((quad_a, quad_b), w_in, w_out, sem_in, sem_out)
        sums_ref[...] = jnp.zeros_like(sums_ref)
        wait_whole(w_o, sem_o)

    def block_cols(block):
        return slice(block * width, (block + 1) * width)

    def out_rows(block):
        return w_out[8 * block : 8 * block + 8].reshape(width, width)

    @pl.when(step == 0)
    def _():
        wait_whole(w_in.at[0:2], sem_in.at[0])
        wait_whole(w_in.at[2:4], sem_in.at[1])
        wait_whole(w_out, sem_out)

    small = small_ref[...]
    halves = range(FFN_SPLIT)
    size = FFN_TILE // FFN_SPLIT
    rows = [slice(part * size, (part + 1) * size) for part in halves]
    state = [{} for part in halves]

    def first_norm(part):
        own = state[part]
        pre_one = stream_ref[rows[part]].astype(F32) + dot_nn(ctx_ref[rows[part]], w_o[...])
        normed, own["scale"] = norm_stats(pre_one + small[2:3])
        own["normed"] = normed
        x_one = normed * small[3:4] + small[4:5]
        own["x"] = x_one.astype(BF)
        x1_ref[rows[part]] = own["x"]
        own["total"] = x_one + small[10:11]

    def forward(part, block):
        own = state[part]
        product = dot_nn(own["x"], w_in[block])
        hidden, gate = gelu_pair(product + small[6 + block : 7 + block])
        hidden = hidden.astype(BF)
        hid_ref[rows[part], block_cols(block)] = hidden
        slope[block, rows[part]] = gate
        own["total"] = own["total"] + dot_nn(hidden, out_rows(block))

    def second_norm(part):
        own = state[part]
        normed, scale = norm_stats(own["total"])
        y_ref[rows[part]] = (normed * small[11:12] + small[12:13]).astype(BF)
        grad_out = grad_ref[rows[part]].astype(F32)
        grad_two = norm_back(grad_out, small[11:12], normed, scale)
        own["low"] = grad_two.astype(BF)
        own["grad"] = grad_two
        dfb_ref[rows[part]] = own["low"]
        sums_ref[10:11] += column_sum(own["low"].astype(F32))
        sums_ref[11:12] += column_sum(grad_out * normed)
        sums_ref[12:13] += column_sum(grad_out)

    def backward(part, block):
        own = state[part]
        product = dot_nt(own["low"], out_rows(block))
        dhid = (product * slope[block, rows[part]]).astype(BF)
        dhid_ref[rows[part], block_cols(block)] = dhid
        sums_ref[6 + block : 7 + block] += column_sum(dhid.astype(F32))
        own["grad"] = own["grad"] + dot_nt(dhid, w_in[block])

    def last_norm(part):
        own = state[part]
        grad_one = own["grad"]
        sums_ref[3:4] += column_sum(grad_one * own["normed"])
        sums_ref[4:5] += column_sum(grad_one)
        dob = norm_back(grad_one, small[3:4], own["normed"], own["scale"]).astype(BF)
        dob_ref[rows[part]] = dob
        sums_ref[2:3] += column_sum(dob.astype(F32))
        dctx_ref[rows[part]] = dot_nt(dob, w_o[...]).astype(BF)

    for part in halves:
        first_norm(part)
    for block in range(FF // width):
        for part in halves:
            forward(part, block)
    for part in halves:
        second_norm(part)
    for block in range(FF // width):
        for part in halves:
            backward(part, block)
    for part in halves:
        last_norm(part)


def feed_forward(stream, ctx, out_grad, small, att_quad, quad_a, quad_b):
    tok, width = ctx.shape
    slots = (8, 2, 48, width)
    quad_a = [array.reshape(slots) for array in quad_a]
    quad_b = [array.reshape(slots) for array in quad_b]
    tile = lambda cols: pl.BlockSpec((FFN_TILE, cols), lambda i: (i, 0))
    bf = lambda cols: jax.ShapeDtypeStruct((tok, cols), BF)
    return pl.pallas_call(
        ffn_kernel,
        grid=(tok // FFN_TILE,),
        out_shape=(
            bf(width),
            bf(width),
            bf(FF),
            bf(FF),
            bf(width),
            bf(width),
            bf(width),
            jax.ShapeDtypeStruct((EXTRA, width), F32),
        ),
        in_specs=[tile(width)] * 3 + [spec_whole((EXTRA, width))] + [spec_any()] * 12,
        out_specs=(
            tile(width),
            tile(width),
            tile(FF),
            tile(FF),
            tile(width),
            tile(width),
            tile(width),
            spec_whole((EXTRA, width)),
        ),
        scratch_shapes=[
            pltpu.VMEM((FF // width, width, width), BF),
            pltpu.VMEM((FF // SLOT, 2, 48, width), BF),
            pltpu.VMEM((width, width), BF),
            pltpu.VMEM((FF // width, FFN_TILE, width), F32),
            pltpu.SemaphoreType.DMA((2,)),
            pltpu.SemaphoreType.DMA,
            pltpu.SemaphoreType.DMA,
        ],
        compiler_params=params(BIG),
        cost_estimate=pl.CostEstimate(
            flops=8 * tok * width * FF, bytes_accessed=40 * MIB, transcendentals=2 * tok * FF
        ),
        name="feed_forward",
    )(stream, ctx, out_grad, small, *att_quad, *quad_a, *quad_b)


def send_slot(parts, far_core, slot, offset, src, sem):
    at = pl.multiple_of(lax.bitwise_and(slot, 7) * SLOT + offset, 16)

    def copy(ref):
        pltpu.make_async_copy(src, ref.at[pl.ds(at, src.shape[0]), :], sem).start()

    pick(2 * far_core + lax.shift_right_logical(slot, 3), parts, copy)


def part_shapes(width, small):
    rows = [8 * SLOT, 8 * SLOT, 8 * SLOT, 8 * SLOT + (EXTRA if small else 0)]
    return tuple(jax.ShapeDtypeStruct((count, width), BF) for count in rows)


def wait_reuse(stage, sems, buf, step):
    @pl.when(step >= 2)
    def _():
        wait_whole(stage.at[buf], sems.at[buf])


def wait_last(stage, sems, step, steps):
    @pl.when(step == steps - 1)
    def _():
        for buf in range(2):
            wait_whole(stage.at[buf], sems.at[buf])


def send_in_blocks(parts, me, late, part, stage, buf, sem):
    def body(chunk, carry):
        far_core, slot = slot_of(chunk, me, late)
        src = stage.at[buf, pl.ds(pl.multiple_of(chunk * 48, 16), 48)]
        send_slot(parts, far_core, slot, part * 48, src, sem)
        return carry

    lax.fori_loop(0, 16, body, 0)


def ffn_grad_kernel(x_ref, hid_ref, dhid_ref, dfb_ref, sums_ref, *refs):
    parts_a, parts_b = refs[0:4], refs[4:8]
    held, stage, small_stage, held_sem, sems, small_sem = refs[8:]
    width = x_ref.shape[1]
    me = lax.axis_index("fsdp")
    step = pl.program_id(0)
    buf = lax.rem(step, 2)
    small_rows = parts_b[3].at[pl.ds(8 * SLOT, EXTRA), :]

    def fetch(index):
        into, sem = held.at[2 + lax.rem(index, 2)], held_sem.at[2 + lax.rem(index, 2)]

        def start(ref, block):
            at = pl.multiple_of(block * width, LANES)
            pltpu.make_async_copy(ref.at[:, pl.ds(at, width)], into, sem).start()

        @pl.when(index < 4)
        def _():
            start(hid_ref, index)

        @pl.when(index >= 4)
        def _():
            start(dhid_ref, index - 2)

    @pl.when(step == 0)
    def _():
        pltpu.make_async_copy(dfb_ref, held.at[0], held_sem.at[0]).start()
        fetch(step)
        pltpu.make_async_copy(x_ref, held.at[1], held_sem.at[1]).start()
        small_stage[...] = sums_ref[...].astype(BF)
        pltpu.make_async_copy(small_stage, small_rows, small_sem).start()
        wait_whole(held.at[0], held_sem.at[0])

    @pl.when(step < 5)
    def _():
        fetch(step + 1)

    @pl.when(step == 4)
    def _():
        wait_whole(held.at[1], held_sem.at[1])

    wait_whole(held.at[2 + buf], held_sem.at[2 + buf])
    wait_reuse(stage, sems, buf, step)
    second = lax.div(step, 4)
    left = (2 + buf) * (1 - second) + second
    stage[buf] = dot_tn(held[left], held[(2 + buf) * second]).astype(BF)

    @pl.when(step < 4)
    def _():

        def body(chunk, carry):
            for unit in range(2):
                far_core, slot = slot_of(16 + 4 * step + chunk, me, unit == 1)
                at = pl.multiple_of((2 * chunk + unit) * SLOT, 32)
                src = stage.at[buf, pl.ds(at, SLOT)]
                send_slot((parts_a, parts_b)[unit], far_core, slot, 0, src, sems.at[buf])
            return carry

        lax.fori_loop(0, 4, body, 0)

    @pl.when(step >= 4)
    def _():
        send_in_blocks(parts_b, me, True, step - 4, stage, buf, sems.at[buf])

    @pl.when(step == 5)
    def _():
        wait_whole(small_stage, small_sem)

    wait_last(stage, sems, step, 6)


def ffn_grads(x_low, hidden, dhid, dfb, sums):
    tok, width = x_low.shape
    out = pl.pallas_call(
        ffn_grad_kernel,
        grid=(6,),
        out_shape=part_shapes(width, False) + part_shapes(width, True),
        in_specs=[spec_any()] * 4 + [spec_whole((EXTRA, width))],
        out_specs=(spec_any(),) * 8,
        scratch_shapes=[
            pltpu.VMEM((4, tok, width), BF),
            pltpu.VMEM((2, width, width), BF),
            pltpu.VMEM((EXTRA, width), BF),
            pltpu.SemaphoreType.DMA((4,)),
            pltpu.SemaphoreType.DMA((2,)),
            pltpu.SemaphoreType.DMA,
        ],
        compiler_params=params(BIG),
        cost_estimate=pl.CostEstimate(
            flops=3 * tok * width * FF, bytes_accessed=24 * MIB, transcendentals=0
        ),
        name="ffn_grads",
    )(x_low, hidden, dhid, dfb, sums)
    return out[0:4], out[4:8]


def ffn_rest_kernel(x_ref, dhid_ref, *refs):
    parts = refs[4:8]
    stage, sems = refs[8:]
    me = lax.axis_index("fsdp")
    step = pl.program_id(0)
    stage[step] = dot_tn(x_ref[...], dhid_ref[...]).astype(BF)
    send_in_blocks(parts, me, False, step, stage, step, sems.at[step])
    wait_last(stage, sems, step, 2)


def ffn_rest(x_low, dhid, parts):
    tok, width = x_low.shape
    return pl.pallas_call(
        ffn_rest_kernel,
        grid=(2,),
        out_shape=part_shapes(width, False),
        in_specs=[spec_whole((tok, width)), pl.BlockSpec((tok, width), lambda i: (0, i))]
        + [spec_any()] * 4,
        out_specs=(spec_any(),) * 4,
        input_output_aliases={2 + i: i for i in range(4)},
        scratch_shapes=[pltpu.VMEM((2, width, width), BF), pltpu.SemaphoreType.DMA((2,))],
        compiler_params=params(BIG),
        cost_estimate=pl.CostEstimate(
            flops=tok * width * FF, bytes_accessed=8 * MIB, transcendentals=0
        ),
        name="ffn_rest",
    )(x_low, dhid, *parts)


def backward_kernel(held, q_ref, k_ref, v_ref, dctx_ref, lse_ref, seg_row_ref, *refs):
    dq_ref, dk_ref, dv_ref = refs[held:]
    left = head_mask(q_ref.shape[0])
    same = as_column(seg_row_ref[0]) == seg_row_ref[0].astype(F32)
    heads = 2 * BWD_PAIRS
    held_a, held_b, held_c = {}, {}, {}

    def pair_cols(head):
        return slice(head // 2 * LANES, (head // 2 + 1) * LANES)

    def products(head):
        cols = pair_cols(head)
        keep = left if head % 2 == 0 else jnp.logical_not(left)
        own = jnp.where(keep, q_ref[:, cols], jnp.zeros((keep.shape), BF))
        own_grad = jnp.where(keep, dctx_ref[:, cols], jnp.zeros((keep.shape), BF))
        scores = dot_nt(k_ref[:, cols], own)
        held_a[head] = (own, own_grad, scores, dot_nt(v_ref[:, cols], own_grad))

    def softmax_back(head):
        own, own_grad, scores, grad_probs = held_a.pop(head)
        scores = jnp.where(same, scores, MASKED_SCORE)
        probs = jnp.exp(scores - lse_ref[0, head // 2, head % 2 : head % 2 + 1, :])
        inner = jnp.sum(grad_probs * probs, axis=0, keepdims=True)
        grad_scores = (probs * (grad_probs - inner)).astype(BF)
        held_b[head] = (own, own_grad, probs.astype(BF), grad_scores)

    def outputs(head):
        own, own_grad, probs, grad_scores = held_b.pop(head)
        cols = pair_cols(head)
        keys_t = k_ref[:, cols].T[(head % 2) * HEAD_DIM : (head % 2 + 1) * HEAD_DIM]
        grad_q = dot_nn(keys_t, grad_scores)
        grad_k = dot_nn(grad_scores, own)
        grad_v = dot_nn(probs, own_grad)
        if head % 2 == 0:
            held_c[0] = (grad_q, grad_k, grad_v)
            return
        first_q, first_k, first_v = held_c.pop(0)
        both_q = jnp.concatenate([first_q, grad_q]).T
        dq_ref[:, cols] = (both_q.astype(BF) * 0.125).astype(BF)
        dk_ref[:, cols] = (first_k + grad_k).astype(BF)
        dv_ref[:, cols] = (first_v + grad_v).astype(BF)

    for tick in range(heads + 2):
        if tick < heads:
            products(tick)
        if 0 <= tick - 1 < heads:
            softmax_back(tick - 1)
        if tick >= 2:
            outputs(tick - 2)


def attention_backward(at, qkv, dctx, lse, seg_row, held=()):
    tok, width = qkv.shape[1:]
    seq = seg_row.shape[2]
    tile, row, stat, parts = sequence_specs(at, seq, BWD_PAIRS)
    return pl.pallas_call(
        functools.partial(backward_kernel, len(held)),
        grid=(width // LANES // BWD_PAIRS,),
        out_shape=(jax.ShapeDtypeStruct((tok, width), BF),) * 3,
        in_specs=parts + [tile(), stat(), row()]
        + [spec_any() for _ in held],
        out_specs=(tile(), tile(), tile()),
        input_output_aliases={6 + i: i for i in range(len(held))},
        compiler_params=params(BIG),
        cost_estimate=pl.CostEstimate(
            flops=40 * seq * seq * width,
            bytes_accessed=6 * MIB,
            transcendentals=seq * seq * width // HEAD_DIM,
        ),
        name="attention_backward",
    )(qkv, qkv, qkv, dctx, lse, seg_row, *held)


def input_grad_kernel(dq_ref, dk_ref, dv_ref, dob_ref, masked_ref, *refs):
    quad = refs[0:4]
    dx_ref, small_ref, weights, sems = refs[4:]
    width = dq_ref.shape[1]
    step = pl.program_id(0)

    @pl.when(step == 0)
    def _():
        load_projections(quad, weights, sems)
        small_ref[...] = jnp.zeros_like(small_ref)

    grad = dob_ref[...].astype(F32)
    for matrix in range(3):
        rows = slice(matrix * width, (matrix + 1) * width)

        @pl.when(step == 0)
        def _():
            wait_whole(weights.at[rows], sems.at[matrix])

        grad = grad + dot_nt((dq_ref, dk_ref, dv_ref)[matrix][...], weights[rows])
    chosen = as_column(masked_ref[0]) == 1.0
    dx_ref[...] = jnp.where(chosen, 0.0, grad)
    small_ref[0:1] += column_sum(dq_ref[...].astype(F32))
    small_ref[1:2] += column_sum(dv_ref[...].astype(F32))
    small_ref[5:6] += column_sum(jnp.where(chosen, grad, 0.0))


def input_grads(dq, dk, dv, dob, masked_row, quad):
    tok, width = dq.shape
    rows = TILE
    per = masked_row.shape[2] // rows
    tile = lambda cols: pl.BlockSpec((rows, cols), lambda i: (i, 0))
    whole = spec_whole((EXTRA, width))
    return pl.pallas_call(
        input_grad_kernel,
        grid=(tok // rows,),
        out_shape=(
            jax.ShapeDtypeStruct((tok, width), F32),
            jax.ShapeDtypeStruct((EXTRA, width), F32),
        ),
        in_specs=[tile(width)] * 4
        + [pl.BlockSpec((1, 1, rows), lambda i: (i // per, 0, i % per))]
        + [spec_any()] * 4,
        out_specs=(tile(width), whole),
        scratch_shapes=[pltpu.VMEM((3 * width, width), BF), pltpu.SemaphoreType.DMA((3,))],
        compiler_params=params(BIG),
        cost_estimate=pl.CostEstimate(
            flops=6 * tok * width * width, bytes_accessed=16 * MIB, transcendentals=0
        ),
        name="input_grads",
    )(dq, dk, dv, dob, masked_row, *quad)


def att_grad_kernel(*refs):
    sources, parts = refs[0:6], refs[6:10]
    held, stage, load_sems, sems = refs[10:]
    me = lax.axis_index("fsdp")
    step = pl.program_id(0)
    buf = lax.rem(step, 2)

    @pl.when(step == 0)
    def _():
        for number in range(6):
            pltpu.make_async_copy(sources[number], held.at[number], load_sems.at[number]).start()

    wait_reuse(stage, sems, buf, step)
    for matrix in range(4):

        @pl.when(step == matrix)
        def _():
            for number in ((0, 1), (2, 3), (4,), (5,))[matrix]:
                wait_whole(held.at[number], load_sems.at[number])

    left = 2 * jnp.minimum(step, 1)
    stage[buf] = dot_tn(held[left], held[left + jnp.maximum(step, 1)]).astype(BF)
    first = lax.rem(step + 3, 4) * 8

    def body(piece, carry):
        far_core, slot = slot_of(first + piece, me)
        src = stage.at[buf, pl.ds(pl.multiple_of(piece * SLOT, 32), SLOT)]
        send_slot(parts, far_core, slot, 0, src, sems.at[buf])
        return carry

    lax.fori_loop(0, 8, body, 0)
    wait_last(stage, sems, step, 4)


def att_grads(ctx, dob, stream, dq, dk, dv):
    tok, width = stream.shape
    return pl.pallas_call(
        att_grad_kernel,
        grid=(4,),
        out_shape=part_shapes(width, False),
        in_specs=[spec_any()] * 6,
        out_specs=(spec_any(),) * 4,
        scratch_shapes=[
            pltpu.VMEM((6, tok, width), BF),
            pltpu.VMEM((2, width, width), BF),
            pltpu.SemaphoreType.DMA((6,)),
            pltpu.SemaphoreType.DMA((2,)),
        ],
        compiler_params=params(BIG),
        cost_estimate=pl.CostEstimate(
            flops=8 * tok * width * width, bytes_accessed=16 * MIB, transcendentals=0
        ),
        name="att_grads",
    )(ctx, dob, stream, dq, dk, dv)


def flat_ffn_kernel(a_ref, b_ref, out_ref):
    first = lax.axis_index("fsdp") < 16

    @pl.when(first)
    def _():
        for block in range(4):
            source = a_ref if block < 2 else b_ref
            rows = slice((block % 2) * 48, (block % 2) * 48 + 48)
            for part in range(6):
                cols = slice(part * LANES, (part + 1) * LANES)
                out_ref[pl.ds(6 * block + part, 48, stride=24), :] = source[rows, cols]

    @pl.when(jnp.logical_not(first))
    def _():
        for part in range(6):
            cols = slice(part * LANES, (part + 1) * LANES)
            out_ref[pl.ds(part, SLOT, stride=6), :] = a_ref[:, cols]
            out_ref[pl.ds(6 * SLOT + part, SLOT, stride=6), :] = b_ref[:, cols]


def flatten_ffn(grad_a, grad_b):
    return pl.pallas_call(
        flat_ffn_kernel,
        out_shape=jax.ShapeDtypeStruct((12 * SLOT, LANES), F32),
        in_specs=[spec_vmem()] * 2,
        out_specs=spec_vmem(),
        compiler_params=params(16),
        name="flatten_ffn",
    )(grad_a, grad_b)


def flat_att_kernel(kept_ref, got_ref, ffn_ref, late_ref, out_ref, head_ref):
    for part in range(6):
        cols = slice(part * LANES, (part + 1) * LANES)
        total = kept_ref[:, cols].astype(F32) + got_ref[0:SLOT, cols].astype(F32)
        out_ref[pl.ds(part, SLOT, stride=6), :] = total
    head_ref[0:64, :] = out_ref[0:64, :]
    head_ref[64:128, :] = ffn_ref[0:64, :]

    @pl.when(lax.axis_index("fsdp") == 0)
    def _():
        for part in range(6):
            cols = slice(part * LANES, (part + 1) * LANES)
            head_ref[pl.ds(part, 6, stride=6), :] = late_ref[0:6, cols]


def flatten_att(kept, got, ffn_flat, late):
    return pl.pallas_call(
        flat_att_kernel,
        out_shape=(
            jax.ShapeDtypeStruct((6 * SLOT, LANES), F32),
            jax.ShapeDtypeStruct((128, LANES), F32),
        ),
        in_specs=[spec_vmem()] * 4,
        out_specs=(spec_vmem(),) * 2,
        compiler_params=params(16),
        name="flatten_att",
    )(kept, got, ffn_flat, late)


def update_kernel(last, rate, *refs):
    inputs, outputs, bufs = refs[0:10], refs[10:18], refs[18:20]
    me = lax.axis_index("fsdp")
    head_ref, small_ref = inputs[2], inputs[3]
    for unit in range(2):
        flat_ref = inputs[unit]
        w_ref, m_ref, a_ref = inputs[4 + 3 * unit : 7 + 3 * unit]
        w_out, m_out, a_out, low_out = outputs[4 * unit : 4 * unit + 4]
        buf = bufs[unit]
        aligned = flat_ref.shape[0]
        first, count = ((0, 6), (6, 7))[unit]
        buf[0:aligned, :] = flat_ref[...]
        buf[aligned : aligned + 64, :] = head_ref[unit * 64 : unit * 64 + 64, :]

        @pl.when(me == last)
        def _():
            buf[aligned : aligned + 64, :] = jnp.zeros((64, LANES), F32)
            for part in range(6):
                cols = slice(part * LANES, (part + 1) * LANES)
                small = small_ref[first : first + count, cols]
                if unit == 0:
                    small = small + head_ref[pl.ds(part, count, stride=6), :]
                buf[pl.ds(aligned + part, count, stride=6), :] = small

        grad = buf[pl.ds(2 * me, w_ref.shape[0]), :]
        moment = 0.5 * m_ref[...] + grad
        master = w_ref[...] - rate * (grad + 0.5 * moment)
        m_out[...] = moment
        w_out[...] = master
        a_out[...] = 0.5 * a_ref[...] + 0.5 * master
        low_out[...] = master.astype(BF)


def update(flats, head, small, rate, devices, att, ffn):
    shapes = []
    for arrays in (att, ffn):
        f32 = jax.ShapeDtypeStruct(arrays[0].shape, F32)
        shapes += [f32, f32, f32, jax.ShapeDtypeStruct(arrays[0].shape, BF)]
    out = pl.pallas_call(
        functools.partial(update_kernel, devices - 1, rate),
        out_shape=tuple(shapes),
        in_specs=[spec_vmem()] * 10,
        out_specs=(spec_vmem(),) * 8,
        scratch_shapes=[pltpu.VMEM((flat.shape[0] + 64, LANES), F32) for flat in flats],
        compiler_params=params(16),
        name="update",
    )(*flats, head, small, *att, *ffn)
    return out


def local_exchange(
    block_input,
    seg_ids,
    masked,
    out_grad,
    att_master,
    att_moment,
    att_average,
    ffn_master,
    ffn_moment,
    ffn_average,
):
    tok, width = block_input.shape
    seq_count, seq = seg_ids.shape
    devices = lax.axis_size("fsdp")
    up = [(i, i + 1) for i in range(devices - 1)]
    down = [(i + 1, i) for i in range(devices - 1)]
    tails = lax.ppermute(row_tails(att_master, ffn_master), "fsdp", up)
    masked_row = masked.reshape(seq_count, 1, seq)
    seg_row = seg_ids.reshape(seq_count, 1, seq)
    att, chunk_a, chunk_b = prepare(att_master, ffn_master, tails, devices, width)
    got, masked_row, seg_row = phase(exchange(att, 0), masked_row, seg_row)
    att = widen_small(att, got)
    got = exchange(att, 1)
    att, unit_a = phase(widen_small(att, got), chunk_a)
    got, got_a = phase(exchange(att, 2), exchange(unit_a, 0))
    att, unit_a, unit_b = phase(widen_small(att, got), widen(unit_a, got_a), chunk_b)
    att_next, att_far, got_a, got_b = phase(
        exchange(att, 3), exchange(att, 4), exchange(unit_a, 1), exchange(unit_b, 0)
    )
    unit_a, unit_b, att_next = phase(widen(unit_a, got_a), widen(unit_b, got_b), att_next)
    att_last, got_b, block_input = phase(exchange(att_next, 4), exchange(unit_b, 2), block_input)
    att = (att, att_next, att_far, att_last)
    unit_a, unit_b, block_input = phase(unit_a, widen(unit_b, got_b), block_input)
    got_b = exchange(unit_b, 1)
    stream, qkv, small = project(block_input, masked_row, att)
    got_a, qkv = phase(exchange(unit_a, 2), qkv)
    unit_a, qkv = phase(widen(unit_a, got_a), qkv)
    held = attention_forward(0, qkv, seg_row)
    a_next, a_far, got_b, held = phase(exchange(unit_a, 3), exchange(unit_a, 4), got_b, held)
    unit_b, a_next, held = phase(widen(unit_b, got_b), a_next, held)
    ctx, lse = attention_forward(1, qkv, seg_row, held)
    b_next, b_far, a_last, ctx = phase(
        exchange(unit_b, 3), exchange(unit_b, 4), exchange(a_next, 4), ctx
    )
    b_last = exchange(b_next, 4)
    block_output, x_low, hidden, dhid, dfb, dob, dctx, sums = feed_forward(
        stream,
        ctx,
        out_grad,
        small,
        att,
        (unit_a, a_next, a_far, a_last),
        (unit_b, b_next, b_far, b_last),
    )
    part_a, part_b = ffn_grads(x_low, hidden, dhid, dfb, sums)
    part_b, dhid = phase(part_b, dhid)
    part_a = ffn_rest(x_low, dhid, part_a)
    high_b, low_b, part_a = phase(exchange(part_b[3], 4), exchange(part_b[2], 4), part_a)
    small_sum = sums + high_b[8 * SLOT :].astype(F32)
    high_b = add_small(total_of((part_b[1], high_b), 0, 8 * SLOT).astype(BF), small_sum)
    high_b, part_a, dctx = phase(high_b, part_a, dctx)
    held = attention_backward(0, qkv, dctx, lse, seg_row)
    got_b, high_a, low_a, held = phase(
        exchange(high_b, 3), exchange(part_a[3], 4), exchange(part_a[2], 4), held
    )
    high_a = total_of((part_a[1], high_a), 0, 8 * SLOT).astype(BF)
    small_sum = small_sum + got_b[8 * SLOT :].astype(F32)
    kept_b, sent_b = halve(part_b[0], low_b, got_b[: 8 * SLOT])
    high_a, sent_b, held = phase(high_a, add_small(sent_b, small_sum), held)
    dq, dk, dv = attention_backward(1, qkv, dctx, lse, seg_row, held)
    got_a, got_b, dq = phase(exchange(high_a, 3), exchange(sent_b, 1), dq)
    kept_a, sent_a = halve(part_a[0], low_a, got_a)
    small_sum = small_sum + got_b[4 * SLOT :].astype(F32)
    kept_b, sent_b = halve(kept_b, got_b[: 4 * SLOT])
    sent_a, sent_b, dq = phase(sent_a, add_small(sent_b, small_sum), dq)
    part = att_grads(ctx, dob, stream, dq, dk, dv)
    got_a, got_b, part = phase(exchange(sent_a, 2), exchange(sent_b, 2), part)
    kept_a, sent_a = halve(kept_a, got_a)
    small_sum = small_sum + got_b[2 * SLOT :].astype(F32)
    kept_b, sent_b = halve(kept_b, got_b[: 2 * SLOT])
    sent_a, sent_b, part = phase(sent_a, add_small(sent_b, small_sum), part)
    got_b = exchange(sent_b, 0)
    high = exchange(part[3], 4)
    high = total_of((part[1], high), 0, 8 * SLOT).astype(BF)
    high, sent_a, dq = phase(high, sent_a, dq)
    input_grad, late = input_grads(dq, dk, dv, dob, masked_row, att)
    got, low, got_a, got_b, late = phase(
        exchange(high, 3), exchange(part[2], 4), exchange(sent_a, 1), got_b, late
    )
    kept, sent = halve(part[0], low, got)
    kept_a, sent_a = halve(kept_a, got_a)
    sent, sent_a, late = phase(sent, sent_a, late)
    got, got_a = phase(exchange(add_small(sent, late), 2), exchange(sent_a, 0))
    late = late + got[4 * SLOT :].astype(F32)
    kept, sent = halve(kept, got[: 4 * SLOT])
    sent, late, got_a, got_b = phase(sent, late, got_a, got_b)
    got = exchange(sent, 1)
    late = late + exchange(late.astype(BF), 3).astype(F32)
    late = late + exchange(late.astype(BF), 4).astype(F32)
    kept, sent = halve(kept, got)
    sent, got_a, got_b = phase(add_small(sent, late), got_a, got_b)
    got = exchange(sent, 0)
    small_sum = small_sum + got_b[SLOT:].astype(F32)
    grad_a = total_of((kept_a, got_a), 0, SLOT)
    grad_b = total_of((kept_b, got_b), 0, SLOT)
    ffn_flat = flatten_ffn(grad_a, grad_b)
    got, ffn_flat, small_sum = phase(got, ffn_flat, small_sum)
    late = late + got[SLOT:].astype(F32)
    att_flat, heads = flatten_att(kept, got, ffn_flat, late)
    heads = lax.ppermute(heads, "fsdp", down + [(0, devices - 1)])
    rate = 0.05 / math.sqrt(tok * devices)
    new = update(
        (att_flat, ffn_flat),
        heads,
        small_sum + late,
        rate,
        devices,
        (att_master, att_moment, att_average),
        (ffn_master, ffn_moment, ffn_average),
    )
    return (block_output, input_grad) + tuple(new)


def chunked(mesh):
    return mesh.shape["fsdp"] == 32


def solution(mesh):
    in_specs = (
        P("fsdp", None),
        P("fsdp", None),
        P("fsdp", None),
        P("fsdp", None),
        P("fsdp", None),
        P("fsdp", None),
        P("fsdp", None),
        P("fsdp", None),
        P("fsdp", None),
        P("fsdp", None),
    )
    out_specs = (
        P("fsdp", None),
        P("fsdp", None),
        P("fsdp", None),
        P("fsdp", None),
        P("fsdp", None),
        P("fsdp", None),
        P("fsdp", None),
        P("fsdp", None),
        P("fsdp", None),
        P("fsdp", None),
    )
    body = local_exchange if chunked(mesh) else local
    return jax.shard_map(body, mesh=mesh, in_specs=in_specs, out_specs=out_specs, check_vma=False)
```

profile of v0, /device:TPU:7, one launch (start us, length us, event | category | flops | bytes accessed | tf_op | source)
XLA Modules:
  0.0 285.2 jit_solution(4530423041016828023)
XLA Ops:
  0.7 1.5 row_tails.1
  2.2 3.7 %collective-permute-start = (f32[128,128]{1,0:T(8,128)}, f32[128,128]{1,0:T(8,128)S(1)}, u32[]{:S(2)}, u32[]{:S(2)}) collective-permute-start(f32[128,128]{1,0:T(8,128)} %row_tails.1), channel_id=1, source_target_pairs={{0,1},{1,2},{2,3},{3,4},{4,5},{5,6},{6,7},{7,8},{8,9},{9,10},{10,1... | collective-permute-start | bytes 196616 | tf_op jit(solution)/shard_map/ppermute | solution.py:1311
  5.9 1.6 collective-permute-done.tail_ref
  7.5 1.0 copy-done.1
  8.7 2.3 collective-permute-start.1
  12.2 6.4 %collective-permute-done.1 = bf16[112,768]{1,0:T(8,128)(2,1)S(1)} collective-permute-done((bf16[112,768]{1,0:T(8,128)(2,1)S(1)}, bf16[112,768]{1,0:T(8,128)(2,1)S(1)}, u32[]{:S(2)}, u32[]{:S(2)}) %collective-permute-start.1) | collective-permute-done | bytes 172064 | tf_op jit(solution)/shard_map/ppermute | solution.py:328
  18.7 7.4 %collective-permute-done.2 = bf16[208,768]{1,0:T(8,128)(2,1)S(1)} collective-permute-done((bf16[208,768]{1,0:T(8,128)(2,1)S(1)}, bf16[208,768]{1,0:T(8,128)(2,1)S(1)}, u32[]{:S(2)}, u32[]{:S(2)}) %collective-permute-start.2) | collective-permute-done | bytes 319520 | tf_op jit(solution)/shard_map/ppermute | solution.py:328
  26.8 4.2 %collective-permute-start.4 = (bf16[96,768]{1,0:T(8,128)(2,1)S(1)}, bf16[96,768]{1,0:T(8,128)(2,1)S(1)}, u32[]{:S(2)}, u32[]{:S(2)}) collective-permute-start(bf16[96,768]{1,0:T(8,128)(2,1)S(1)} %get-tuple-element.175), channel_id=1, source_target_pairs={{0,16},{1,17},{2,18},{3,19},{4,20},{5,21},{6,22},{7,23},{8,24},{9,... | collective-permute-start | bytes 442376 | tf_op jit(solution)/shard_map/ppermute | solution.py:328
  31.0 6.5 %collective-permute-done.4 = bf16[96,768]{1,0:T(8,128)(2,1)S(1)} collective-permute-done((bf16[96,768]{1,0:T(8,128)(2,1)S(1)}, bf16[96,768]{1,0:T(8,128)(2,1)S(1)}, u32[]{:S(2)}, u32[]{:S(2)}) %collective-permute-start.4) | collective-permute-done | bytes 147488 | tf_op jit(solution)/shard_map/ppermute | solution.py:328
  37.8 1.4 collective-permute-start.6
  40.1 3.1 %collective-permute-start.8 = (bf16[96,768]{1,0:T(8,128)(2,1)S(1)}, bf16[96,768]{1,0:T(8,128)(2,1)S(1)}, u32[]{:S(2)}, u32[]{:S(2)}) collective-permute-start(bf16[96,768]{1,0:T(8,128)(2,1)S(1)} %get-tuple-element.181), channel_id=1, source_target_pairs={{0,16},{1,17},{2,18},{3,19},{4,20},{5,21},{6,22},{7,23},{8,24},{9,... | collective-permute-start | bytes 442376 | tf_op jit(solution)/shard_map/ppermute | solution.py:328
  43.2 5.3 %collective-permute-done.8 = bf16[96,768]{1,0:T(8,128)(2,1)S(1)} collective-permute-done((bf16[96,768]{1,0:T(8,128)(2,1)S(1)}, bf16[96,768]{1,0:T(8,128)(2,1)S(1)}, u32[]{:S(2)}, u32[]{:S(2)}) %collective-permute-start.8) | collective-permute-done | bytes 147488 | tf_op jit(solution)/shard_map/ppermute | solution.py:328
  48.4 2.4 collective-permute-done.7
  50.9 4.0 %collective-permute-done.5.refs_1_ = bf16[784,768]{1,0:T(8,128)(2,1)S(1)} collective-permute-done((bf16[784,768]{1,0:T(8,128)(2,1)S(1)}, bf16[784,768]{1,0:T(8,128)(2,1)S(1)}, u32[]{:S(2)}, u32[]{:S(2)}) %collective-permute-start.5) | collective-permute-done | bytes 1204256 | tf_op jit(solution)/shard_map/ppermute | solution.py:328
  54.9 1.0 collective-permute-start.9
  56.1 5.7 %collective-permute-done.10 = bf16[192,768]{1,0:T(8,128)(2,1)S(1)} collective-permute-done((bf16[192,768]{1,0:T(8,128)(2,1)S(1)}, bf16[192,768]{1,0:T(8,128)(2,1)S(1)}, u32[]{:S(2)}, u32[]{:S(2)}) %collective-permute-start.10) | collective-permute-done | bytes 294944 | tf_op jit(solution)/shard_map/ppermute | solution.py:328
  61.8 1.0 copy-done.26
  63.1 9.7 %project.1 = (bf16[1024,768]{1,0:T(8,128)(2,1)}, bf16[3,1024,768]{2,1,0:T(8,128)(2,1)}, f32[16,768]{1,0:T(8,128)}) custom-call(bf16[1024,768]{1,0:T(8,128)(2,1)} %x_ref, s32[2,1,512]{2,1,0:T(1,128)} %reshape.50.masked_ref, bf16[784,768]{1,0:T(8,128)(2,1)} %copy-done.9, bf16[784,768]{1,0:T(8,128)(2,1)} %copy-done.25, bf16[784,768]{1,0:T(8,128)(2,1)} %copy-done.24, ...), custom_call_target="tpu_custom_call" | custom-call | flops 3623878656 | bytes 16777216 | tf_op jit(solution)/shard_map/project/pallas_call | solution.py:583
  73.0 1.3 collective-permute-start.13
  74.3 1.3 collective-permute-start.12
  76.1 10.3 %attention_forward.2 = (bf16[1024,768]{1,0:T(8,128)(2,1)}, f32[2,6,2,512]{3,2,1,0:T(2,128)}) custom-call(bf16[3,1024,768]{2,1,0:T(8,128)(2,1)} %get-tuple-element.201.q_ref.k_ref.v_ref, bf16[3,1024,768]{2,1,0:T(8,128)(2,1)} %get-tuple-element.201.q_ref.k_ref.v_ref, bf16[3,1024,768]{2,1,0:T(8,128)(2,1)} %get-tuple-element.201.q_ref.k_ref.v_ref, ...), custom_call_target="tpu_custom_call" | custom-call | flops 3221225472 | bytes 4194304 | tf_op jit(solution)/shard_map/attention_forward/pallas_call | solution.py:647
  86.4 4.4 %collective-permute-done.14 = bf16[384,768]{1,0:T(8,128)(2,1)S(1)} collective-permute-done((bf16[384,768]{1,0:T(8,128)(2,1)S(1)}, bf16[384,768]{1,0:T(8,128)(2,1)S(1)}, u32[]{:S(2)}, u32[]{:S(2)}) %collective-permute-start.14) | collective-permute-done | bytes 589856 | tf_op jit(solution)/shard_map/ppermute | solution.py:328
  90.9 0.9 copy-done.27
  92.9 10.3 %attention_forward.3 = (bf16[1024,768]{1,0:T(8,128)(2,1)}, f32[2,6,2,512]{3,2,1,0:T(2,128)}) custom-call(bf16[3,1024,768]{2,1,0:T(8,128)(2,1)} %get-tuple-element.201.q_ref.k_ref.v_ref, bf16[3,1024,768]{2,1,0:T(8,128)(2,1)} %get-tuple-element.201.q_ref.k_ref.v_ref, ...), custom_call_target="tpu_custom_call", output_to_operand_aliasing={{0}: (4, {}), {1}: (5, {})} | custom-call | flops 3221225472 | bytes 4194304 | tf_op jit(solution)/shard_map/attention_forward/pallas_call | solution.py:647
  103.2 5.0 %collective-permute-done.15 = bf16[768,768]{1,0:T(8,128)(2,1)} collective-permute-done((bf16[768,768]{1,0:T(8,128)(2,1)S(1)}, bf16[768,768]{1,0:T(8,128)(2,1)}, u32[]{:S(2)}, u32[]{:S(2)}) %collective-permute-start.15) | collective-permute-done | bytes 1179680 | tf_op jit(solution)/shard_map/ppermute | solution.py:328
  108.2 1.3 collective-permute-start.18
  109.5 2.7 collective-permute-done.18
  112.2 1.0 copy-done.32
  113.2 35.5 %feed_forward.1 = (bf16[1024,768]{1,0:T(8,128)(2,1)}, bf16[1024,768]{1,0:T(8,128)(2,1)}, bf16[1024,3072]{1,0:T(8,128)(2,1)}, bf16[1024,3072]{1,0:T(8,128)(2,1)},...) custom-call(bf16[1024,768]{1,0:T(8,128)(2,1)} %get-tuple-element.194.stre, ...), custom_call_target="tpu_custom_call" | custom-call | flops 19327352832 | bytes 41943040 | tf_op jit(solution)/shard_map/feed_forward/pallas_call | solution.py:799
  148.7 13.7 %ffn_grads.1 = (bf16[768,768]{1,0:T(8,128)(2,1)}, bf16[768,768]{1,0:T(8,128)(2,1)}, bf16[768,768]{1,0:T(8,128)(2,1)}, bf16[768,768]{1,0:T(8,128)(2,1)}, bf16[768...) custom-call(bf16[1024,768]{1,0:T(8,128)(2,1)} %get-tuple-element.221.x_ref, ...), custom_call_target="tpu_custom_call" | custom-call | flops 7247757312 | bytes 25165824 | tf_op jit(solution)/shard_map/ffn_grads/pallas_call | solution.py:950
  163.0 6.4 %ffn_rest.1 = (bf16[768,768]{1,0:T(8,128)(2,1)}, bf16[768,768]{1,0:T(8,128)(2,1)}, bf16[768,768]{1,0:T(8,128)(2,1)}, bf16[768,768]{1,0:T(8,128)(2,1)}) custom-call(bf16[1024,768]{1,0:T(8,128)(2,1)} %get-tuple-element.221.x_ref, ...), custom_call_target="tpu_custom_call", output_to_operand_aliasing={{0}: (2, {}), {1}: (3, {}), {2}: (4, {}), {3}: (5, {})} | custom-call | flops 2415919104 | bytes 8388608 | tf_op jit(solution)/shard_map/ffn_rest/pallas_call | solution.py:985
  169.4 1.0 copy-done.16
  172.4 12.2 %attention_backward.2 = (bf16[1024,768]{1,0:T(8,128)(2,1)}, bf16[1024,768]{1,0:T(8,128)(2,1)}, bf16[1024,768]{1,0:T(8,128)(2,1)}) custom-call(bf16[3,1024,768]{2,1,0:T(8,128)(2,1)} %get-tuple-element.201.q_ref.k_ref.v_ref, bf16[3,1024,768]{2,1,0:T(8,128)(2,1)} %get-tuple-element.201.q_ref.k_ref.v_ref, ...), custom_call_target="tpu_custom_call" | custom-call | flops 8053063680 | bytes 6291456 | tf_op jit(solution)/shard_map/attention_backward/pallas_call | solution.py:1057
  184.7 1.9 collective-permute-done.21
  186.6 2.1 add_convert_fusion.5
  188.7 1.6 add_convert_fusion.1
  191.4 12.4 %attention_backward.3 = (bf16[1024,768]{1,0:T(8,128)(2,1)}, bf16[1024,768]{1,0:T(8,128)(2,1)}, bf16[1024,768]{1,0:T(8,128)(2,1)}) custom-call(bf16[3,1024,768]{2,1,0:T(8,128)(2,1)} %get-tuple-element.201.q_ref.k_ref.v_ref, bf16[3,1024,768]{2,1,0:T(8,128)(2,1)} %get-tuple-element.201.q_ref.k_ref.v_ref, ...), custom_call_target="tpu_custom_call", output_to_operand_aliasing={{0}: (6, {}), {1}: (7, {}), {2}: (8, {})} | custom-call | flops 8053063680 | bytes 6291456 | tf_op jit(solution)/shard_map/attention_backward/pallas_call | solution.py:1057
  204.5 1.3 collective-permute-done.24
  206.0 1.1 copy-done.8
  207.0 1.7 add_convert_fusion.6
  209.1 1.2 collective-permute-start.27
  210.2 9.4 %att_grads.1 = (bf16[768,768]{1,0:T(8,128)(2,1)}, bf16[768,768]{1,0:T(8,128)(2,1)}, bf16[768,768]{1,0:T(8,128)(2,1)}, bf16[768,768]{1,0:T(8,128)(2,1)}) custom-call(bf16[1024,768]{1,0:T(8,128)(2,1)} %get-tuple-element.214.ctx_ref.refs_0_, bf16[1024,768]{1,0:T(8,128)(2,1)} %get-tuple-element.277.refs_1_.dob_ref, ...), custom_call_target="tpu_custom_call" | custom-call | flops 4831838208 | bytes 16777216 | tf_op jit(solution)/shard_map/att_grads/pallas_call | solution.py:1164
  219.6 1.6 collective-permute-done.27
  221.3 0.9 add_convert_fusion.11
  222.9 2.9 %collective-permute-start.28 = (bf16[768,768]{1,0:T(8,128)(2,1)S(1)}, bf16[768,768]{1,0:T(8,128)(2,1)S(1)}, u32[]{:S(2)}, u32[]{:S(2)}) collective-permute-start(bf16[768,768]{1,0:T(8,128)(2,1)S(1)} %copy-done.31), channel_id=1, source_target_pairs={{0,1},{1,0},{2,3},{3,2},{4,5},{5,4},{6,7},{7,6},{8,9},{9,8},{10,11... | collective-permute-start | bytes 3538952 | tf_op jit(solution)/shard_map/ppermute | solution.py:328
  225.9 3.4 %collective-permute-done.28 = bf16[768,768]{1,0:T(8,128)(2,1)S(1)} collective-permute-done((bf16[768,768]{1,0:T(8,128)(2,1)S(1)}, bf16[768,768]{1,0:T(8,128)(2,1)S(1)}, u32[]{:S(2)}, u32[]{:S(2)}) %collective-permute-start.28) | collective-permute-done | bytes 1179680 | tf_op jit(solution)/shard_map/ppermute | solution.py:328
  230.2 2.4 collective-permute-start.32
  232.6 1.4 collective-permute-start.31
  234.0 11.6 %input_grads.1 = (f32[1024,768]{1,0:T(8,128)}, f32[16,768]{1,0:T(8,128)}) custom-call(bf16[1024,768]{1,0:T(8,128)(2,1)} %get-tuple-element.294.refs_3_.dq_ref, bf16[1024,768]{1,0:T(8,128)(2,1)} %get-tuple-element.279.refs_4_.dk_ref, bf16[1024,768]{1,0:T(8,128)(2,1)} %get-tuple-element.280.refs_5_.dv_ref, ...), custom_call_target="tpu_custom_call" | custom-call | flops 3623878656 | bytes 16777216 | tf_op jit(solution)/shard_map/input_grads/pallas_call | solution.py:1108
  245.7 1.0 add_convert_fusion.19
  247.5 1.2 collective-permute-start.33
  248.7 1.6 collective-permute-start.34
  250.3 7.7 %collective-permute-done.34 = bf16[96,768]{1,0:T(8,128)(2,1)S(1)} collective-permute-done((bf16[96,768]{1,0:T(8,128)(2,1)S(1)}, bf16[96,768]{1,0:T(8,128)(2,1)S(1)}, u32[]{:S(2)}, u32[]{:S(2)}) %collective-permute-start.34) | collective-permute-done | bytes 147488 | tf_op jit(solution)/shard_map/ppermute | solution.py:328
  258.2 1.5 collective-permute-start.36
  259.7 1.2 collective-permute-done.36
  260.9 2.8 collective-permute-start.37
  263.7 0.8 collective-permute-done.37
  264.6 2.9 %collective-permute-done.35 = bf16[192,768]{1,0:T(8,128)(2,1)S(1)} collective-permute-done((bf16[192,768]{1,0:T(8,128)(2,1)S(1)}, bf16[192,768]{1,0:T(8,128)(2,1)S(1)}, u32[]{:S(2)}, u32[]{:S(2)}) %collective-permute-start.35) | collective-permute-done | bytes 294944 | tf_op jit(solution)/shard_map/ppermute | solution.py:328
  267.8 1.0 convert_add_fusion
  269.0 0.9 convert_add_fusion.3
  269.9 7.8 %collective-permute-done.38.got_ref = bf16[112,768]{1,0:T(8,128)(2,1)S(1)} collective-permute-done((bf16[112,768]{1,0:T(8,128)(2,1)S(1)}, bf16[112,768]{1,0:T(8,128)(2,1)S(1)}, u32[]{:S(2)}, u32[]{:S(2)}) %collective-permute-start.38) | collective-permute-done | bytes 172064 | tf_op jit(solution)/shard_map/ppermute | solution.py:328
  277.8 0.9 collective-permute-start.39
  278.7 4.6 %collective-permute-done.39.refs_2_ = f32[128,128]{1,0:T(8,128)S(1)} collective-permute-done((f32[128,128]{1,0:T(8,128)S(1)}, f32[128,128]{1,0:T(8,128)S(1)}, u32[]{:S(2)}, u32[]{:S(2)}) %collective-permute-start.39) | collective-permute-done | bytes 65568 | tf_op jit(solution)/shard_map/ppermute | solution.py:1404
  283.3 1.9 update.1
  (146 shorter events, 13.9 us)
Async XLA Ops:
  0.6 6.8 %copy-start = (f32[1154,128]{1,0:T(8,128)S(1)}, f32[1154,128]{1,0:T(8,128)}, u32[]{:S(2)}) copy-start(f32[1154,128]{1,0:T(8,128)} %refs_7_.1) | copy-start | bytes 1772548
  0.7 10.3 %copy-start.22 = (s32[2,512]{1,0:T(2,128)S(1)}, s32[2,512]{1,0:T(2,128)}, u32[]{:S(2)}) copy-start(s32[2,512]{1,0:T(2,128)} %param.11) | copy-start | bytes 12292
  0.7 10.9 %copy-start.23 = (s32[2,512]{1,0:T(2,128)S(1)}, s32[2,512]{1,0:T(2,128)}, u32[]{:S(2)}) copy-start(s32[2,512]{1,0:T(2,128)} %param.12) | copy-start | bytes 12292
  2.2 5.3 %collective-permute-start = (f32[128,128]{1,0:T(8,128)}, f32[128,128]{1,0:T(8,128)S(1)}, u32[]{:S(2)}, u32[]{:S(2)}) collective-permute-start(f32[128,128]{1,0:T(8,128)} %row_tails.1), channel_id=1, source_target_pairs={{0,1},{1,2},{2,3},{3,4},{4,5},{5,6},{6,7},{7,8},{8,9},{9,10},{10,1... | collective-permute-start | bytes 196616 | tf_op jit(solution)/shard_map/ppermute | solution.py:1311
  8.7 9.9 %collective-permute-start.1 = (bf16[112,768]{1,0:T(8,128)(2,1)S(1)}, bf16[112,768]{1,0:T(8,128)(2,1)S(1)}, u32[]{:S(2)}, u32[]{:S(2)}) collective-permute-start(bf16[112,768]{1,0:T(8,128)(2,1)S(1)} %get-tuple-element.171), channel_id=1, source_target_pairs={{0,16},{1,17},{2,18},{3,19},{4,20},{5,21},{6,22},{7,23},{8,24},{9,... | collective-permute-start | bytes 516104 | tf_op jit(solution)/shard_map/ppermute | solution.py:328
  18.6 7.5 %collective-permute-start.2 = (bf16[208,768]{1,0:T(8,128)(2,1)S(1)}, bf16[208,768]{1,0:T(8,128)(2,1)S(1)}, u32[]{:S(2)}, u32[]{:S(2)}) collective-permute-start(bf16[208,768]{1,0:T(8,128)(2,1)S(1)} %pad_maximum_fusion.9), channel_id=1, source_target_pairs={{0,8},{1,9},{2,10},{3,11},{4,12},{5,13},{6,14},{7,15},{8,0},{9,1},... | collective-permute-start | bytes 958472 | tf_op jit(solution)/shard_map/ppermute | solution.py:328
  26.2 11.4 %collective-permute-start.3 = (bf16[400,768]{1,0:T(8,128)(2,1)S(1)}, bf16[400,768]{1,0:T(8,128)(2,1)S(1)}, u32[]{:S(2)}, u32[]{:S(2)}) collective-permute-start(bf16[400,768]{1,0:T(8,128)(2,1)S(1)} %pad_maximum_fusion.4), channel_id=1, source_target_pairs={{0,2},{1,5},{2,0},{3,7},{4,6},{5,1},{6,4},{7,3},{8,10},{9,13},{10,... | collective-permute-start | bytes 1843208 | tf_op jit(solution)/shard_map/ppermute | solution.py:328
  26.8 10.7 %collective-permute-start.4 = (bf16[96,768]{1,0:T(8,128)(2,1)S(1)}, bf16[96,768]{1,0:T(8,128)(2,1)S(1)}, u32[]{:S(2)}, u32[]{:S(2)}) collective-permute-start(bf16[96,768]{1,0:T(8,128)(2,1)S(1)} %get-tuple-element.175), channel_id=1, source_target_pairs={{0,16},{1,17},{2,18},{3,19},{4,20},{5,21},{6,22},{7,23},{8,24},{9,... | collective-permute-start | bytes 442376 | tf_op jit(solution)/shard_map/ppermute | solution.py:328
  37.8 25.1 %copy-start.9 = (bf16[784,768]{1,0:T(8,128)(2,1)}, bf16[784,768]{1,0:T(8,128)(2,1)S(1)}, u32[]{:S(2)}) copy-start(bf16[784,768]{1,0:T(8,128)(2,1)S(1)} %pad_maximum_fusion.refs_0_) | copy-start | bytes 3612676
  37.8 13.1 %collective-permute-start.6 = (bf16[784,768]{1,0:T(8,128)(2,1)S(1)}, bf16[784,768]{1,0:T(8,128)(2,1)S(1)}, u32[]{:S(2)}, u32[]{:S(2)}) collective-permute-start(bf16[784,768]{1,0:T(8,128)(2,1)S(1)} %pad_maximum_fusion.refs_0_), channel_id=1, source_target_pairs={{0,1},{1,0},{2,3},{3,2},{4,5},{5,4},{6,7},{7,6},{8,9},{9,8},{10,11... | collective-permute-start | bytes 3612680 | tf_op jit(solution)/shard_map/ppermute | solution.py:328
  39.2 15.6 %collective-permute-start.5 = (bf16[784,768]{1,0:T(8,128)(2,1)S(1)}, bf16[784,768]{1,0:T(8,128)(2,1)S(1)}, u32[]{:S(2)}, u32[]{:S(2)}) collective-permute-start(bf16[784,768]{1,0:T(8,128)(2,1)S(1)} %pad_maximum_fusion.refs_0_), channel_id=1, source_target_pairs={{0,4},{1,3},{2,6},{3,1},{4,0},{5,7},{6,2},{7,5},{8,12},{9,11},{10,... | collective-permute-start | bytes 3612680 | tf_op jit(solution)/shard_map/ppermute | solution.py:328
  39.4 11.4 %collective-permute-start.7 = (bf16[192,768]{1,0:T(8,128)(2,1)S(1)}, bf16[192,768]{1,0:T(8,128)(2,1)S(1)}, u32[]{:S(2)}, u32[]{:S(2)}) collective-permute-start(bf16[192,768]{1,0:T(8,128)(2,1)S(1)} %pad_maximum_fusion.11), channel_id=1, source_target_pairs={{0,8},{1,9},{2,10},{3,11},{4,12},{5,13},{6,14},{7,15},{8,0},{9,1},... | collective-permute-start | bytes 884744 | tf_op jit(solution)/shard_map/ppermute | solution.py:328
  40.1 8.4 %collective-permute-start.8 = (bf16[96,768]{1,0:T(8,128)(2,1)S(1)}, bf16[96,768]{1,0:T(8,128)(2,1)S(1)}, u32[]{:S(2)}, u32[]{:S(2)}) collective-permute-start(bf16[96,768]{1,0:T(8,128)(2,1)S(1)} %get-tuple-element.181), channel_id=1, source_target_pairs={{0,16},{1,17},{2,18},{3,19},{4,20},{5,21},{6,22},{7,23},{8,24},{9,... | collective-permute-start | bytes 442376 | tf_op jit(solution)/shard_map/ppermute | solution.py:328
  50.9 12.0 %copy-start.24 = (bf16[784,768]{1,0:T(8,128)(2,1)}, bf16[784,768]{1,0:T(8,128)(2,1)S(1)}, u32[]{:S(2)}) copy-start(bf16[784,768]{1,0:T(8,128)(2,1)S(1)} %collective-permute-done.6.refs_2_) | copy-start | bytes 3612676
  54.8 8.3 %copy-start.25 = (bf16[784,768]{1,0:T(8,128)(2,1)}, bf16[784,768]{1,0:T(8,128)(2,1)S(1)}, u32[]{:S(2)}) copy-start(bf16[784,768]{1,0:T(8,128)(2,1)S(1)} %collective-permute-done.5.refs_1_) | copy-start | bytes 3612676
  54.9 6.9 %collective-permute-start.9 = (bf16[784,768]{1,0:T(8,128)(2,1)S(1)}, bf16[784,768]{1,0:T(8,128)(2,1)S(1)}, u32[]{:S(2)}, u32[]{:S(2)}) collective-permute-start(bf16[784,768]{1,0:T(8,128)(2,1)S(1)} %collective-permute-done.5.refs_1_), channel_id=1, source_target_pairs={{0,1},{1,0},{2,3},{3,2},{4,5},{5,4},{6,7},{7,6},{8,9},{9,8},{10,11... | collective-permute-start | bytes 3612680 | tf_op jit(solution)/shard_map/ppermute | solution.py:328
  55.9 5.9 %collective-permute-start.10 = (bf16[192,768]{1,0:T(8,128)(2,1)S(1)}, bf16[192,768]{1,0:T(8,128)(2,1)S(1)}, u32[]{:S(2)}, u32[]{:S(2)}) collective-permute-start(bf16[192,768]{1,0:T(8,128)(2,1)S(1)} %pad_maximum_fusion.12), channel_id=1, source_target_pairs={{0,2},{1,5},{2,0},{3,7},{4,6},{5,1},{6,4},{7,3},{8,10},{9,13},{10,... | collective-permute-start | bytes 884744 | tf_op jit(solution)/shard_map/ppermute | solution.py:328
  62.9 10.0 %collective-permute-start.11 = (bf16[384,768]{1,0:T(8,128)(2,1)S(1)}, bf16[384,768]{1,0:T(8,128)(2,1)S(1)}, u32[]{:S(2)}, u32[]{:S(2)}) collective-permute-start(bf16[384,768]{1,0:T(8,128)(2,1)S(1)} %pad_maximum_fusion.7), channel_id=1, source_target_pairs={{0,2},{1,5},{2,0},{3,7},{4,6},{5,1},{6,4},{7,3},{8,10},{9,13},{10,... | collective-permute-start | bytes 1769480 | tf_op jit(solution)/shard_map/ppermute | solution.py:328
  73.0 13.4 %copy-start.13 = (bf16[768,768]{1,0:T(8,128)(2,1)}, bf16[768,768]{1,0:T(8,128)(2,1)S(1)}, u32[]{:S(2)}) copy-start(bf16[768,768]{1,0:T(8,128)(2,1)S(1)} %pad_maximum_fusion.2) | copy-start | bytes 3538948
  73.0 17.9 %collective-permute-start.13 = (bf16[768,768]{1,0:T(8,128)(2,1)S(1)}, bf16[768,768]{1,0:T(8,128)(2,1)S(1)}, u32[]{:S(2)}, u32[]{:S(2)}) collective-permute-start(bf16[768,768]{1,0:T(8,128)(2,1)S(1)} %pad_maximum_fusion.2), channel_id=1, source_target_pairs={{0,1},{1,0},{2,3},{3,2},{4,5},{5,4},{6,7},{7,6},{8,9},{9,8},{10,11... | collective-permute-start | bytes 3538952 | tf_op jit(solution)/shard_map/ppermute | solution.py:328
  74.3 16.6 %collective-permute-start.12 = (bf16[768,768]{1,0:T(8,128)(2,1)S(1)}, bf16[768,768]{1,0:T(8,128)(2,1)S(1)}, u32[]{:S(2)}, u32[]{:S(2)}) collective-permute-start(bf16[768,768]{1,0:T(8,128)(2,1)S(1)} %pad_maximum_fusion.2), channel_id=1, source_target_pairs={{0,4},{1,3},{2,6},{3,1},{4,0},{5,7},{6,2},{7,5},{8,12},{9,11},{10,... | collective-permute-start | bytes 3538952 | tf_op jit(solution)/shard_map/ppermute | solution.py:328
  75.5 15.3 %collective-permute-start.14 = (bf16[384,768]{1,0:T(8,128)(2,1)S(1)}, bf16[384,768]{1,0:T(8,128)(2,1)S(1)}, u32[]{:S(2)}, u32[]{:S(2)}) collective-permute-start(bf16[384,768]{1,0:T(8,128)(2,1)S(1)} %pad_maximum_fusion.8), channel_id=1, source_target_pairs={{0,8},{1,9},{2,10},{3,11},{4,12},{5,13},{6,14},{7,15},{8,0},{9,1},... | collective-permute-start | bytes 1769480 | tf_op jit(solution)/shard_map/ppermute | solution.py:328
  92.2 10.9 %copy-start.14 = (bf16[768,768]{1,0:T(8,128)(2,1)}, bf16[768,768]{1,0:T(8,128)(2,1)S(1)}, u32[]{:S(2)}) copy-start(bf16[768,768]{1,0:T(8,128)(2,1)S(1)} %pad_maximum_fusion.3) | copy-start | bytes 3538948
  92.2 11.0 %collective-permute-start.17 = (bf16[768,768]{1,0:T(8,128)(2,1)S(1)}, bf16[768,768]{1,0:T(8,128)(2,1)S(1)}, u32[]{:S(2)}, u32[]{:S(2)}) collective-permute-start(bf16[768,768]{1,0:T(8,128)(2,1)S(1)} %collective-permute-done.12), channel_id=1, source_target_pairs={{0,1},{1,0},{2,3},{3,2},{4,5},{5,4},{6,7},{7,6},{8,9},{9,8},{10,11... | collective-permute-start | bytes 3538952 | tf_op jit(solution)/shard_map/ppermute | solution.py:328
  92.7 10.5 %collective-permute-start.16 = (bf16[768,768]{1,0:T(8,128)(2,1)S(1)}, bf16[768,768]{1,0:T(8,128)(2,1)S(1)}, u32[]{:S(2)}, u32[]{:S(2)}) collective-permute-start(bf16[768,768]{1,0:T(8,128)(2,1)S(1)} %pad_maximum_fusion.3), channel_id=1, source_target_pairs={{0,1},{1,0},{2,3},{3,2},{4,5},{5,4},{6,7},{7,6},{8,9},{9,8},{10,11... | collective-permute-start | bytes 3538952 | tf_op jit(solution)/shard_map/ppermute | solution.py:328
  92.8 15.5 %collective-permute-start.15 = (bf16[768,768]{1,0:T(8,128)(2,1)S(1)}, bf16[768,768]{1,0:T(8,128)(2,1)}, u32[]{:S(2)}, u32[]{:S(2)}) collective-permute-start(bf16[768,768]{1,0:T(8,128)(2,1)S(1)} %pad_maximum_fusion.3), channel_id=1, source_target_pairs={{0,4},{1,3},{2,6},{3,1},{4,0},{5,7},{6,2},{7,5},{8,12},{9,11},{10,... | collective-permute-start | bytes 3538952 | tf_op jit(solution)/shard_map/ppermute | solution.py:328
  103.2 9.0 %copy-start.29 = (bf16[768,768]{1,0:T(8,128)(2,1)}, bf16[768,768]{1,0:T(8,128)(2,1)S(1)}, u32[]{:S(2)}) copy-start(bf16[768,768]{1,0:T(8,128)(2,1)S(1)} %collective-permute-done.17) | copy-start | bytes 3538948
  103.2 9.0 %copy-start.30 = (bf16[768,768]{1,0:T(8,128)(2,1)}, bf16[768,768]{1,0:T(8,128)(2,1)S(1)}, u32[]{:S(2)}) copy-start(bf16[768,768]{1,0:T(8,128)(2,1)S(1)} %collective-permute-done.16) | copy-start | bytes 3538948
  108.2 4.0 %collective-permute-start.18 = (bf16[768,768]{1,0:T(8,128)(2,1)}, bf16[768,768]{1,0:T(8,128)(2,1)S(1)}, u32[]{:S(2)}, u32[]{:S(2)}) collective-permute-start(bf16[768,768]{1,0:T(8,128)(2,1)} %collective-permute-done.15), channel_id=1, source_target_pairs={{0,1},{1,0},{2,3},{3,2},{4,5},{5,4},{6,7},{7,6},{8,9},{9,8},{10,11... | collective-permute-start | bytes 3538952 | tf_op jit(solution)/shard_map/ppermute | solution.py:328
  162.4 7.0 %collective-permute-start.19 = (bf16[784,768]{1,0:T(8,128)(2,1)}, bf16[784,768]{1,0:T(8,128)(2,1)S(1)}, u32[]{:S(2)}, u32[]{:S(2)}) collective-permute-start(bf16[784,768]{1,0:T(8,128)(2,1)} %get-tuple-element.231), channel_id=1, source_target_pairs={{0,1},{1,0},{2,3},{3,2},{4,5},{5,4},{6,7},{7,6},{8,9},{9,8},{10,11... | collective-permute-start | bytes 3612680 | tf_op jit(solution)/shard_map/ppermute | solution.py:328
  162.9 6.5 %collective-permute-start.20 = (bf16[768,768]{1,0:T(8,128)(2,1)}, bf16[768,768]{1,0:T(8,128)(2,1)S(1)}, u32[]{:S(2)}, u32[]{:S(2)}) collective-permute-start(bf16[768,768]{1,0:T(8,128)(2,1)} %get-tuple-element.232), channel_id=1, source_target_pairs={{0,1},{1,0},{2,3},{3,2},{4,5},{5,4},{6,7},{7,6},{8,9},{9,8},{10,11... | collective-permute-start | bytes 3538952 | tf_op jit(solution)/shard_map/ppermute | solution.py:328
  163.0 6.4 %copy-start.20 = (f32[16,768]{1,0:T(8,128)S(1)}, f32[16,768]{1,0:T(8,128)}, u32[]{:S(2)}) copy-start(f32[16,768]{1,0:T(8,128)} %get-tuple-element.225.sums_ref) | copy-start | bytes 147460
  163.0 7.4 %copy-start.12 = (bf16[768,768]{1,0:T(8,128)(2,1)S(1)}, bf16[768,768]{1,0:T(8,128)(2,1)}, u32[]{:S(2)}) copy-start(bf16[768,768]{1,0:T(8,128)(2,1)} %get-tuple-element.230) | copy-start | bytes 3538948
  170.9 15.7 %collective-permute-start.21 = (bf16[784,768]{1,0:T(8,128)(2,1)S(1)}, bf16[784,768]{1,0:T(8,128)(2,1)S(1)}, u32[]{:S(2)}, u32[]{:S(2)}) collective-permute-start(bf16[784,768]{1,0:T(8,128)(2,1)S(1)} %pad_maximum_fusion.1), channel_id=1, source_target_pairs={{0,4},{1,3},{2,6},{3,1},{4,0},{5,7},{6,2},{7,5},{8,12},{9,11},{10,... | collective-permute-start | bytes 3612680 | tf_op jit(solution)/shard_map/ppermute | solution.py:328
  171.2 13.5 %collective-permute-start.22 = (bf16[768,768]{1,0:T(8,128)(2,1)}, bf16[768,768]{1,0:T(8,128)(2,1)}, u32[]{:S(2)}, u32[]{:S(2)}) collective-permute-start(bf16[768,768]{1,0:T(8,128)(2,1)} %get-tuple-element.250), channel_id=1, source_target_pairs={{0,1},{1,0},{2,3},{3,2},{4,5},{5,4},{6,7},{7,6},{8,9},{9,8},{10,11... | collective-permute-start | bytes 3538952 | tf_op jit(solution)/shard_map/ppermute | solution.py:328
  172.0 12.6 %collective-permute-start.23 = (bf16[768,768]{1,0:T(8,128)(2,1)S(1)}, bf16[768,768]{1,0:T(8,128)(2,1)}, u32[]{:S(2)}, u32[]{:S(2)}) collective-permute-start(bf16[768,768]{1,0:T(8,128)(2,1)S(1)} %copy-done.10), channel_id=1, source_target_pairs={{0,1},{1,0},{2,3},{3,2},{4,5},{5,4},{6,7},{7,6},{8,9},{9,8},{10,11... | collective-permute-start | bytes 3538952 | tf_op jit(solution)/shard_map/ppermute | solution.py:328
  186.6 2.1 copy-start.7
  190.3 15.4 %collective-permute-start.24 = (bf16[768,768]{1,0:T(8,128)(2,1)S(1)}, bf16[768,768]{1,0:T(8,128)(2,1)S(1)}, u32[]{:S(2)}, u32[]{:S(2)}) collective-permute-start(bf16[768,768]{1,0:T(8,128)(2,1)S(1)} %add_convert_fusion.1), channel_id=1, source_target_pairs={{0,4},{1,3},{2,6},{3,1},{4,0},{5,7},{6,2},{7,5},{8,12},{9,11},{10,... | collective-permute-start | bytes 3538952 | tf_op jit(solution)/shard_map/ppermute | solution.py:328
  190.6 13.8 %collective-permute-start.25 = (bf16[400,768]{1,0:T(8,128)(2,1)S(1)}, bf16[400,768]{1,0:T(8,128)(2,1)S(1)}, u32[]{:S(2)}, u32[]{:S(2)}) collective-permute-start(bf16[400,768]{1,0:T(8,128)(2,1)S(1)} %pad_maximum_fusion.5), channel_id=1, source_target_pairs={{0,8},{1,9},{2,10},{3,11},{4,12},{5,13},{6,14},{7,15},{8,0},{9,1},... | collective-permute-start | bytes 1843208 | tf_op jit(solution)/shard_map/ppermute | solution.py:328
  204.5 16.8 %copy-start.17 = (bf16[400,768]{1,0:T(8,128)(2,1)}, bf16[400,768]{1,0:T(8,128)(2,1)S(1)}, u32[]{:S(2)}) copy-start(bf16[400,768]{1,0:T(8,128)(2,1)S(1)} %collective-permute-done.25) | copy-start | bytes 1843204
  208.7 12.5 %collective-permute-start.26 = (bf16[384,768]{1,0:T(8,128)(2,1)S(1)}, bf16[384,768]{1,0:T(8,128)(2,1)S(1)}, u32[]{:S(2)}, u32[]{:S(2)}) collective-permute-start(bf16[384,768]{1,0:T(8,128)(2,1)S(1)} %get-tuple-element.275), channel_id=1, source_target_pairs={{0,2},{1,5},{2,0},{3,7},{4,6},{5,1},{6,4},{7,3},{8,10},{9,13},{10,... | collective-permute-start | bytes 1769480 | tf_op jit(solution)/shard_map/ppermute | solution.py:328
  209.1 12.2 %collective-permute-start.27 = (bf16[208,768]{1,0:T(8,128)(2,1)S(1)}, bf16[208,768]{1,0:T(8,128)(2,1)S(1)}, u32[]{:S(2)}, u32[]{:S(2)}) collective-permute-start(bf16[208,768]{1,0:T(8,128)(2,1)S(1)} %pad_maximum_fusion.10), channel_id=1, source_target_pairs={{0,2},{1,5},{2,0},{3,7},{4,6},{5,1},{6,4},{7,3},{8,10},{9,13},{10,... | collective-permute-start | bytes 958472 | tf_op jit(solution)/shard_map/ppermute | solution.py:328
  221.2 1.6 copy-start.18
  221.3 1.6 copy-start.31
  221.3 8.0 %copy-start.11 = (bf16[768,768]{1,0:T(8,128)(2,1)S(1)}, bf16[768,768]{1,0:T(8,128)(2,1)}, u32[]{:S(2)}) copy-start(bf16[768,768]{1,0:T(8,128)(2,1)} %get-tuple-element.291) | copy-start | bytes 3538948
  222.9 6.4 %collective-permute-start.28 = (bf16[768,768]{1,0:T(8,128)(2,1)S(1)}, bf16[768,768]{1,0:T(8,128)(2,1)S(1)}, u32[]{:S(2)}, u32[]{:S(2)}) collective-permute-start(bf16[768,768]{1,0:T(8,128)(2,1)S(1)} %copy-done.31), channel_id=1, source_target_pairs={{0,1},{1,0},{2,3},{3,2},{4,5},{5,4},{6,7},{7,6},{8,9},{9,8},{10,11... | collective-permute-start | bytes 3538952 | tf_op jit(solution)/shard_map/ppermute | solution.py:328
  225.8 19.8 %collective-permute-start.30 = (bf16[768,768]{1,0:T(8,128)(2,1)}, bf16[768,768]{1,0:T(8,128)(2,1)S(1)}, u32[]{:S(2)}, u32[]{:S(2)}) collective-permute-start(bf16[768,768]{1,0:T(8,128)(2,1)} %get-tuple-element.298), channel_id=1, source_target_pairs={{0,1},{1,0},{2,3},{3,2},{4,5},{5,4},{6,7},{7,6},{8,9},{9,8},{10,11... | collective-permute-start | bytes 3538952 | tf_op jit(solution)/shard_map/ppermute | solution.py:328
  229.6 16.1 %collective-permute-start.29 = (bf16[768,768]{1,0:T(8,128)(2,1)S(1)}, bf16[768,768]{1,0:T(8,128)(2,1)S(1)}, u32[]{:S(2)}, u32[]{:S(2)}) collective-permute-start(bf16[768,768]{1,0:T(8,128)(2,1)S(1)} %add_convert_fusion), channel_id=1, source_target_pairs={{0,4},{1,3},{2,6},{3,1},{4,0},{5,7},{6,2},{7,5},{8,12},{9,11},{10,... | collective-permute-start | bytes 3538952 | tf_op jit(solution)/shard_map/ppermute | solution.py:328
  230.2 15.4 %collective-permute-start.32 = (bf16[112,768]{1,0:T(8,128)(2,1)}, bf16[112,768]{1,0:T(8,128)(2,1)S(1)}, u32[]{:S(2)}, u32[]{:S(2)}) collective-permute-start(bf16[112,768]{1,0:T(8,128)(2,1)} %pad_maximum_fusion.13), channel_id=1, source_target_pairs={{0,16},{1,17},{2,18},{3,19},{4,20},{5,21},{6,22},{7,23},{8,24},{9,... | collective-permute-start | bytes 516104 | tf_op jit(solution)/shard_map/ppermute | solution.py:328
  232.6 13.1 %collective-permute-start.31 = (bf16[192,768]{1,0:T(8,128)(2,1)}, bf16[192,768]{1,0:T(8,128)(2,1)}, u32[]{:S(2)}, u32[]{:S(2)}) collective-permute-start(bf16[192,768]{1,0:T(8,128)(2,1)} %get-tuple-element.299), channel_id=1, source_target_pairs={{0,8},{1,9},{2,10},{3,11},{4,12},{5,13},{6,14},{7,15},{8,0},{9,1},... | collective-permute-start | bytes 884744 | tf_op jit(solution)/shard_map/ppermute | solution.py:328
  234.0 12.6 %copy-start.15 = (bf16[768,768]{1,0:T(8,128)(2,1)S(1)}, bf16[768,768]{1,0:T(8,128)(2,1)}, u32[]{:S(2)}) copy-start(bf16[768,768]{1,0:T(8,128)(2,1)} %get-tuple-element.296) | copy-start | bytes 3538948
  247.5 10.5 %collective-permute-start.33 = (bf16[400,768]{1,0:T(8,128)(2,1)S(1)}, bf16[400,768]{1,0:T(8,128)(2,1)S(1)}, u32[]{:S(2)}, u32[]{:S(2)}) collective-permute-start(bf16[400,768]{1,0:T(8,128)(2,1)S(1)} %pad_maximum_fusion.6), channel_id=1, source_target_pairs={{0,2},{1,5},{2,0},{3,7},{4,6},{5,1},{6,4},{7,3},{8,10},{9,13},{10,... | collective-permute-start | bytes 1843208 | tf_op jit(solution)/shard_map/ppermute | solution.py:328
  248.7 9.3 %collective-permute-start.34 = (bf16[96,768]{1,0:T(8,128)(2,1)S(1)}, bf16[96,768]{1,0:T(8,128)(2,1)S(1)}, u32[]{:S(2)}, u32[]{:S(2)}) collective-permute-start(bf16[96,768]{1,0:T(8,128)(2,1)S(1)} %add_convert_fusion.19), channel_id=1, source_target_pairs={{0,16},{1,17},{2,18},{3,19},{4,20},{5,21},{6,22},{7,23},{8,24},{9,... | collective-permute-start | bytes 442376 | tf_op jit(solution)/shard_map/ppermute | solution.py:328
  258.2 9.6 %copy-start.19 = (bf16[208,768]{1,0:T(8,128)(2,1)S(1)}, bf16[208,768]{1,0:T(8,128)(2,1)}, u32[]{:S(2)}) copy-start(bf16[208,768]{1,0:T(8,128)(2,1)} %copy-done.18) | copy-start | bytes 958468
  258.2 2.7 collective-permute-start.36
  259.7 7.8 %collective-permute-start.35 = (bf16[192,768]{1,0:T(8,128)(2,1)S(1)}, bf16[192,768]{1,0:T(8,128)(2,1)S(1)}, u32[]{:S(2)}, u32[]{:S(2)}) collective-permute-start(bf16[192,768]{1,0:T(8,128)(2,1)S(1)} %get-tuple-element.312), channel_id=1, source_target_pairs={{0,8},{1,9},{2,10},{3,11},{4,12},{5,13},{6,14},{7,15},{8,0},{9,1},... | collective-permute-start | bytes 884744 | tf_op jit(solution)/shard_map/ppermute | solution.py:328
  260.9 3.6 %collective-permute-start.37 = (bf16[16,768]{1,0:T(8,128)(2,1)S(1)}, bf16[16,768]{1,0:T(8,128)(2,1)S(1)}, u32[]{:S(2)}, u32[]{:S(2)}) collective-permute-start(bf16[16,768]{1,0:T(8,128)(2,1)S(1)} %fusion.2), channel_id=1, source_target_pairs={{0,1},{1,0},{2,3},{3,2},{4,5},{5,4},{6,7},{7,6},{8,9},{9,8},{10,11... | collective-permute-start | bytes 73736 | tf_op jit(solution)/shard_map/ppermute | solution.py:328
  267.6 10.1 %collective-permute-start.38 = (bf16[112,768]{1,0:T(8,128)(2,1)S(1)}, bf16[112,768]{1,0:T(8,128)(2,1)S(1)}, u32[]{:S(2)}, u32[]{:S(2)}) collective-permute-start(bf16[112,768]{1,0:T(8,128)(2,1)S(1)} %pad_maximum_fusion.14), channel_id=1, source_target_pairs={{0,16},{1,17},{2,18},{3,19},{4,20},{5,21},{6,22},{7,23},{8,24},{9,... | collective-permute-start | bytes 516104 | tf_op jit(solution)/shard_map/ppermute | solution.py:328
  268.8 14.5 %copy-start.2 = (f32[578,128]{1,0:T(8,128)S(1)}, f32[578,128]{1,0:T(8,128)}, u32[]{:S(2)}) copy-start(f32[578,128]{1,0:T(8,128)} %refs_4_.1) | copy-start | bytes 887812
  268.8 14.5 %copy-start.3 = (f32[1154,128]{1,0:T(8,128)S(1)}, f32[1154,128]{1,0:T(8,128)}, u32[]{:S(2)}) copy-start(f32[1154,128]{1,0:T(8,128)} %refs_8_.1) | copy-start | bytes 1772548
  268.8 14.5 %copy-start.4 = (f32[1154,128]{1,0:T(8,128)S(1)}, f32[1154,128]{1,0:T(8,128)}, u32[]{:S(2)}) copy-start(f32[1154,128]{1,0:T(8,128)} %refs_9_.1) | copy-start | bytes 1772548
  268.8 14.5 %copy-start.5 = (f32[578,128]{1,0:T(8,128)S(1)}, f32[578,128]{1,0:T(8,128)}, u32[]{:S(2)}) copy-start(f32[578,128]{1,0:T(8,128)} %refs_5_.1) | copy-start | bytes 887812
  268.8 14.5 %copy-start.6 = (f32[578,128]{1,0:T(8,128)S(1)}, f32[578,128]{1,0:T(8,128)}, u32[]{:S(2)}) copy-start(f32[578,128]{1,0:T(8,128)} %refs_6_.1) | copy-start | bytes 887812
  277.8 5.5 %collective-permute-start.39 = (f32[128,128]{1,0:T(8,128)S(1)}, f32[128,128]{1,0:T(8,128)S(1)}, u32[]{:S(2)}, u32[]{:S(2)}) collective-permute-start(f32[128,128]{1,0:T(8,128)S(1)} %get-tuple-element.322), channel_id=1, source_target_pairs={{1,0},{2,1},{3,2},{4,3},{5,4},{6,5},{7,6},{8,7},{9,8},{10,9},{11,1... | collective-permute-start | bytes 196616 | tf_op jit(solution)/shard_map/ppermute | solution.py:1404
  (9 other events, 9.9 us)
where the time goes:
time: 286 us; the launch traced here: 285 us
  Pallas kernels  135 us (47%)
  waiting for transfers between devices  85.4 us (30%)
  starting transfers between devices  42.8 us (15%)
  other arithmetic  12.1 us (4%)
  local copies, waits for them, and re-layouts  8.37 us (3%)
    ppermute x38, waiting for transfers between devices, exchange(): return lax.ppermute(array, 'fsdp', stage_perm(stage))  79.2 us
    ppermute x38, starting transfers between devices, exchange(): return lax.ppermute(array, 'fsdp', stage_perm(stage))  38.2 us
    pallas_call x1, Pallas kernels, feed_forward(): pl.pallas_call(ffn_kernel, grid=(tok // FFN_TILE,), out_shape=(bf(width),...  35.5 us
    pallas_call x2, Pallas kernels, attention_backward(): pl.pallas_call(functools.partial(backward_kernel, len(held)), grid=(width...  24.6 us
    pallas_call x2, Pallas kernels, attention_forward(): pl.pallas_call(functools.partial(forward_kernel, len(held)), grid=(pairs...  20.6 us
    pallas_call x1, Pallas kernels, ffn_grads(): pl.pallas_call(ffn_grad_kernel, grid=(6,), out_shape=part_shapes(width, F...  13.7 us
    pallas_call x1, Pallas kernels, input_grads(): pl.pallas_call(input_grad_kernel, grid=(tok // rows,), out_shape=(jax.Sha...  11.6 us
    pallas_call x1, Pallas kernels, project(): pl.pallas_call(project_kernel, grid=(tok // rows,), out_shape=(bf, jax.Sh...  9.72 us
  transfers between devices with their start and end apart: 40, of which 22 were waited for; matrix products, arithmetic and copies ran while one was open for 1% of the time, Pallas kernels for 29%

commit v1 on v0

--- a/solution.py
+++ b/solution.py
@@ -447,7 +447,7 @@
         out_specs=(spec_vmem(),) * 3,
         scratch_shapes=[
             pltpu.VMEM((64 + att_rows + 6, LANES), F32),
-            pltpu.VMEM((64 + ffn_rows + 6, LANES), F32),
+            pltpu.VMEM((64 + ffn_rows + 30, LANES), F32),
         ],
         compiler_params=params(16),
         name="prep",
@@ -1062,7 +1062,7 @@
         + [spec_any() for _ in held],
         out_specs=(tile(), tile(), tile()),
         input_output_aliases={6 + i: i for i in range(len(held))},
-        compiler_params=params(BIG),
+        compiler_params=params(54),
         cost_estimate=pl.CostEstimate(
             flops=40 * seq * seq * width,
             bytes_accessed=6 * MIB,
@@ -1368,20 +1368,20 @@
     kept_b, sent_b = halve(kept_b, got_b[: 4 * SLOT])
     sent_a, sent_b, dq = phase(sent_a, add_small(sent_b, small_sum), dq)
     part = att_grads(ctx, dob, stream, dq, dk, dv)
-    got_a, got_b, part = phase(exchange(sent_a, 2), exchange(sent_b, 2), part)
+    high = exchange(part[3], 4)
+    got_a, got_b, kept = phase(exchange(sent_a, 2), exchange(sent_b, 2), part[0])
     kept_a, sent_a = halve(kept_a, got_a)
     small_sum = small_sum + got_b[2 * SLOT :].astype(F32)
     kept_b, sent_b = halve(kept_b, got_b[: 2 * SLOT])
-    sent_a, sent_b, part = phase(sent_a, add_small(sent_b, small_sum), part)
+    high, sent_a, sent_b = phase(high, sent_a, add_small(sent_b, small_sum))
     got_b = exchange(sent_b, 0)
-    high = exchange(part[3], 4)
     high = total_of((part[1], high), 0, 8 * SLOT).astype(BF)
     high, sent_a, dq = phase(high, sent_a, dq)
     input_grad, late = input_grads(dq, dk, dv, dob, masked_row, att)
     got, low, got_a, got_b, late = phase(
         exchange(high, 3), exchange(part[2], 4), exchange(sent_a, 1), got_b, late
     )
-    kept, sent = halve(part[0], low, got)
+    kept, sent = halve(kept, low, got)
     kept_a, sent_a = halve(kept_a, got_a)
     sent, sent_a, late = phase(sent, sent_a, late)
     got, got_a = phase(exchange(add_small(sent, late), 2), exchange(sent_a, 0))

time: 286 us -> 281 us (0.983)
  waiting for transfers between devices: 85.4 us -> 80.2 us
    ppermute x38, waiting for transfers between devices: 79.2 us -> 75.1 us  [exchange(): return lax.ppermute(array, 'fsdp', stage_perm(stage))]
  transfers between devices with their start and end apart: 40 -> 40, of which waited for: 22 -> 21; matrix products, arithmetic and copies ran while one was open for 1% -> 2% of each run, Pallas kernels for 29% -> 29%
where the time goes in v1:
time: 281 us; the launch traced here: 280 us
  Pallas kernels  135 us (48%)
  waiting for transfers between devices  80.2 us (29%)
  starting transfers between devices  44.3 us (16%)
  other arithmetic  9.51 us (3%)
  local copies, waits for them, and re-layouts  9.03 us (3%)
    ppermute x38, waiting for transfers between devices, exchange(): return lax.ppermute(array, 'fsdp', stage_perm(stage))  75.1 us
    ppermute x38, starting transfers between devices, exchange(): return lax.ppermute(array, 'fsdp', stage_perm(stage))  38.6 us
    pallas_call x1, Pallas kernels, feed_forward(): pl.pallas_call(ffn_kernel, grid=(tok // FFN_TILE,), out_shape=(bf(width),...  35.5 us
    pallas_call x2, Pallas kernels, attention_backward(): pl.pallas_call(functools.partial(backward_kernel, len(held)), grid=(width...  24.6 us
    pallas_call x2, Pallas kernels, attention_forward(): pl.pallas_call(functools.partial(forward_kernel, len(held)), grid=(pairs...  20.6 us
    pallas_call x1, Pallas kernels, ffn_grads(): pl.pallas_call(ffn_grad_kernel, grid=(6,), out_shape=part_shapes(width, F...  13.7 us
    pallas_call x1, Pallas kernels, input_grads(): pl.pallas_call(input_grad_kernel, grid=(tok // rows,), out_shape=(jax.Sha...  11.6 us
    pallas_call x1, Pallas kernels, project(): pl.pallas_call(project_kernel, grid=(tok // rows,), out_shape=(bf, jax.Sh...  9.72 us
  transfers between devices with their start and end apart: 40, of which 21 were waited for; matrix products, arithmetic and copies ran while one was open for 2% of the time, Pallas kernels for 29%

profile of v1, /device:TPU:7, one launch (start us, length us, event | category | flops | bytes accessed | tf_op | source)
XLA Modules:
  0.0 279.7 jit_solution(17719540135628491195)
XLA Ops:
  0.7 1.5 row_tails.1
  2.2 3.7 %collective-permute-start = (f32[128,128]{1,0:T(8,128)}, f32[128,128]{1,0:T(8,128)S(1)}, u32[]{:S(2)}, u32[]{:S(2)}) collective-permute-start(f32[128,128]{1,0:T(8,128)} %row_tails.1), channel_id=1, source_target_pairs={{0,1},{1,2},{2,3},{3,4},{4,5},{5,6},{6,7},{7,8},{8,9},{9,10},{10,1... | collective-permute-start | bytes 196616 | tf_op jit(solution)/shard_map/ppermute | solution.py:1311
  5.9 1.6 collective-permute-done.tail_ref
  7.5 1.0 copy-done.1
  8.7 2.3 collective-permute-start.1
  12.2 6.4 %collective-permute-done.1 = bf16[112,768]{1,0:T(8,128)(2,1)S(1)} collective-permute-done((bf16[112,768]{1,0:T(8,128)(2,1)S(1)}, bf16[112,768]{1,0:T(8,128)(2,1)S(1)}, u32[]{:S(2)}, u32[]{:S(2)}) %collective-permute-start.1) | collective-permute-done | bytes 172064 | tf_op jit(solution)/shard_map/ppermute | solution.py:328
  18.7 7.4 %collective-permute-done.2 = bf16[208,768]{1,0:T(8,128)(2,1)S(1)} collective-permute-done((bf16[208,768]{1,0:T(8,128)(2,1)S(1)}, bf16[208,768]{1,0:T(8,128)(2,1)S(1)}, u32[]{:S(2)}, u32[]{:S(2)}) %collective-permute-start.2) | collective-permute-done | bytes 319520 | tf_op jit(solution)/shard_map/ppermute | solution.py:328
  26.8 4.2 %collective-permute-start.4 = (bf16[96,768]{1,0:T(8,128)(2,1)S(1)}, bf16[96,768]{1,0:T(8,128)(2,1)S(1)}, u32[]{:S(2)}, u32[]{:S(2)}) collective-permute-start(bf16[96,768]{1,0:T(8,128)(2,1)S(1)} %get-tuple-element.169), channel_id=1, source_target_pairs={{0,16},{1,17},{2,18},{3,19},{4,20},{5,21},{6,22},{7,23},{8,24},{9,... | collective-permute-start | bytes 442376 | tf_op jit(solution)/shard_map/ppermute | solution.py:328
  31.0 6.5 %collective-permute-done.4 = bf16[96,768]{1,0:T(8,128)(2,1)S(1)} collective-permute-done((bf16[96,768]{1,0:T(8,128)(2,1)S(1)}, bf16[96,768]{1,0:T(8,128)(2,1)S(1)}, u32[]{:S(2)}, u32[]{:S(2)}) %collective-permute-start.4) | collective-permute-done | bytes 147488 | tf_op jit(solution)/shard_map/ppermute | solution.py:328
  37.8 1.4 collective-permute-start.6
  40.1 3.1 %collective-permute-start.8 = (bf16[96,768]{1,0:T(8,128)(2,1)S(1)}, bf16[96,768]{1,0:T(8,128)(2,1)S(1)}, u32[]{:S(2)}, u32[]{:S(2)}) collective-permute-start(bf16[96,768]{1,0:T(8,128)(2,1)S(1)} %get-tuple-element.175), channel_id=1, source_target_pairs={{0,16},{1,17},{2,18},{3,19},{4,20},{5,21},{6,22},{7,23},{8,24},{9,... | collective-permute-start | bytes 442376 | tf_op jit(solution)/shard_map/ppermute | solution.py:328
  43.2 5.3 %collective-permute-done.8 = bf16[96,768]{1,0:T(8,128)(2,1)S(1)} collective-permute-done((bf16[96,768]{1,0:T(8,128)(2,1)S(1)}, bf16[96,768]{1,0:T(8,128)(2,1)S(1)}, u32[]{:S(2)}, u32[]{:S(2)}) %collective-permute-start.8) | collective-permute-done | bytes 147488 | tf_op jit(solution)/shard_map/ppermute | solution.py:328
  48.4 2.4 collective-permute-done.7
  50.9 4.0 %collective-permute-done.5.refs_1_ = bf16[784,768]{1,0:T(8,128)(2,1)S(1)} collective-permute-done((bf16[784,768]{1,0:T(8,128)(2,1)S(1)}, bf16[784,768]{1,0:T(8,128)(2,1)S(1)}, u32[]{:S(2)}, u32[]{:S(2)}) %collective-permute-start.5) | collective-permute-done | bytes 1204256 | tf_op jit(solution)/shard_map/ppermute | solution.py:328
  54.9 1.0 collective-permute-start.9
  56.1 5.7 %collective-permute-done.10 = bf16[192,768]{1,0:T(8,128)(2,1)S(1)} collective-permute-done((bf16[192,768]{1,0:T(8,128)(2,1)S(1)}, bf16[192,768]{1,0:T(8,128)(2,1)S(1)}, u32[]{:S(2)}, u32[]{:S(2)}) %collective-permute-start.10) | collective-permute-done | bytes 294944 | tf_op jit(solution)/shard_map/ppermute | solution.py:328
  61.8 1.0 copy-done.27
  63.1 9.7 %project.1 = (bf16[1024,768]{1,0:T(8,128)(2,1)}, bf16[3,1024,768]{2,1,0:T(8,128)(2,1)}, f32[16,768]{1,0:T(8,128)}) custom-call(bf16[1024,768]{1,0:T(8,128)(2,1)} %x_ref, s32[2,1,512]{2,1,0:T(1,128)} %reshape.50.masked_ref, bf16[784,768]{1,0:T(8,128)(2,1)} %copy-done.9, bf16[784,768]{1,0:T(8,128)(2,1)} %copy-done.26, bf16[784,768]{1,0:T(8,128)(2,1)} %copy-done.25, ...), custom_call_target="tpu_custom_call" | custom-call | flops 3623878656 | bytes 16777216 | tf_op jit(solution)/shard_map/project/pallas_call | solution.py:583
  73.0 1.3 collective-permute-start.13
  74.3 1.3 collective-permute-start.12
  76.1 10.3 %attention_forward.2 = (bf16[1024,768]{1,0:T(8,128)(2,1)}, f32[2,6,2,512]{3,2,1,0:T(2,128)}) custom-call(bf16[3,1024,768]{2,1,0:T(8,128)(2,1)} %get-tuple-element.195.q_ref.k_ref.v_ref, bf16[3,1024,768]{2,1,0:T(8,128)(2,1)} %get-tuple-element.195.q_ref.k_ref.v_ref, bf16[3,1024,768]{2,1,0:T(8,128)(2,1)} %get-tuple-element.195.q_ref.k_ref.v_ref, ...), custom_call_target="tpu_custom_call" | custom-call | flops 3221225472 | bytes 4194304 | tf_op jit(solution)/shard_map/attention_forward/pallas_call | solution.py:647
  86.4 4.4 %collective-permute-done.14 = bf16[384,768]{1,0:T(8,128)(2,1)S(1)} collective-permute-done((bf16[384,768]{1,0:T(8,128)(2,1)S(1)}, bf16[384,768]{1,0:T(8,128)(2,1)S(1)}, u32[]{:S(2)}, u32[]{:S(2)}) %collective-permute-start.14) | collective-permute-done | bytes 589856 | tf_op jit(solution)/shard_map/ppermute | solution.py:328
  90.9 0.9 copy-done.28
  92.9 10.3 %attention_forward.3 = (bf16[1024,768]{1,0:T(8,128)(2,1)}, f32[2,6,2,512]{3,2,1,0:T(2,128)}) custom-call(bf16[3,1024,768]{2,1,0:T(8,128)(2,1)} %get-tuple-element.195.q_ref.k_ref.v_ref, bf16[3,1024,768]{2,1,0:T(8,128)(2,1)} %get-tuple-element.195.q_ref.k_ref.v_ref, ...), custom_call_target="tpu_custom_call", output_to_operand_aliasing={{0}: (4, {}), {1}: (5, {})} | custom-call | flops 3221225472 | bytes 4194304 | tf_op jit(solution)/shard_map/attention_forward/pallas_call | solution.py:647
  103.2 5.0 %collective-permute-done.15 = bf16[768,768]{1,0:T(8,128)(2,1)} collective-permute-done((bf16[768,768]{1,0:T(8,128)(2,1)S(1)}, bf16[768,768]{1,0:T(8,128)(2,1)}, u32[]{:S(2)}, u32[]{:S(2)}) %collective-permute-start.15) | collective-permute-done | bytes 1179680 | tf_op jit(solution)/shard_map/ppermute | solution.py:328
  108.2 1.3 collective-permute-start.18
  109.5 2.7 collective-permute-done.18
  112.2 1.0 copy-done.32
  113.2 35.5 %feed_forward.1 = (bf16[1024,768]{1,0:T(8,128)(2,1)}, bf16[1024,768]{1,0:T(8,128)(2,1)}, bf16[1024,3072]{1,0:T(8,128)(2,1)}, bf16[1024,3072]{1,0:T(8,128)(2,1)},...) custom-call(bf16[1024,768]{1,0:T(8,128)(2,1)} %get-tuple-element.188.stre, ...), custom_call_target="tpu_custom_call" | custom-call | flops 19327352832 | bytes 41943040 | tf_op jit(solution)/shard_map/feed_forward/pallas_call | solution.py:799
  148.7 13.7 %ffn_grads.1 = (bf16[768,768]{1,0:T(8,128)(2,1)}, bf16[768,768]{1,0:T(8,128)(2,1)}, bf16[768,768]{1,0:T(8,128)(2,1)}, bf16[768,768]{1,0:T(8,128)(2,1)}, bf16[768...) custom-call(bf16[1024,768]{1,0:T(8,128)(2,1)} %get-tuple-element.216.x_ref, ...), custom_call_target="tpu_custom_call" | custom-call | flops 7247757312 | bytes 25165824 | tf_op jit(solution)/shard_map/ffn_grads/pallas_call | solution.py:950
  163.0 6.4 %ffn_rest.1 = (bf16[768,768]{1,0:T(8,128)(2,1)}, bf16[768,768]{1,0:T(8,128)(2,1)}, bf16[768,768]{1,0:T(8,128)(2,1)}, bf16[768,768]{1,0:T(8,128)(2,1)}) custom-call(bf16[1024,768]{1,0:T(8,128)(2,1)} %get-tuple-element.216.x_ref, ...), custom_call_target="tpu_custom_call", output_to_operand_aliasing={{0}: (2, {}), {1}: (3, {}), {2}: (4, {}), {3}: (5, {})} | custom-call | flops 2415919104 | bytes 8388608 | tf_op jit(solution)/shard_map/ffn_rest/pallas_call | solution.py:985
  169.4 1.0 copy-done.17
  171.2 0.9 copy-done.11
  172.8 12.3 %attention_backward.2 = (bf16[1024,768]{1,0:T(8,128)(2,1)}, bf16[1024,768]{1,0:T(8,128)(2,1)}, bf16[1024,768]{1,0:T(8,128)(2,1)}) custom-call(bf16[3,1024,768]{2,1,0:T(8,128)(2,1)} %get-tuple-element.195.q_ref.k_ref.v_ref, bf16[3,1024,768]{2,1,0:T(8,128)(2,1)} %get-tuple-element.195.q_ref.k_ref.v_ref, ...), custom_call_target="tpu_custom_call" | custom-call | flops 8053063680 | bytes 6291456 | tf_op jit(solution)/shard_map/attention_backward/pallas_call | solution.py:1057
  185.0 1.5 collective-permute-done.21
  186.6 2.1 add_convert_fusion.6
  189.4 0.8 collective-permute-start.25
  190.2 12.4 %attention_backward.3 = (bf16[1024,768]{1,0:T(8,128)(2,1)}, bf16[1024,768]{1,0:T(8,128)(2,1)}, bf16[1024,768]{1,0:T(8,128)(2,1)}) custom-call(bf16[3,1024,768]{2,1,0:T(8,128)(2,1)} %get-tuple-element.195.q_ref.k_ref.v_ref, bf16[3,1024,768]{2,1,0:T(8,128)(2,1)} %get-tuple-element.195.q_ref.k_ref.v_ref, ...), custom_call_target="tpu_custom_call", output_to_operand_aliasing={{0}: (6, {}), {1}: (7, {}), {2}: (8, {})} | custom-call | flops 8053063680 | bytes 6291456 | tf_op jit(solution)/shard_map/attention_backward/pallas_call | solution.py:1057
  202.5 0.7 collective-permute-done.25
  203.2 1.3 collective-permute-done.24
  204.7 1.1 copy-done.8
  206.6 9.4 %att_grads.1 = (bf16[768,768]{1,0:T(8,128)(2,1)}, bf16[768,768]{1,0:T(8,128)(2,1)}, bf16[768,768]{1,0:T(8,128)(2,1)}, bf16[768,768]{1,0:T(8,128)(2,1)}) custom-call(bf16[1024,768]{1,0:T(8,128)(2,1)} %get-tuple-element.208.ctx_ref.refs_0_, bf16[1024,768]{1,0:T(8,128)(2,1)} %get-tuple-element.215.refs_1_.dob_ref, ...), custom_call_target="tpu_custom_call" | custom-call | flops 4831838208 | bytes 16777216 | tf_op jit(solution)/shard_map/att_grads/pallas_call | solution.py:1164
  216.0 2.7 collective-permute-start.26
  218.9 1.0 collective-permute-start.30
  219.9 4.9 %collective-permute-done.28 = bf16[208,768]{1,0:T(8,128)(2,1)S(1)} collective-permute-done((bf16[208,768]{1,0:T(8,128)(2,1)S(1)}, bf16[208,768]{1,0:T(8,128)(2,1)S(1)}, u32[]{:S(2)}, u32[]{:S(2)}) %collective-permute-start.28) | collective-permute-done | bytes 319520 | tf_op jit(solution)/shard_map/ppermute | solution.py:328
  225.6 0.9 add_convert_fusion.11
  226.7 1.0 collective-permute-start.29
  227.7 2.4 collective-permute-start.32
  230.1 1.5 collective-permute-start.31
  231.5 11.6 %input_grads.1 = (f32[1024,768]{1,0:T(8,128)}, f32[16,768]{1,0:T(8,128)}) custom-call(bf16[1024,768]{1,0:T(8,128)(2,1)} %get-tuple-element.282.refs_3_.dq_ref, bf16[1024,768]{1,0:T(8,128)(2,1)} %get-tuple-element.271.refs_4_.dk_ref, bf16[1024,768]{1,0:T(8,128)(2,1)} %get-tuple-element.272.refs_5_.dv_ref, ...), custom_call_target="tpu_custom_call" | custom-call | flops 3623878656 | bytes 16777216 | tf_op jit(solution)/shard_map/input_grads/pallas_call | solution.py:1108
  243.2 1.0 add_convert_fusion.19
  245.0 1.2 collective-permute-start.33
  246.3 1.3 collective-permute-start.34
  247.5 7.8 %collective-permute-done.34 = bf16[96,768]{1,0:T(8,128)(2,1)S(1)} collective-permute-done((bf16[96,768]{1,0:T(8,128)(2,1)S(1)}, bf16[96,768]{1,0:T(8,128)(2,1)S(1)}, u32[]{:S(2)}, u32[]{:S(2)}) %collective-permute-start.34) | collective-permute-done | bytes 147488 | tf_op jit(solution)/shard_map/ppermute | solution.py:328
  256.1 2.1 collective-permute-done.36
  258.3 3.1 %collective-permute-start.37 = (bf16[16,768]{1,0:T(8,128)(2,1)S(1)}, bf16[16,768]{1,0:T(8,128)(2,1)S(1)}, u32[]{:S(2)}, u32[]{:S(2)}) collective-permute-start(bf16[16,768]{1,0:T(8,128)(2,1)S(1)} %fusion.2), channel_id=1, source_target_pairs={{0,1},{1,0},{2,3},{3,2},{4,5},{5,4},{6,7},{7,6},{8,9},{9,8},{10,11... | collective-permute-start | bytes 73736 | tf_op jit(solution)/shard_map/ppermute | solution.py:328
  261.4 0.8 collective-permute-done.37
  262.7 1.5 collective-permute-start.38
  264.2 1.0 convert_add_fusion
  265.4 0.9 convert_add_fusion.3
  266.3 5.8 %collective-permute-done.38.got_ref = bf16[112,768]{1,0:T(8,128)(2,1)S(1)} collective-permute-done((bf16[112,768]{1,0:T(8,128)(2,1)S(1)}, bf16[112,768]{1,0:T(8,128)(2,1)S(1)}, u32[]{:S(2)}, u32[]{:S(2)}) %collective-permute-start.38) | collective-permute-done | bytes 172064 | tf_op jit(solution)/shard_map/ppermute | solution.py:328
  272.2 2.0 collective-permute-start.39
  274.3 3.5 %collective-permute-done.39.refs_2_ = f32[128,128]{1,0:T(8,128)S(1)} collective-permute-done((f32[128,128]{1,0:T(8,128)S(1)}, f32[128,128]{1,0:T(8,128)S(1)}, u32[]{:S(2)}, u32[]{:S(2)}) %collective-permute-start.39) | collective-permute-done | bytes 65568 | tf_op jit(solution)/shard_map/ppermute | solution.py:1404
  277.8 1.9 update.1
  (146 shorter events, 13.0 us)
Async XLA Ops:
  0.6 6.8 %copy-start = (f32[1154,128]{1,0:T(8,128)S(1)}, f32[1154,128]{1,0:T(8,128)}, u32[]{:S(2)}) copy-start(f32[1154,128]{1,0:T(8,128)} %refs_7_.1) | copy-start | bytes 1772548
  0.7 10.3 %copy-start.23 = (s32[2,512]{1,0:T(2,128)S(1)}, s32[2,512]{1,0:T(2,128)}, u32[]{:S(2)}) copy-start(s32[2,512]{1,0:T(2,128)} %param.11) | copy-start | bytes 12292
  0.7 10.9 %copy-start.24 = (s32[2,512]{1,0:T(2,128)S(1)}, s32[2,512]{1,0:T(2,128)}, u32[]{:S(2)}) copy-start(s32[2,512]{1,0:T(2,128)} %param.12) | copy-start | bytes 12292
  2.2 5.3 %collective-permute-start = (f32[128,128]{1,0:T(8,128)}, f32[128,128]{1,0:T(8,128)S(1)}, u32[]{:S(2)}, u32[]{:S(2)}) collective-permute-start(f32[128,128]{1,0:T(8,128)} %row_tails.1), channel_id=1, source_target_pairs={{0,1},{1,2},{2,3},{3,4},{4,5},{5,6},{6,7},{7,8},{8,9},{9,10},{10,1... | collective-permute-start | bytes 196616 | tf_op jit(solution)/shard_map/ppermute | solution.py:1311
  8.7 9.9 %collective-permute-start.1 = (bf16[112,768]{1,0:T(8,128)(2,1)S(1)}, bf16[112,768]{1,0:T(8,128)(2,1)S(1)}, u32[]{:S(2)}, u32[]{:S(2)}) collective-permute-start(bf16[112,768]{1,0:T(8,128)(2,1)S(1)} %get-tuple-element.165), channel_id=1, source_target_pairs={{0,16},{1,17},{2,18},{3,19},{4,20},{5,21},{6,22},{7,23},{8,24},{9,... | collective-permute-start | bytes 516104 | tf_op jit(solution)/shard_map/ppermute | solution.py:328
  18.6 7.5 %collective-permute-start.2 = (bf16[208,768]{1,0:T(8,128)(2,1)S(1)}, bf16[208,768]{1,0:T(8,128)(2,1)S(1)}, u32[]{:S(2)}, u32[]{:S(2)}) collective-permute-start(bf16[208,768]{1,0:T(8,128)(2,1)S(1)} %pad_maximum_fusion.9), channel_id=1, source_target_pairs={{0,8},{1,9},{2,10},{3,11},{4,12},{5,13},{6,14},{7,15},{8,0},{9,1},... | collective-permute-start | bytes 958472 | tf_op jit(solution)/shard_map/ppermute | solution.py:328
  26.2 11.4 %collective-permute-start.3 = (bf16[400,768]{1,0:T(8,128)(2,1)S(1)}, bf16[400,768]{1,0:T(8,128)(2,1)S(1)}, u32[]{:S(2)}, u32[]{:S(2)}) collective-permute-start(bf16[400,768]{1,0:T(8,128)(2,1)S(1)} %pad_maximum_fusion.4), channel_id=1, source_target_pairs={{0,2},{1,5},{2,0},{3,7},{4,6},{5,1},{6,4},{7,3},{8,10},{9,13},{10,... | collective-permute-start | bytes 1843208 | tf_op jit(solution)/shard_map/ppermute | solution.py:328
  26.8 10.7 %collective-permute-start.4 = (bf16[96,768]{1,0:T(8,128)(2,1)S(1)}, bf16[96,768]{1,0:T(8,128)(2,1)S(1)}, u32[]{:S(2)}, u32[]{:S(2)}) collective-permute-start(bf16[96,768]{1,0:T(8,128)(2,1)S(1)} %get-tuple-element.169), channel_id=1, source_target_pairs={{0,16},{1,17},{2,18},{3,19},{4,20},{5,21},{6,22},{7,23},{8,24},{9,... | collective-permute-start | bytes 442376 | tf_op jit(solution)/shard_map/ppermute | solution.py:328
  37.8 25.1 %copy-start.9 = (bf16[784,768]{1,0:T(8,128)(2,1)}, bf16[784,768]{1,0:T(8,128)(2,1)S(1)}, u32[]{:S(2)}) copy-start(bf16[784,768]{1,0:T(8,128)(2,1)S(1)} %pad_maximum_fusion.refs_0_) | copy-start | bytes 3612676
  37.8 13.1 %collective-permute-start.6 = (bf16[784,768]{1,0:T(8,128)(2,1)S(1)}, bf16[784,768]{1,0:T(8,128)(2,1)S(1)}, u32[]{:S(2)}, u32[]{:S(2)}) collective-permute-start(bf16[784,768]{1,0:T(8,128)(2,1)S(1)} %pad_maximum_fusion.refs_0_), channel_id=1, source_target_pairs={{0,1},{1,0},{2,3},{3,2},{4,5},{5,4},{6,7},{7,6},{8,9},{9,8},{10,11... | collective-permute-start | bytes 3612680 | tf_op jit(solution)/shard_map/ppermute | solution.py:328
  39.2 15.6 %collective-permute-start.5 = (bf16[784,768]{1,0:T(8,128)(2,1)S(1)}, bf16[784,768]{1,0:T(8,128)(2,1)S(1)}, u32[]{:S(2)}, u32[]{:S(2)}) collective-permute-start(bf16[784,768]{1,0:T(8,128)(2,1)S(1)} %pad_maximum_fusion.refs_0_), channel_id=1, source_target_pairs={{0,4},{1,3},{2,6},{3,1},{4,0},{5,7},{6,2},{7,5},{8,12},{9,11},{10,... | collective-permute-start | bytes 3612680 | tf_op jit(solution)/shard_map/ppermute | solution.py:328
  39.4 11.4 %collective-permute-start.7 = (bf16[192,768]{1,0:T(8,128)(2,1)S(1)}, bf16[192,768]{1,0:T(8,128)(2,1)S(1)}, u32[]{:S(2)}, u32[]{:S(2)}) collective-permute-start(bf16[192,768]{1,0:T(8,128)(2,1)S(1)} %pad_maximum_fusion.11), channel_id=1, source_target_pairs={{0,8},{1,9},{2,10},{3,11},{4,12},{5,13},{6,14},{7,15},{8,0},{9,1},... | collective-permute-start | bytes 884744 | tf_op jit(solution)/shard_map/ppermute | solution.py:328
  40.1 8.4 %collective-permute-start.8 = (bf16[96,768]{1,0:T(8,128)(2,1)S(1)}, bf16[96,768]{1,0:T(8,128)(2,1)S(1)}, u32[]{:S(2)}, u32[]{:S(2)}) collective-permute-start(bf16[96,768]{1,0:T(8,128)(2,1)S(1)} %get-tuple-element.175), channel_id=1, source_target_pairs={{0,16},{1,17},{2,18},{3,19},{4,20},{5,21},{6,22},{7,23},{8,24},{9,... | collective-permute-start | bytes 442376 | tf_op jit(solution)/shard_map/ppermute | solution.py:328
  50.9 12.0 %copy-start.25 = (bf16[784,768]{1,0:T(8,128)(2,1)}, bf16[784,768]{1,0:T(8,128)(2,1)S(1)}, u32[]{:S(2)}) copy-start(bf16[784,768]{1,0:T(8,128)(2,1)S(1)} %collective-permute-done.6.refs_2_) | copy-start | bytes 3612676
  54.8 8.3 %copy-start.26 = (bf16[784,768]{1,0:T(8,128)(2,1)}, bf16[784,768]{1,0:T(8,128)(2,1)S(1)}, u32[]{:S(2)}) copy-start(bf16[784,768]{1,0:T(8,128)(2,1)S(1)} %collective-permute-done.5.refs_1_) | copy-start | bytes 3612676
  54.9 6.9 %collective-permute-start.9 = (bf16[784,768]{1,0:T(8,128)(2,1)S(1)}, bf16[784,768]{1,0:T(8,128)(2,1)S(1)}, u32[]{:S(2)}, u32[]{:S(2)}) collective-permute-start(bf16[784,768]{1,0:T(8,128)(2,1)S(1)} %collective-permute-done.5.refs_1_), channel_id=1, source_target_pairs={{0,1},{1,0},{2,3},{3,2},{4,5},{5,4},{6,7},{7,6},{8,9},{9,8},{10,11... | collective-permute-start | bytes 3612680 | tf_op jit(solution)/shard_map/ppermute | solution.py:328
  55.9 5.9 %collective-permute-start.10 = (bf16[192,768]{1,0:T(8,128)(2,1)S(1)}, bf16[192,768]{1,0:T(8,128)(2,1)S(1)}, u32[]{:S(2)}, u32[]{:S(2)}) collective-permute-start(bf16[192,768]{1,0:T(8,128)(2,1)S(1)} %pad_maximum_fusion.12), channel_id=1, source_target_pairs={{0,2},{1,5},{2,0},{3,7},{4,6},{5,1},{6,4},{7,3},{8,10},{9,13},{10,... | collective-permute-start | bytes 884744 | tf_op jit(solution)/shard_map/ppermute | solution.py:328
  62.9 10.0 %collective-permute-start.11 = (bf16[384,768]{1,0:T(8,128)(2,1)S(1)}, bf16[384,768]{1,0:T(8,128)(2,1)S(1)}, u32[]{:S(2)}, u32[]{:S(2)}) collective-permute-start(bf16[384,768]{1,0:T(8,128)(2,1)S(1)} %pad_maximum_fusion.7), channel_id=1, source_target_pairs={{0,2},{1,5},{2,0},{3,7},{4,6},{5,1},{6,4},{7,3},{8,10},{9,13},{10,... | collective-permute-start | bytes 1769480 | tf_op jit(solution)/shard_map/ppermute | solution.py:328
  73.0 13.4 %copy-start.14 = (bf16[768,768]{1,0:T(8,128)(2,1)}, bf16[768,768]{1,0:T(8,128)(2,1)S(1)}, u32[]{:S(2)}) copy-start(bf16[768,768]{1,0:T(8,128)(2,1)S(1)} %pad_maximum_fusion.2) | copy-start | bytes 3538948
  73.0 17.9 %collective-permute-start.13 = (bf16[768,768]{1,0:T(8,128)(2,1)S(1)}, bf16[768,768]{1,0:T(8,128)(2,1)S(1)}, u32[]{:S(2)}, u32[]{:S(2)}) collective-permute-start(bf16[768,768]{1,0:T(8,128)(2,1)S(1)} %pad_maximum_fusion.2), channel_id=1, source_target_pairs={{0,1},{1,0},{2,3},{3,2},{4,5},{5,4},{6,7},{7,6},{8,9},{9,8},{10,11... | collective-permute-start | bytes 3538952 | tf_op jit(solution)/shard_map/ppermute | solution.py:328
  74.3 16.6 %collective-permute-start.12 = (bf16[768,768]{1,0:T(8,128)(2,1)S(1)}, bf16[768,768]{1,0:T(8,128)(2,1)S(1)}, u32[]{:S(2)}, u32[]{:S(2)}) collective-permute-start(bf16[768,768]{1,0:T(8,128)(2,1)S(1)} %pad_maximum_fusion.2), channel_id=1, source_target_pairs={{0,4},{1,3},{2,6},{3,1},{4,0},{5,7},{6,2},{7,5},{8,12},{9,11},{10,... | collective-permute-start | bytes 3538952 | tf_op jit(solution)/shard_map/ppermute | solution.py:328
  75.5 15.3 %collective-permute-start.14 = (bf16[384,768]{1,0:T(8,128)(2,1)S(1)}, bf16[384,768]{1,0:T(8,128)(2,1)S(1)}, u32[]{:S(2)}, u32[]{:S(2)}) collective-permute-start(bf16[384,768]{1,0:T(8,128)(2,1)S(1)} %pad_maximum_fusion.8), channel_id=1, source_target_pairs={{0,8},{1,9},{2,10},{3,11},{4,12},{5,13},{6,14},{7,15},{8,0},{9,1},... | collective-permute-start | bytes 1769480 | tf_op jit(solution)/shard_map/ppermute | solution.py:328
  92.2 10.9 %copy-start.15 = (bf16[768,768]{1,0:T(8,128)(2,1)}, bf16[768,768]{1,0:T(8,128)(2,1)S(1)}, u32[]{:S(2)}) copy-start(bf16[768,768]{1,0:T(8,128)(2,1)S(1)} %pad_maximum_fusion.3) | copy-start | bytes 3538948
  92.2 11.0 %collective-permute-start.17 = (bf16[768,768]{1,0:T(8,128)(2,1)S(1)}, bf16[768,768]{1,0:T(8,128)(2,1)S(1)}, u32[]{:S(2)}, u32[]{:S(2)}) collective-permute-start(bf16[768,768]{1,0:T(8,128)(2,1)S(1)} %collective-permute-done.12), channel_id=1, source_target_pairs={{0,1},{1,0},{2,3},{3,2},{4,5},{5,4},{6,7},{7,6},{8,9},{9,8},{10,11... | collective-permute-start | bytes 3538952 | tf_op jit(solution)/shard_map/ppermute | solution.py:328
  92.7 10.5 %collective-permute-start.16 = (bf16[768,768]{1,0:T(8,128)(2,1)S(1)}, bf16[768,768]{1,0:T(8,128)(2,1)S(1)}, u32[]{:S(2)}, u32[]{:S(2)}) collective-permute-start(bf16[768,768]{1,0:T(8,128)(2,1)S(1)} %pad_maximum_fusion.3), channel_id=1, source_target_pairs={{0,1},{1,0},{2,3},{3,2},{4,5},{5,4},{6,7},{7,6},{8,9},{9,8},{10,11... | collective-permute-start | bytes 3538952 | tf_op jit(solution)/shard_map/ppermute | solution.py:328
  92.8 15.5 %collective-permute-start.15 = (bf16[768,768]{1,0:T(8,128)(2,1)S(1)}, bf16[768,768]{1,0:T(8,128)(2,1)}, u32[]{:S(2)}, u32[]{:S(2)}) collective-permute-start(bf16[768,768]{1,0:T(8,128)(2,1)S(1)} %pad_maximum_fusion.3), channel_id=1, source_target_pairs={{0,4},{1,3},{2,6},{3,1},{4,0},{5,7},{6,2},{7,5},{8,12},{9,11},{10,... | collective-permute-start | bytes 3538952 | tf_op jit(solution)/shard_map/ppermute | solution.py:328
  103.2 9.0 %copy-start.30 = (bf16[768,768]{1,0:T(8,128)(2,1)}, bf16[768,768]{1,0:T(8,128)(2,1)S(1)}, u32[]{:S(2)}) copy-start(bf16[768,768]{1,0:T(8,128)(2,1)S(1)} %collective-permute-done.17) | copy-start | bytes 3538948
  103.2 9.0 %copy-start.31 = (bf16[768,768]{1,0:T(8,128)(2,1)}, bf16[768,768]{1,0:T(8,128)(2,1)S(1)}, u32[]{:S(2)}) copy-start(bf16[768,768]{1,0:T(8,128)(2,1)S(1)} %collective-permute-done.16) | copy-start | bytes 3538948
  108.2 4.0 %collective-permute-start.18 = (bf16[768,768]{1,0:T(8,128)(2,1)}, bf16[768,768]{1,0:T(8,128)(2,1)S(1)}, u32[]{:S(2)}, u32[]{:S(2)}) collective-permute-start(bf16[768,768]{1,0:T(8,128)(2,1)} %collective-permute-done.15), channel_id=1, source_target_pairs={{0,1},{1,0},{2,3},{3,2},{4,5},{5,4},{6,7},{7,6},{8,9},{9,8},{10,11... | collective-permute-start | bytes 3538952 | tf_op jit(solution)/shard_map/ppermute | solution.py:328
  162.4 7.0 %collective-permute-start.19 = (bf16[784,768]{1,0:T(8,128)(2,1)}, bf16[784,768]{1,0:T(8,128)(2,1)S(1)}, u32[]{:S(2)}, u32[]{:S(2)}) collective-permute-start(bf16[784,768]{1,0:T(8,128)(2,1)} %get-tuple-element.226), channel_id=1, source_target_pairs={{0,1},{1,0},{2,3},{3,2},{4,5},{5,4},{6,7},{7,6},{8,9},{9,8},{10,11... | collective-permute-start | bytes 3612680 | tf_op jit(solution)/shard_map/ppermute | solution.py:328
  162.9 6.5 %collective-permute-start.20 = (bf16[768,768]{1,0:T(8,128)(2,1)}, bf16[768,768]{1,0:T(8,128)(2,1)S(1)}, u32[]{:S(2)}, u32[]{:S(2)}) collective-permute-start(bf16[768,768]{1,0:T(8,128)(2,1)} %get-tuple-element.227), channel_id=1, source_target_pairs={{0,1},{1,0},{2,3},{3,2},{4,5},{5,4},{6,7},{7,6},{8,9},{9,8},{10,11... | collective-permute-start | bytes 3538952 | tf_op jit(solution)/shard_map/ppermute | solution.py:328
  163.0 6.4 %copy-start.21 = (f32[16,768]{1,0:T(8,128)S(1)}, f32[16,768]{1,0:T(8,128)}, u32[]{:S(2)}) copy-start(f32[16,768]{1,0:T(8,128)} %get-tuple-element.220.sums_ref) | copy-start | bytes 147460
  163.0 7.4 %copy-start.13 = (bf16[768,768]{1,0:T(8,128)(2,1)S(1)}, bf16[768,768]{1,0:T(8,128)(2,1)}, u32[]{:S(2)}) copy-start(bf16[768,768]{1,0:T(8,128)(2,1)} %get-tuple-element.225) | copy-start | bytes 3538948
  170.8 1.6 copy-start.10
  170.9 15.7 %collective-permute-start.21 = (bf16[784,768]{1,0:T(8,128)(2,1)S(1)}, bf16[784,768]{1,0:T(8,128)(2,1)S(1)}, u32[]{:S(2)}, u32[]{:S(2)}) collective-permute-start(bf16[784,768]{1,0:T(8,128)(2,1)S(1)} %pad_maximum_fusion.1), channel_id=1, source_target_pairs={{0,4},{1,3},{2,6},{3,1},{4,0},{5,7},{6,2},{7,5},{8,12},{9,11},{10,... | collective-permute-start | bytes 3612680 | tf_op jit(solution)/shard_map/ppermute | solution.py:328
  172.0 13.0 %collective-permute-start.22 = (bf16[768,768]{1,0:T(8,128)(2,1)S(1)}, bf16[768,768]{1,0:T(8,128)(2,1)S(1)}, u32[]{:S(2)}, u32[]{:S(2)}) collective-permute-start(bf16[768,768]{1,0:T(8,128)(2,1)S(1)} %copy-done.11), channel_id=1, source_target_pairs={{0,1},{1,0},{2,3},{3,2},{4,5},{5,4},{6,7},{7,6},{8,9},{9,8},{10,11... | collective-permute-start | bytes 3538952 | tf_op jit(solution)/shard_map/ppermute | solution.py:328
  172.4 12.6 %collective-permute-start.23 = (bf16[768,768]{1,0:T(8,128)(2,1)S(1)}, bf16[768,768]{1,0:T(8,128)(2,1)S(1)}, u32[]{:S(2)}, u32[]{:S(2)}) collective-permute-start(bf16[768,768]{1,0:T(8,128)(2,1)S(1)} %copy-done.10), channel_id=1, source_target_pairs={{0,1},{1,0},{2,3},{3,2},{4,5},{5,4},{6,7},{7,6},{8,9},{9,8},{10,11... | collective-permute-start | bytes 3538952 | tf_op jit(solution)/shard_map/ppermute | solution.py:328
  186.6 2.2 copy-start.7
  189.1 15.4 %collective-permute-start.24 = (bf16[768,768]{1,0:T(8,128)(2,1)S(1)}, bf16[768,768]{1,0:T(8,128)(2,1)S(1)}, u32[]{:S(2)}, u32[]{:S(2)}) collective-permute-start(bf16[768,768]{1,0:T(8,128)(2,1)S(1)} %add_convert_fusion.1), channel_id=1, source_target_pairs={{0,4},{1,3},{2,6},{3,1},{4,0},{5,7},{6,2},{7,5},{8,12},{9,11},{10,... | collective-permute-start | bytes 3538952 | tf_op jit(solution)/shard_map/ppermute | solution.py:328
  189.4 13.8 %collective-permute-start.25 = (bf16[400,768]{1,0:T(8,128)(2,1)S(1)}, bf16[400,768]{1,0:T(8,128)(2,1)S(1)}, u32[]{:S(2)}, u32[]{:S(2)}) collective-permute-start(bf16[400,768]{1,0:T(8,128)(2,1)S(1)} %pad_maximum_fusion.5), channel_id=1, source_target_pairs={{0,8},{1,9},{2,10},{3,11},{4,12},{5,13},{6,14},{7,15},{8,0},{9,1},... | collective-permute-start | bytes 1843208 | tf_op jit(solution)/shard_map/ppermute | solution.py:328
  203.2 21.6 %copy-start.18 = (bf16[400,768]{1,0:T(8,128)(2,1)}, bf16[400,768]{1,0:T(8,128)(2,1)S(1)}, u32[]{:S(2)}) copy-start(bf16[400,768]{1,0:T(8,128)(2,1)S(1)} %collective-permute-done.25) | copy-start | bytes 1843204
  206.2 18.6 %collective-permute-start.27 = (bf16[384,768]{1,0:T(8,128)(2,1)S(1)}, bf16[384,768]{1,0:T(8,128)(2,1)S(1)}, u32[]{:S(2)}, u32[]{:S(2)}) collective-permute-start(bf16[384,768]{1,0:T(8,128)(2,1)S(1)} %get-tuple-element.275), channel_id=1, source_target_pairs={{0,2},{1,5},{2,0},{3,7},{4,6},{5,1},{6,4},{7,3},{8,10},{9,13},{10,... | collective-permute-start | bytes 1769480 | tf_op jit(solution)/shard_map/ppermute | solution.py:328
  216.0 10.5 %collective-permute-start.26 = (bf16[768,768]{1,0:T(8,128)(2,1)}, bf16[768,768]{1,0:T(8,128)(2,1)S(1)}, u32[]{:S(2)}, u32[]{:S(2)}) collective-permute-start(bf16[768,768]{1,0:T(8,128)(2,1)} %get-tuple-element.274), channel_id=1, source_target_pairs={{0,1},{1,0},{2,3},{3,2},{4,5},{5,4},{6,7},{7,6},{8,9},{9,8},{10,11... | collective-permute-start | bytes 3538952 | tf_op jit(solution)/shard_map/ppermute | solution.py:328
  218.7 6.1 %collective-permute-start.28 = (bf16[208,768]{1,0:T(8,128)(2,1)S(1)}, bf16[208,768]{1,0:T(8,128)(2,1)S(1)}, u32[]{:S(2)}, u32[]{:S(2)}) collective-permute-start(bf16[208,768]{1,0:T(8,128)(2,1)S(1)} %pad_maximum_fusion.10), channel_id=1, source_target_pairs={{0,2},{1,5},{2,0},{3,7},{4,6},{5,1},{6,4},{7,3},{8,10},{9,13},{10,... | collective-permute-start | bytes 958472 | tf_op jit(solution)/shard_map/ppermute | solution.py:328
  218.9 24.2 %collective-permute-start.30 = (bf16[768,768]{1,0:T(8,128)(2,1)}, bf16[768,768]{1,0:T(8,128)(2,1)S(1)}, u32[]{:S(2)}, u32[]{:S(2)}) collective-permute-start(bf16[768,768]{1,0:T(8,128)(2,1)} %get-tuple-element.286), channel_id=1, source_target_pairs={{0,1},{1,0},{2,3},{3,2},{4,5},{5,4},{6,7},{7,6},{8,9},{9,8},{10,11... | collective-permute-start | bytes 3538952 | tf_op jit(solution)/shard_map/ppermute | solution.py:328
  224.8 1.6 copy-start.19
  224.8 1.6 copy-start.12
  226.7 16.4 %collective-permute-start.29 = (bf16[768,768]{1,0:T(8,128)(2,1)S(1)}, bf16[768,768]{1,0:T(8,128)(2,1)S(1)}, u32[]{:S(2)}, u32[]{:S(2)}) collective-permute-start(bf16[768,768]{1,0:T(8,128)(2,1)S(1)} %add_convert_fusion), channel_id=1, source_target_pairs={{0,4},{1,3},{2,6},{3,1},{4,0},{5,7},{6,2},{7,5},{8,12},{9,11},{10,... | collective-permute-start | bytes 3538952 | tf_op jit(solution)/shard_map/ppermute | solution.py:328
  227.7 15.5 %collective-permute-start.32 = (bf16[112,768]{1,0:T(8,128)(2,1)}, bf16[112,768]{1,0:T(8,128)(2,1)S(1)}, u32[]{:S(2)}, u32[]{:S(2)}) collective-permute-start(bf16[112,768]{1,0:T(8,128)(2,1)} %pad_maximum_fusion.13), channel_id=1, source_target_pairs={{0,16},{1,17},{2,18},{3,19},{4,20},{5,21},{6,22},{7,23},{8,24},{9,... | collective-permute-start | bytes 516104 | tf_op jit(solution)/shard_map/ppermute | solution.py:328
  230.1 13.1 %collective-permute-start.31 = (bf16[192,768]{1,0:T(8,128)(2,1)}, bf16[192,768]{1,0:T(8,128)(2,1)}, u32[]{:S(2)}, u32[]{:S(2)}) collective-permute-start(bf16[192,768]{1,0:T(8,128)(2,1)} %get-tuple-element.287), channel_id=1, source_target_pairs={{0,8},{1,9},{2,10},{3,11},{4,12},{5,13},{6,14},{7,15},{8,0},{9,1},... | collective-permute-start | bytes 884744 | tf_op jit(solution)/shard_map/ppermute | solution.py:328
  231.5 12.6 %copy-start.16 = (bf16[768,768]{1,0:T(8,128)(2,1)S(1)}, bf16[768,768]{1,0:T(8,128)(2,1)}, u32[]{:S(2)}) copy-start(bf16[768,768]{1,0:T(8,128)(2,1)} %get-tuple-element.284) | copy-start | bytes 3538948
  245.0 10.3 %collective-permute-start.33 = (bf16[400,768]{1,0:T(8,128)(2,1)S(1)}, bf16[400,768]{1,0:T(8,128)(2,1)S(1)}, u32[]{:S(2)}, u32[]{:S(2)}) collective-permute-start(bf16[400,768]{1,0:T(8,128)(2,1)S(1)} %pad_maximum_fusion.6), channel_id=1, source_target_pairs={{0,2},{1,5},{2,0},{3,7},{4,6},{5,1},{6,4},{7,3},{8,10},{9,13},{10,... | collective-permute-start | bytes 1843208 | tf_op jit(solution)/shard_map/ppermute | solution.py:328
  246.3 9.1 %collective-permute-start.34 = (bf16[96,768]{1,0:T(8,128)(2,1)S(1)}, bf16[96,768]{1,0:T(8,128)(2,1)S(1)}, u32[]{:S(2)}, u32[]{:S(2)}) collective-permute-start(bf16[96,768]{1,0:T(8,128)(2,1)S(1)} %add_convert_fusion.19), channel_id=1, source_target_pairs={{0,16},{1,17},{2,18},{3,19},{4,20},{5,21},{6,22},{7,23},{8,24},{9,... | collective-permute-start | bytes 442376 | tf_op jit(solution)/shard_map/ppermute | solution.py:328
  255.5 8.7 %copy-start.20 = (bf16[208,768]{1,0:T(8,128)(2,1)S(1)}, bf16[208,768]{1,0:T(8,128)(2,1)}, u32[]{:S(2)}) copy-start(bf16[208,768]{1,0:T(8,128)(2,1)} %copy-done.19) | copy-start | bytes 958468
  255.5 2.7 collective-permute-start.36
  256.1 6.5 %collective-permute-start.35 = (bf16[192,768]{1,0:T(8,128)(2,1)S(1)}, bf16[192,768]{1,0:T(8,128)(2,1)S(1)}, u32[]{:S(2)}, u32[]{:S(2)}) collective-permute-start(bf16[192,768]{1,0:T(8,128)(2,1)S(1)} %get-tuple-element.300), channel_id=1, source_target_pairs={{0,8},{1,9},{2,10},{3,11},{4,12},{5,13},{6,14},{7,15},{8,0},{9,1},... | collective-permute-start | bytes 884744 | tf_op jit(solution)/shard_map/ppermute | solution.py:328
  258.3 4.0 %collective-permute-start.37 = (bf16[16,768]{1,0:T(8,128)(2,1)S(1)}, bf16[16,768]{1,0:T(8,128)(2,1)S(1)}, u32[]{:S(2)}, u32[]{:S(2)}) collective-permute-start(bf16[16,768]{1,0:T(8,128)(2,1)S(1)} %fusion.2), channel_id=1, source_target_pairs={{0,1},{1,0},{2,3},{3,2},{4,5},{5,4},{6,7},{7,6},{8,9},{9,8},{10,11... | collective-permute-start | bytes 73736 | tf_op jit(solution)/shard_map/ppermute | solution.py:328
  262.7 9.4 %collective-permute-start.38 = (bf16[112,768]{1,0:T(8,128)(2,1)S(1)}, bf16[112,768]{1,0:T(8,128)(2,1)S(1)}, u32[]{:S(2)}, u32[]{:S(2)}) collective-permute-start(bf16[112,768]{1,0:T(8,128)(2,1)S(1)} %pad_maximum_fusion.14), channel_id=1, source_target_pairs={{0,16},{1,17},{2,18},{3,19},{4,20},{5,21},{6,22},{7,23},{8,24},{9,... | collective-permute-start | bytes 516104 | tf_op jit(solution)/shard_map/ppermute | solution.py:328
  265.3 12.5 %copy-start.2 = (f32[578,128]{1,0:T(8,128)S(1)}, f32[578,128]{1,0:T(8,128)}, u32[]{:S(2)}) copy-start(f32[578,128]{1,0:T(8,128)} %refs_4_.1) | copy-start | bytes 887812
  265.3 12.5 %copy-start.3 = (f32[1154,128]{1,0:T(8,128)S(1)}, f32[1154,128]{1,0:T(8,128)}, u32[]{:S(2)}) copy-start(f32[1154,128]{1,0:T(8,128)} %refs_8_.1) | copy-start | bytes 1772548
  265.3 12.5 %copy-start.4 = (f32[1154,128]{1,0:T(8,128)S(1)}, f32[1154,128]{1,0:T(8,128)}, u32[]{:S(2)}) copy-start(f32[1154,128]{1,0:T(8,128)} %refs_9_.1) | copy-start | bytes 1772548
  265.3 12.5 %copy-start.5 = (f32[578,128]{1,0:T(8,128)S(1)}, f32[578,128]{1,0:T(8,128)}, u32[]{:S(2)}) copy-start(f32[578,128]{1,0:T(8,128)} %refs_5_.1) | copy-start | bytes 887812
  265.3 12.5 %copy-start.6 = (f32[578,128]{1,0:T(8,128)S(1)}, f32[578,128]{1,0:T(8,128)}, u32[]{:S(2)}) copy-start(f32[578,128]{1,0:T(8,128)} %refs_6_.1) | copy-start | bytes 887812
  272.2 5.5 %collective-permute-start.39 = (f32[128,128]{1,0:T(8,128)S(1)}, f32[128,128]{1,0:T(8,128)S(1)}, u32[]{:S(2)}, u32[]{:S(2)}) collective-permute-start(f32[128,128]{1,0:T(8,128)S(1)} %get-tuple-element.310), channel_id=1, source_target_pairs={{1,0},{2,1},{3,2},{4,3},{5,4},{6,5},{7,6},{8,7},{9,8},{10,9},{11,1... | collective-permute-start | bytes 196616 | tf_op jit(solution)/shard_map/ppermute | solution.py:1404
  (9 other events, 9.9 us)

commit v2 on v1

--- a/solution.py
+++ b/solution.py
@@ -1366,10 +1366,11 @@
     kept_a, sent_a = halve(part_a[0], low_a, got_a)
     small_sum = small_sum + got_b[4 * SLOT :].astype(F32)
     kept_b, sent_b = halve(kept_b, got_b[: 4 * SLOT])
-    sent_a, sent_b, dq = phase(sent_a, add_small(sent_b, small_sum), dq)
+    joined, dq = phase(jnp.concatenate([sent_a, sent_b, small_sum.astype(BF)]), dq)
     part = att_grads(ctx, dob, stream, dq, dk, dv)
     high = exchange(part[3], 4)
-    got_a, got_b, kept = phase(exchange(sent_a, 2), exchange(sent_b, 2), part[0])
+    got, kept = phase(exchange(joined, 2), part[0])
+    got_a, got_b = got[: 4 * SLOT], got[4 * SLOT :]
     kept_a, sent_a = halve(kept_a, got_a)
     small_sum = small_sum + got_b[2 * SLOT :].astype(F32)
     kept_b, sent_b = halve(kept_b, got_b[: 2 * SLOT])

time: 281 us -> 278 us (0.989)
  waiting for transfers between devices: 80.2 us -> 76.8 us
    ppermute x38 -> x37, waiting for transfers between devices: 75.1 us -> 71.2 us  [exchange(): return lax.ppermute(array, 'fsdp', stage_perm(stage))]
    ppermute x38 -> x37, starting transfers between devices: 38.6 us -> 38.7 us  [exchange(): return lax.ppermute(array, 'fsdp', stage_perm(stage))]
  transfers between devices with their start and end apart: 40 -> 39, of which waited for: 21 -> 21; matrix products, arithmetic and copies ran while one was open for 2% -> 2% of each run, Pallas kernels for 29% -> 30%
where the time goes in v2:
time: 278 us; the launch traced here: 276 us
  Pallas kernels  135 us (49%)
  waiting for transfers between devices  76.8 us (28%)
  starting transfers between devices  43.9 us (16%)
  other arithmetic  10.6 us (4%)
  local copies, waits for them, and re-layouts  8.05 us (3%)
    ppermute x37, waiting for transfers between devices, exchange(): return lax.ppermute(array, 'fsdp', stage_perm(stage))  71.2 us
    ppermute x37, starting transfers between devices, exchange(): return lax.ppermute(array, 'fsdp', stage_perm(stage))  38.7 us
    pallas_call x1, Pallas kernels, feed_forward(): pl.pallas_call(ffn_kernel, grid=(tok // FFN_TILE,), out_shape=(bf(width),...  35.5 us
    pallas_call x2, Pallas kernels, attention_backward(): pl.pallas_call(functools.partial(backward_kernel, len(held)), grid=(width...  24.7 us
    pallas_call x2, Pallas kernels, attention_forward(): pl.pallas_call(functools.partial(forward_kernel, len(held)), grid=(pairs...  20.5 us
    pallas_call x1, Pallas kernels, ffn_grads(): pl.pallas_call(ffn_grad_kernel, grid=(6,), out_shape=part_shapes(width, F...  13.7 us
    pallas_call x1, Pallas kernels, input_grads(): pl.pallas_call(input_grad_kernel, grid=(tok // rows,), out_shape=(jax.Sha...  11.6 us
    pallas_call x1, Pallas kernels, project(): pl.pallas_call(project_kernel, grid=(tok // rows,), out_shape=(bf, jax.Sh...  9.72 us
  transfers between devices with their start and end apart: 39, of which 21 were waited for; matrix products, arithmetic and copies ran while one was open for 2% of the time, Pallas kernels for 30%

profile of v2, /device:TPU:7, one launch (start us, length us, event | category | flops | bytes accessed | tf_op | source)
XLA Modules:
  0.0 276.0 jit_solution(8895206058275204995)
XLA Ops:
  0.7 1.5 row_tails.1
  2.2 3.7 %collective-permute-start = (f32[128,128]{1,0:T(8,128)}, f32[128,128]{1,0:T(8,128)S(1)}, u32[]{:S(2)}, u32[]{:S(2)}) collective-permute-start(f32[128,128]{1,0:T(8,128)} %row_tails.1), channel_id=1, source_target_pairs={{0,1},{1,2},{2,3},{3,4},{4,5},{5,6},{6,7},{7,8},{8,9},{9,10},{10,1... | collective-permute-start | bytes 196616 | tf_op jit(solution)/shard_map/ppermute | solution.py:1311
  5.9 1.6 collective-permute-done.tail_ref
  7.5 1.0 copy-done.1
  8.7 2.3 collective-permute-start.1
  12.2 6.4 %collective-permute-done.1 = bf16[112,768]{1,0:T(8,128)(2,1)S(1)} collective-permute-done((bf16[112,768]{1,0:T(8,128)(2,1)S(1)}, bf16[112,768]{1,0:T(8,128)(2,1)S(1)}, u32[]{:S(2)}, u32[]{:S(2)}) %collective-permute-start.1) | collective-permute-done | bytes 172064 | tf_op jit(solution)/shard_map/ppermute | solution.py:328
  18.7 7.4 %collective-permute-done.2 = bf16[208,768]{1,0:T(8,128)(2,1)S(1)} collective-permute-done((bf16[208,768]{1,0:T(8,128)(2,1)S(1)}, bf16[208,768]{1,0:T(8,128)(2,1)S(1)}, u32[]{:S(2)}, u32[]{:S(2)}) %collective-permute-start.2) | collective-permute-done | bytes 319520 | tf_op jit(solution)/shard_map/ppermute | solution.py:328
  26.8 4.2 %collective-permute-start.4 = (bf16[96,768]{1,0:T(8,128)(2,1)S(1)}, bf16[96,768]{1,0:T(8,128)(2,1)S(1)}, u32[]{:S(2)}, u32[]{:S(2)}) collective-permute-start(bf16[96,768]{1,0:T(8,128)(2,1)S(1)} %get-tuple-element.167), channel_id=1, source_target_pairs={{0,16},{1,17},{2,18},{3,19},{4,20},{5,21},{6,22},{7,23},{8,24},{9,... | collective-permute-start | bytes 442376 | tf_op jit(solution)/shard_map/ppermute | solution.py:328
  31.0 6.5 %collective-permute-done.4 = bf16[96,768]{1,0:T(8,128)(2,1)S(1)} collective-permute-done((bf16[96,768]{1,0:T(8,128)(2,1)S(1)}, bf16[96,768]{1,0:T(8,128)(2,1)S(1)}, u32[]{:S(2)}, u32[]{:S(2)}) %collective-permute-start.4) | collective-permute-done | bytes 147488 | tf_op jit(solution)/shard_map/ppermute | solution.py:328
  37.8 1.4 collective-permute-start.6
  40.1 3.1 %collective-permute-start.8 = (bf16[96,768]{1,0:T(8,128)(2,1)S(1)}, bf16[96,768]{1,0:T(8,128)(2,1)S(1)}, u32[]{:S(2)}, u32[]{:S(2)}) collective-permute-start(bf16[96,768]{1,0:T(8,128)(2,1)S(1)} %get-tuple-element.173), channel_id=1, source_target_pairs={{0,16},{1,17},{2,18},{3,19},{4,20},{5,21},{6,22},{7,23},{8,24},{9,... | collective-permute-start | bytes 442376 | tf_op jit(solution)/shard_map/ppermute | solution.py:328
  43.2 5.3 %collective-permute-done.8 = bf16[96,768]{1,0:T(8,128)(2,1)S(1)} collective-permute-done((bf16[96,768]{1,0:T(8,128)(2,1)S(1)}, bf16[96,768]{1,0:T(8,128)(2,1)S(1)}, u32[]{:S(2)}, u32[]{:S(2)}) %collective-permute-start.8) | collective-permute-done | bytes 147488 | tf_op jit(solution)/shard_map/ppermute | solution.py:328
  48.4 2.4 collective-permute-done.7
  50.9 4.0 %collective-permute-done.5.refs_1_ = bf16[784,768]{1,0:T(8,128)(2,1)S(1)} collective-permute-done((bf16[784,768]{1,0:T(8,128)(2,1)S(1)}, bf16[784,768]{1,0:T(8,128)(2,1)S(1)}, u32[]{:S(2)}, u32[]{:S(2)}) %collective-permute-start.5) | collective-permute-done | bytes 1204256 | tf_op jit(solution)/shard_map/ppermute | solution.py:328
  54.9 1.0 collective-permute-start.9
  56.1 5.7 %collective-permute-done.10 = bf16[192,768]{1,0:T(8,128)(2,1)S(1)} collective-permute-done((bf16[192,768]{1,0:T(8,128)(2,1)S(1)}, bf16[192,768]{1,0:T(8,128)(2,1)S(1)}, u32[]{:S(2)}, u32[]{:S(2)}) %collective-permute-start.10) | collective-permute-done | bytes 294944 | tf_op jit(solution)/shard_map/ppermute | solution.py:328
  61.8 1.0 copy-done.27
  63.1 9.7 %project.1 = (bf16[1024,768]{1,0:T(8,128)(2,1)}, bf16[3,1024,768]{2,1,0:T(8,128)(2,1)}, f32[16,768]{1,0:T(8,128)}) custom-call(bf16[1024,768]{1,0:T(8,128)(2,1)} %x_ref, s32[2,1,512]{2,1,0:T(1,128)} %reshape.50.masked_ref, bf16[784,768]{1,0:T(8,128)(2,1)} %copy-done.9, bf16[784,768]{1,0:T(8,128)(2,1)} %copy-done.26, bf16[784,768]{1,0:T(8,128)(2,1)} %copy-done.25, ...), custom_call_target="tpu_custom_call" | custom-call | flops 3623878656 | bytes 16777216 | tf_op jit(solution)/shard_map/project/pallas_call | solution.py:583
  72.9 1.3 collective-permute-start.13
  74.3 1.3 collective-permute-start.12
  76.1 10.3 %attention_forward.2 = (bf16[1024,768]{1,0:T(8,128)(2,1)}, f32[2,6,2,512]{3,2,1,0:T(2,128)}) custom-call(bf16[3,1024,768]{2,1,0:T(8,128)(2,1)} %get-tuple-element.193.q_ref.k_ref.v_ref, bf16[3,1024,768]{2,1,0:T(8,128)(2,1)} %get-tuple-element.193.q_ref.k_ref.v_ref, bf16[3,1024,768]{2,1,0:T(8,128)(2,1)} %get-tuple-element.193.q_ref.k_ref.v_ref, ...), custom_call_target="tpu_custom_call" | custom-call | flops 3221225472 | bytes 4194304 | tf_op jit(solution)/shard_map/attention_forward/pallas_call | solution.py:647
  86.3 4.5 %collective-permute-done.14 = bf16[384,768]{1,0:T(8,128)(2,1)S(1)} collective-permute-done((bf16[384,768]{1,0:T(8,128)(2,1)S(1)}, bf16[384,768]{1,0:T(8,128)(2,1)S(1)}, u32[]{:S(2)}, u32[]{:S(2)}) %collective-permute-start.14) | collective-permute-done | bytes 589856 | tf_op jit(solution)/shard_map/ppermute | solution.py:328
  90.9 0.9 copy-done.28
  92.9 10.3 %attention_forward.3 = (bf16[1024,768]{1,0:T(8,128)(2,1)}, f32[2,6,2,512]{3,2,1,0:T(2,128)}) custom-call(bf16[3,1024,768]{2,1,0:T(8,128)(2,1)} %get-tuple-element.193.q_ref.k_ref.v_ref, bf16[3,1024,768]{2,1,0:T(8,128)(2,1)} %get-tuple-element.193.q_ref.k_ref.v_ref, ...), custom_call_target="tpu_custom_call", output_to_operand_aliasing={{0}: (4, {}), {1}: (5, {})} | custom-call | flops 3221225472 | bytes 4194304 | tf_op jit(solution)/shard_map/attention_forward/pallas_call | solution.py:647
  103.2 5.0 %collective-permute-done.15 = bf16[768,768]{1,0:T(8,128)(2,1)} collective-permute-done((bf16[768,768]{1,0:T(8,128)(2,1)S(1)}, bf16[768,768]{1,0:T(8,128)(2,1)}, u32[]{:S(2)}, u32[]{:S(2)}) %collective-permute-start.15) | collective-permute-done | bytes 1179680 | tf_op jit(solution)/shard_map/ppermute | solution.py:328
  108.2 1.3 collective-permute-start.18
  109.5 2.7 collective-permute-done.18
  112.2 1.0 copy-done.32
  113.2 35.5 %feed_forward.1 = (bf16[1024,768]{1,0:T(8,128)(2,1)}, bf16[1024,768]{1,0:T(8,128)(2,1)}, bf16[1024,3072]{1,0:T(8,128)(2,1)}, bf16[1024,3072]{1,0:T(8,128)(2,1)},...) custom-call(bf16[1024,768]{1,0:T(8,128)(2,1)} %get-tuple-element.186.stre, ...), custom_call_target="tpu_custom_call" | custom-call | flops 19327352832 | bytes 41943040 | tf_op jit(solution)/shard_map/feed_forward/pallas_call | solution.py:799
  148.7 13.7 %ffn_grads.1 = (bf16[768,768]{1,0:T(8,128)(2,1)}, bf16[768,768]{1,0:T(8,128)(2,1)}, bf16[768,768]{1,0:T(8,128)(2,1)}, bf16[768,768]{1,0:T(8,128)(2,1)}, bf16[768...) custom-call(bf16[1024,768]{1,0:T(8,128)(2,1)} %get-tuple-element.214.x_ref, ...), custom_call_target="tpu_custom_call" | custom-call | flops 7247757312 | bytes 25165824 | tf_op jit(solution)/shard_map/ffn_grads/pallas_call | solution.py:950
  163.0 6.3 %ffn_rest.1 = (bf16[768,768]{1,0:T(8,128)(2,1)}, bf16[768,768]{1,0:T(8,128)(2,1)}, bf16[768,768]{1,0:T(8,128)(2,1)}, bf16[768,768]{1,0:T(8,128)(2,1)}) custom-call(bf16[1024,768]{1,0:T(8,128)(2,1)} %get-tuple-element.214.x_ref, ...), custom_call_target="tpu_custom_call", output_to_operand_aliasing={{0}: (2, {}), {1}: (3, {}), {2}: (4, {}), {3}: (5, {})} | custom-call | flops 2415919104 | bytes 8388608 | tf_op jit(solution)/shard_map/ffn_rest/pallas_call | solution.py:985
  169.4 1.0 copy-done.18
  171.1 0.9 copy-done.11
  172.7 12.4 %attention_backward.2 = (bf16[1024,768]{1,0:T(8,128)(2,1)}, bf16[1024,768]{1,0:T(8,128)(2,1)}, bf16[1024,768]{1,0:T(8,128)(2,1)}) custom-call(bf16[3,1024,768]{2,1,0:T(8,128)(2,1)} %get-tuple-element.193.q_ref.k_ref.v_ref, bf16[3,1024,768]{2,1,0:T(8,128)(2,1)} %get-tuple-element.193.q_ref.k_ref.v_ref, ...), custom_call_target="tpu_custom_call" | custom-call | flops 8053063680 | bytes 6291456 | tf_op jit(solution)/shard_map/attention_backward/pallas_call | solution.py:1057
  185.2 1.4 collective-permute-done.21
  186.6 1.8 add_convert_fusion.6
  189.1 0.8 collective-permute-start.25
  189.9 12.3 %attention_backward.3 = (bf16[1024,768]{1,0:T(8,128)(2,1)}, bf16[1024,768]{1,0:T(8,128)(2,1)}, bf16[1024,768]{1,0:T(8,128)(2,1)}) custom-call(bf16[3,1024,768]{2,1,0:T(8,128)(2,1)} %get-tuple-element.193.q_ref.k_ref.v_ref, bf16[3,1024,768]{2,1,0:T(8,128)(2,1)} %get-tuple-element.193.q_ref.k_ref.v_ref, ...), custom_call_target="tpu_custom_call", output_to_operand_aliasing={{0}: (6, {}), {1}: (7, {}), {2}: (8, {})} | custom-call | flops 8053063680 | bytes 6291456 | tf_op jit(solution)/shard_map/attention_backward/pallas_call | solution.py:1057
  202.1 0.7 collective-permute-done.25
  202.9 1.4 collective-permute-done.24
  204.4 1.7 add_convert_fusion.5
  206.5 9.4 %att_grads.1 = (bf16[768,768]{1,0:T(8,128)(2,1)}, bf16[768,768]{1,0:T(8,128)(2,1)}, bf16[768,768]{1,0:T(8,128)(2,1)}, bf16[768,768]{1,0:T(8,128)(2,1)}) custom-call(bf16[1024,768]{1,0:T(8,128)(2,1)} %get-tuple-element.206.ctx_ref.refs_0_, bf16[1024,768]{1,0:T(8,128)(2,1)} %get-tuple-element.213.refs_1_.dob_ref, ...), custom_call_target="tpu_custom_call" | custom-call | flops 4831838208 | bytes 16777216 | tf_op jit(solution)/shard_map/att_grads/pallas_call | solution.py:1164
  215.9 2.5 collective-permute-start.26
  218.8 0.7 pad_maximum_fusion.13
  219.5 0.9 add_convert_fusion.11
  220.3 0.8 collective-permute-done.26
  221.4 1.2 collective-permute-start.28
  222.6 3.0 %collective-permute-start.31 = (bf16[112,768]{1,0:T(8,128)(2,1)}, bf16[112,768]{1,0:T(8,128)(2,1)S(1)}, u32[]{:S(2)}, u32[]{:S(2)}) collective-permute-start(bf16[112,768]{1,0:T(8,128)(2,1)} %pad_maximum_fusion.13), channel_id=1, source_target_pairs={{0,16},{1,17},{2,18},{3,19},{4,20},{5,21},{6,22},{7,23},{8,24},{9,... | collective-permute-start | bytes 516104 | tf_op jit(solution)/shard_map/ppermute | solution.py:328
  225.5 0.9 collective-permute-start.30
  226.5 11.6 %input_grads.1 = (f32[1024,768]{1,0:T(8,128)}, f32[16,768]{1,0:T(8,128)}) custom-call(bf16[1024,768]{1,0:T(8,128)(2,1)} %get-tuple-element.278.refs_3_.dq_ref, bf16[1024,768]{1,0:T(8,128)(2,1)} %get-tuple-element.269.refs_4_.dk_ref, bf16[1024,768]{1,0:T(8,128)(2,1)} %get-tuple-element.270.refs_5_.dv_ref, ...), custom_call_target="tpu_custom_call" | custom-call | flops 3623878656 | bytes 16777216 | tf_op jit(solution)/shard_map/input_grads/pallas_call | solution.py:1108
  238.1 1.0 add_convert_fusion.19
  240.0 1.3 collective-permute-start.32
  241.2 1.0 collective-permute-start.33
  242.3 7.2 %collective-permute-done.33 = bf16[96,768]{1,0:T(8,128)(2,1)S(1)} collective-permute-done((bf16[96,768]{1,0:T(8,128)(2,1)S(1)}, bf16[96,768]{1,0:T(8,128)(2,1)S(1)}, u32[]{:S(2)}, u32[]{:S(2)}) %collective-permute-start.33) | collective-permute-done | bytes 147488 | tf_op jit(solution)/shard_map/ppermute | solution.py:328
  250.3 2.7 collective-permute-done.35
  253.1 4.6 %collective-permute-start.36 = (bf16[16,768]{1,0:T(8,128)(2,1)S(1)}, bf16[16,768]{1,0:T(8,128)(2,1)S(1)}, u32[]{:S(2)}, u32[]{:S(2)}) collective-permute-start(bf16[16,768]{1,0:T(8,128)(2,1)S(1)} %fusion.2), channel_id=1, source_target_pairs={{0,1},{1,0},{2,3},{3,2},{4,5},{5,4},{6,7},{7,6},{8,9},{9,8},{10,11... | collective-permute-start | bytes 73736 | tf_op jit(solution)/shard_map/ppermute | solution.py:328
  257.7 0.8 collective-permute-done.36
  258.6 1.7 collective-permute-start.37
  260.3 1.1 convert_add_fusion
  261.6 0.9 convert_add_fusion.3
  262.5 6.0 %collective-permute-done.37.got_ref = bf16[112,768]{1,0:T(8,128)(2,1)S(1)} collective-permute-done((bf16[112,768]{1,0:T(8,128)(2,1)S(1)}, bf16[112,768]{1,0:T(8,128)(2,1)S(1)}, u32[]{:S(2)}, u32[]{:S(2)}) %collective-permute-start.37) | collective-permute-done | bytes 172064 | tf_op jit(solution)/shard_map/ppermute | solution.py:328
  268.5 1.5 collective-permute-start.38
  270.0 4.0 %collective-permute-done.38.refs_2_ = f32[128,128]{1,0:T(8,128)S(1)} collective-permute-done((f32[128,128]{1,0:T(8,128)S(1)}, f32[128,128]{1,0:T(8,128)S(1)}, u32[]{:S(2)}, u32[]{:S(2)}) %collective-permute-start.38) | collective-permute-done | bytes 65568 | tf_op jit(solution)/shard_map/ppermute | solution.py:1405
  274.1 1.9 update.1
  (144 shorter events, 11.5 us)
Async XLA Ops:
  0.6 6.8 %copy-start = (f32[1154,128]{1,0:T(8,128)S(1)}, f32[1154,128]{1,0:T(8,128)}, u32[]{:S(2)}) copy-start(f32[1154,128]{1,0:T(8,128)} %refs_7_.1) | copy-start | bytes 1772548
  0.7 10.3 %copy-start.23 = (s32[2,512]{1,0:T(2,128)S(1)}, s32[2,512]{1,0:T(2,128)}, u32[]{:S(2)}) copy-start(s32[2,512]{1,0:T(2,128)} %param.11) | copy-start | bytes 12292
  0.7 10.9 %copy-start.24 = (s32[2,512]{1,0:T(2,128)S(1)}, s32[2,512]{1,0:T(2,128)}, u32[]{:S(2)}) copy-start(s32[2,512]{1,0:T(2,128)} %param.12) | copy-start | bytes 12292
  2.2 5.3 %collective-permute-start = (f32[128,128]{1,0:T(8,128)}, f32[128,128]{1,0:T(8,128)S(1)}, u32[]{:S(2)}, u32[]{:S(2)}) collective-permute-start(f32[128,128]{1,0:T(8,128)} %row_tails.1), channel_id=1, source_target_pairs={{0,1},{1,2},{2,3},{3,4},{4,5},{5,6},{6,7},{7,8},{8,9},{9,10},{10,1... | collective-permute-start | bytes 196616 | tf_op jit(solution)/shard_map/ppermute | solution.py:1311
  8.7 9.9 %collective-permute-start.1 = (bf16[112,768]{1,0:T(8,128)(2,1)S(1)}, bf16[112,768]{1,0:T(8,128)(2,1)S(1)}, u32[]{:S(2)}, u32[]{:S(2)}) collective-permute-start(bf16[112,768]{1,0:T(8,128)(2,1)S(1)} %get-tuple-element.163), channel_id=1, source_target_pairs={{0,16},{1,17},{2,18},{3,19},{4,20},{5,21},{6,22},{7,23},{8,24},{9,... | collective-permute-start | bytes 516104 | tf_op jit(solution)/shard_map/ppermute | solution.py:328
  18.6 7.5 %collective-permute-start.2 = (bf16[208,768]{1,0:T(8,128)(2,1)S(1)}, bf16[208,768]{1,0:T(8,128)(2,1)S(1)}, u32[]{:S(2)}, u32[]{:S(2)}) collective-permute-start(bf16[208,768]{1,0:T(8,128)(2,1)S(1)} %pad_maximum_fusion.10), channel_id=1, source_target_pairs={{0,8},{1,9},{2,10},{3,11},{4,12},{5,13},{6,14},{7,15},{8,0},{9,1},... | collective-permute-start | bytes 958472 | tf_op jit(solution)/shard_map/ppermute | solution.py:328
  26.2 11.4 %collective-permute-start.3 = (bf16[400,768]{1,0:T(8,128)(2,1)S(1)}, bf16[400,768]{1,0:T(8,128)(2,1)S(1)}, u32[]{:S(2)}, u32[]{:S(2)}) collective-permute-start(bf16[400,768]{1,0:T(8,128)(2,1)S(1)} %pad_maximum_fusion.5), channel_id=1, source_target_pairs={{0,2},{1,5},{2,0},{3,7},{4,6},{5,1},{6,4},{7,3},{8,10},{9,13},{10,... | collective-permute-start | bytes 1843208 | tf_op jit(solution)/shard_map/ppermute | solution.py:328
  26.8 10.7 %collective-permute-start.4 = (bf16[96,768]{1,0:T(8,128)(2,1)S(1)}, bf16[96,768]{1,0:T(8,128)(2,1)S(1)}, u32[]{:S(2)}, u32[]{:S(2)}) collective-permute-start(bf16[96,768]{1,0:T(8,128)(2,1)S(1)} %get-tuple-element.167), channel_id=1, source_target_pairs={{0,16},{1,17},{2,18},{3,19},{4,20},{5,21},{6,22},{7,23},{8,24},{9,... | collective-permute-start | bytes 442376 | tf_op jit(solution)/shard_map/ppermute | solution.py:328
  37.8 25.1 %copy-start.9 = (bf16[784,768]{1,0:T(8,128)(2,1)}, bf16[784,768]{1,0:T(8,128)(2,1)S(1)}, u32[]{:S(2)}) copy-start(bf16[784,768]{1,0:T(8,128)(2,1)S(1)} %pad_maximum_fusion.refs_0_) | copy-start | bytes 3612676
  37.8 13.1 %collective-permute-start.6 = (bf16[784,768]{1,0:T(8,128)(2,1)S(1)}, bf16[784,768]{1,0:T(8,128)(2,1)S(1)}, u32[]{:S(2)}, u32[]{:S(2)}) collective-permute-start(bf16[784,768]{1,0:T(8,128)(2,1)S(1)} %pad_maximum_fusion.refs_0_), channel_id=1, source_target_pairs={{0,1},{1,0},{2,3},{3,2},{4,5},{5,4},{6,7},{7,6},{8,9},{9,8},{10,11... | collective-permute-start | bytes 3612680 | tf_op jit(solution)/shard_map/ppermute | solution.py:328
  39.2 15.6 %collective-permute-start.5 = (bf16[784,768]{1,0:T(8,128)(2,1)S(1)}, bf16[784,768]{1,0:T(8,128)(2,1)S(1)}, u32[]{:S(2)}, u32[]{:S(2)}) collective-permute-start(bf16[784,768]{1,0:T(8,128)(2,1)S(1)} %pad_maximum_fusion.refs_0_), channel_id=1, source_target_pairs={{0,4},{1,3},{2,6},{3,1},{4,0},{5,7},{6,2},{7,5},{8,12},{9,11},{10,... | collective-permute-start | bytes 3612680 | tf_op jit(solution)/shard_map/ppermute | solution.py:328
  39.4 11.4 %collective-permute-start.7 = (bf16[192,768]{1,0:T(8,128)(2,1)S(1)}, bf16[192,768]{1,0:T(8,128)(2,1)S(1)}, u32[]{:S(2)}, u32[]{:S(2)}) collective-permute-start(bf16[192,768]{1,0:T(8,128)(2,1)S(1)} %pad_maximum_fusion.11), channel_id=1, source_target_pairs={{0,8},{1,9},{2,10},{3,11},{4,12},{5,13},{6,14},{7,15},{8,0},{9,1},... | collective-permute-start | bytes 884744 | tf_op jit(solution)/shard_map/ppermute | solution.py:328
  40.1 8.4 %collective-permute-start.8 = (bf16[96,768]{1,0:T(8,128)(2,1)S(1)}, bf16[96,768]{1,0:T(8,128)(2,1)S(1)}, u32[]{:S(2)}, u32[]{:S(2)}) collective-permute-start(bf16[96,768]{1,0:T(8,128)(2,1)S(1)} %get-tuple-element.173), channel_id=1, source_target_pairs={{0,16},{1,17},{2,18},{3,19},{4,20},{5,21},{6,22},{7,23},{8,24},{9,... | collective-permute-start | bytes 442376 | tf_op jit(solution)/shard_map/ppermute | solution.py:328
  50.9 12.0 %copy-start.25 = (bf16[784,768]{1,0:T(8,128)(2,1)}, bf16[784,768]{1,0:T(8,128)(2,1)S(1)}, u32[]{:S(2)}) copy-start(bf16[784,768]{1,0:T(8,128)(2,1)S(1)} %collective-permute-done.6.refs_2_) | copy-start | bytes 3612676
  54.8 8.3 %copy-start.26 = (bf16[784,768]{1,0:T(8,128)(2,1)}, bf16[784,768]{1,0:T(8,128)(2,1)S(1)}, u32[]{:S(2)}) copy-start(bf16[784,768]{1,0:T(8,128)(2,1)S(1)} %collective-permute-done.5.refs_1_) | copy-start | bytes 3612676
  54.9 6.9 %collective-permute-start.9 = (bf16[784,768]{1,0:T(8,128)(2,1)S(1)}, bf16[784,768]{1,0:T(8,128)(2,1)S(1)}, u32[]{:S(2)}, u32[]{:S(2)}) collective-permute-start(bf16[784,768]{1,0:T(8,128)(2,1)S(1)} %collective-permute-done.5.refs_1_), channel_id=1, source_target_pairs={{0,1},{1,0},{2,3},{3,2},{4,5},{5,4},{6,7},{7,6},{8,9},{9,8},{10,11... | collective-permute-start | bytes 3612680 | tf_op jit(solution)/shard_map/ppermute | solution.py:328
  55.9 5.9 %collective-permute-start.10 = (bf16[192,768]{1,0:T(8,128)(2,1)S(1)}, bf16[192,768]{1,0:T(8,128)(2,1)S(1)}, u32[]{:S(2)}, u32[]{:S(2)}) collective-permute-start(bf16[192,768]{1,0:T(8,128)(2,1)S(1)} %pad_maximum_fusion.12), channel_id=1, source_target_pairs={{0,2},{1,5},{2,0},{3,7},{4,6},{5,1},{6,4},{7,3},{8,10},{9,13},{10,... | collective-permute-start | bytes 884744 | tf_op jit(solution)/shard_map/ppermute | solution.py:328
  62.9 10.0 %collective-permute-start.11 = (bf16[384,768]{1,0:T(8,128)(2,1)S(1)}, bf16[384,768]{1,0:T(8,128)(2,1)S(1)}, u32[]{:S(2)}, u32[]{:S(2)}) collective-permute-start(bf16[384,768]{1,0:T(8,128)(2,1)S(1)} %pad_maximum_fusion.8), channel_id=1, source_target_pairs={{0,2},{1,5},{2,0},{3,7},{4,6},{5,1},{6,4},{7,3},{8,10},{9,13},{10,... | collective-permute-start | bytes 1769480 | tf_op jit(solution)/shard_map/ppermute | solution.py:328
  72.9 13.4 %copy-start.14 = (bf16[768,768]{1,0:T(8,128)(2,1)}, bf16[768,768]{1,0:T(8,128)(2,1)S(1)}, u32[]{:S(2)}) copy-start(bf16[768,768]{1,0:T(8,128)(2,1)S(1)} %pad_maximum_fusion.2) | copy-start | bytes 3538948
  72.9 17.9 %collective-permute-start.13 = (bf16[768,768]{1,0:T(8,128)(2,1)S(1)}, bf16[768,768]{1,0:T(8,128)(2,1)S(1)}, u32[]{:S(2)}, u32[]{:S(2)}) collective-permute-start(bf16[768,768]{1,0:T(8,128)(2,1)S(1)} %pad_maximum_fusion.2), channel_id=1, source_target_pairs={{0,1},{1,0},{2,3},{3,2},{4,5},{5,4},{6,7},{7,6},{8,9},{9,8},{10,11... | collective-permute-start | bytes 3538952 | tf_op jit(solution)/shard_map/ppermute | solution.py:328
  74.3 16.6 %collective-permute-start.12 = (bf16[768,768]{1,0:T(8,128)(2,1)S(1)}, bf16[768,768]{1,0:T(8,128)(2,1)S(1)}, u32[]{:S(2)}, u32[]{:S(2)}) collective-permute-start(bf16[768,768]{1,0:T(8,128)(2,1)S(1)} %pad_maximum_fusion.2), channel_id=1, source_target_pairs={{0,4},{1,3},{2,6},{3,1},{4,0},{5,7},{6,2},{7,5},{8,12},{9,11},{10,... | collective-permute-start | bytes 3538952 | tf_op jit(solution)/shard_map/ppermute | solution.py:328
  75.5 15.3 %collective-permute-start.14 = (bf16[384,768]{1,0:T(8,128)(2,1)S(1)}, bf16[384,768]{1,0:T(8,128)(2,1)S(1)}, u32[]{:S(2)}, u32[]{:S(2)}) collective-permute-start(bf16[384,768]{1,0:T(8,128)(2,1)S(1)} %pad_maximum_fusion.9), channel_id=1, source_target_pairs={{0,8},{1,9},{2,10},{3,11},{4,12},{5,13},{6,14},{7,15},{8,0},{9,1},... | collective-permute-start | bytes 1769480 | tf_op jit(solution)/shard_map/ppermute | solution.py:328
  92.2 10.9 %copy-start.15 = (bf16[768,768]{1,0:T(8,128)(2,1)}, bf16[768,768]{1,0:T(8,128)(2,1)S(1)}, u32[]{:S(2)}) copy-start(bf16[768,768]{1,0:T(8,128)(2,1)S(1)} %pad_maximum_fusion.3) | copy-start | bytes 3538948
  92.2 10.9 %collective-permute-start.17 = (bf16[768,768]{1,0:T(8,128)(2,1)S(1)}, bf16[768,768]{1,0:T(8,128)(2,1)S(1)}, u32[]{:S(2)}, u32[]{:S(2)}) collective-permute-start(bf16[768,768]{1,0:T(8,128)(2,1)S(1)} %collective-permute-done.12), channel_id=1, source_target_pairs={{0,1},{1,0},{2,3},{3,2},{4,5},{5,4},{6,7},{7,6},{8,9},{9,8},{10,11... | collective-permute-start | bytes 3538952 | tf_op jit(solution)/shard_map/ppermute | solution.py:328
  92.7 10.5 %collective-permute-start.16 = (bf16[768,768]{1,0:T(8,128)(2,1)S(1)}, bf16[768,768]{1,0:T(8,128)(2,1)S(1)}, u32[]{:S(2)}, u32[]{:S(2)}) collective-permute-start(bf16[768,768]{1,0:T(8,128)(2,1)S(1)} %pad_maximum_fusion.3), channel_id=1, source_target_pairs={{0,1},{1,0},{2,3},{3,2},{4,5},{5,4},{6,7},{7,6},{8,9},{9,8},{10,11... | collective-permute-start | bytes 3538952 | tf_op jit(solution)/shard_map/ppermute | solution.py:328
  92.8 15.5 %collective-permute-start.15 = (bf16[768,768]{1,0:T(8,128)(2,1)S(1)}, bf16[768,768]{1,0:T(8,128)(2,1)}, u32[]{:S(2)}, u32[]{:S(2)}) collective-permute-start(bf16[768,768]{1,0:T(8,128)(2,1)S(1)} %pad_maximum_fusion.3), channel_id=1, source_target_pairs={{0,4},{1,3},{2,6},{3,1},{4,0},{5,7},{6,2},{7,5},{8,12},{9,11},{10,... | collective-permute-start | bytes 3538952 | tf_op jit(solution)/shard_map/ppermute | solution.py:328
  103.2 9.0 %copy-start.30 = (bf16[768,768]{1,0:T(8,128)(2,1)}, bf16[768,768]{1,0:T(8,128)(2,1)S(1)}, u32[]{:S(2)}) copy-start(bf16[768,768]{1,0:T(8,128)(2,1)S(1)} %collective-permute-done.17) | copy-start | bytes 3538948
  103.2 9.0 %copy-start.31 = (bf16[768,768]{1,0:T(8,128)(2,1)}, bf16[768,768]{1,0:T(8,128)(2,1)S(1)}, u32[]{:S(2)}) copy-start(bf16[768,768]{1,0:T(8,128)(2,1)S(1)} %collective-permute-done.16) | copy-start | bytes 3538948
  108.2 4.0 %collective-permute-start.18 = (bf16[768,768]{1,0:T(8,128)(2,1)}, bf16[768,768]{1,0:T(8,128)(2,1)S(1)}, u32[]{:S(2)}, u32[]{:S(2)}) collective-permute-start(bf16[768,768]{1,0:T(8,128)(2,1)} %collective-permute-done.15), channel_id=1, source_target_pairs={{0,1},{1,0},{2,3},{3,2},{4,5},{5,4},{6,7},{7,6},{8,9},{9,8},{10,11... | collective-permute-start | bytes 3538952 | tf_op jit(solution)/shard_map/ppermute | solution.py:328
  162.4 7.0 %collective-permute-start.19 = (bf16[784,768]{1,0:T(8,128)(2,1)}, bf16[784,768]{1,0:T(8,128)(2,1)S(1)}, u32[]{:S(2)}, u32[]{:S(2)}) collective-permute-start(bf16[784,768]{1,0:T(8,128)(2,1)} %get-tuple-element.224), channel_id=1, source_target_pairs={{0,1},{1,0},{2,3},{3,2},{4,5},{5,4},{6,7},{7,6},{8,9},{9,8},{10,11... | collective-permute-start | bytes 3612680 | tf_op jit(solution)/shard_map/ppermute | solution.py:328
  162.8 6.5 %collective-permute-start.20 = (bf16[768,768]{1,0:T(8,128)(2,1)}, bf16[768,768]{1,0:T(8,128)(2,1)S(1)}, u32[]{:S(2)}, u32[]{:S(2)}) collective-permute-start(bf16[768,768]{1,0:T(8,128)(2,1)} %get-tuple-element.225), channel_id=1, source_target_pairs={{0,1},{1,0},{2,3},{3,2},{4,5},{5,4},{6,7},{7,6},{8,9},{9,8},{10,11... | collective-permute-start | bytes 3538952 | tf_op jit(solution)/shard_map/ppermute | solution.py:328
  163.0 7.4 %copy-start.21 = (f32[16,768]{1,0:T(8,128)S(1)}, f32[16,768]{1,0:T(8,128)}, u32[]{:S(2)}) copy-start(f32[16,768]{1,0:T(8,128)} %get-tuple-element.218.sums_ref) | copy-start | bytes 147460
  163.0 7.4 %copy-start.12 = (bf16[768,768]{1,0:T(8,128)(2,1)S(1)}, bf16[768,768]{1,0:T(8,128)(2,1)}, u32[]{:S(2)}) copy-start(bf16[768,768]{1,0:T(8,128)(2,1)} %get-tuple-element.223) | copy-start | bytes 3538948
  170.8 1.6 copy-start.10
  170.9 15.7 %collective-permute-start.21 = (bf16[784,768]{1,0:T(8,128)(2,1)S(1)}, bf16[784,768]{1,0:T(8,128)(2,1)S(1)}, u32[]{:S(2)}, u32[]{:S(2)}) collective-permute-start(bf16[784,768]{1,0:T(8,128)(2,1)S(1)} %pad_maximum_fusion.1), channel_id=1, source_target_pairs={{0,4},{1,3},{2,6},{3,1},{4,0},{5,7},{6,2},{7,5},{8,12},{9,11},{10,... | collective-permute-start | bytes 3612680 | tf_op jit(solution)/shard_map/ppermute | solution.py:328
  172.0 13.1 %collective-permute-start.22 = (bf16[768,768]{1,0:T(8,128)(2,1)S(1)}, bf16[768,768]{1,0:T(8,128)(2,1)S(1)}, u32[]{:S(2)}, u32[]{:S(2)}) collective-permute-start(bf16[768,768]{1,0:T(8,128)(2,1)S(1)} %copy-done.11), channel_id=1, source_target_pairs={{0,1},{1,0},{2,3},{3,2},{4,5},{5,4},{6,7},{7,6},{8,9},{9,8},{10,11... | collective-permute-start | bytes 3538952 | tf_op jit(solution)/shard_map/ppermute | solution.py:328
  172.4 12.8 %collective-permute-start.23 = (bf16[768,768]{1,0:T(8,128)(2,1)S(1)}, bf16[768,768]{1,0:T(8,128)(2,1)}, u32[]{:S(2)}, u32[]{:S(2)}) collective-permute-start(bf16[768,768]{1,0:T(8,128)(2,1)S(1)} %copy-done.10), channel_id=1, source_target_pairs={{0,1},{1,0},{2,3},{3,2},{4,5},{5,4},{6,7},{7,6},{8,9},{9,8},{10,11... | collective-permute-start | bytes 3538952 | tf_op jit(solution)/shard_map/ppermute | solution.py:328
  172.7 13.8 %copy-start.17 = (bf16[768,768]{1,0:T(8,128)(2,1)S(1)}, bf16[768,768]{1,0:T(8,128)(2,1)}, u32[]{:S(2)}) copy-start(bf16[768,768]{1,0:T(8,128)(2,1)} %get-tuple-element.253) | copy-start | bytes 3538948
  186.6 1.8 copy-start.7
  188.8 15.4 %collective-permute-start.24 = (bf16[768,768]{1,0:T(8,128)(2,1)S(1)}, bf16[768,768]{1,0:T(8,128)(2,1)S(1)}, u32[]{:S(2)}, u32[]{:S(2)}) collective-permute-start(bf16[768,768]{1,0:T(8,128)(2,1)S(1)} %add_convert_fusion.1), channel_id=1, source_target_pairs={{0,4},{1,3},{2,6},{3,1},{4,0},{5,7},{6,2},{7,5},{8,12},{9,11},{10,... | collective-permute-start | bytes 3538952 | tf_op jit(solution)/shard_map/ppermute | solution.py:328
  189.1 13.8 %collective-permute-start.25 = (bf16[400,768]{1,0:T(8,128)(2,1)S(1)}, bf16[400,768]{1,0:T(8,128)(2,1)S(1)}, u32[]{:S(2)}, u32[]{:S(2)}) collective-permute-start(bf16[400,768]{1,0:T(8,128)(2,1)S(1)} %pad_maximum_fusion.6), channel_id=1, source_target_pairs={{0,8},{1,9},{2,10},{3,11},{4,12},{5,13},{6,14},{7,15},{8,0},{9,1},... | collective-permute-start | bytes 1843208 | tf_op jit(solution)/shard_map/ppermute | solution.py:328
  202.1 2.3 copy-start.8
  202.9 15.8 %copy-start.20 = (bf16[400,768]{1,0:T(8,128)(2,1)}, bf16[400,768]{1,0:T(8,128)(2,1)S(1)}, u32[]{:S(2)}) copy-start(bf16[400,768]{1,0:T(8,128)(2,1)S(1)} %collective-permute-done.25) | copy-start | bytes 1843204
  206.2 12.5 %collective-permute-start.27 = (bf16[592,768]{1,0:T(8,128)(2,1)S(1)}, bf16[592,768]{1,0:T(8,128)(2,1)S(1)}, u32[]{:S(2)}, u32[]{:S(2)}) collective-permute-start(bf16[592,768]{1,0:T(8,128)(2,1)S(1)} %pad_maximum_fusion.4), channel_id=1, source_target_pairs={{0,2},{1,5},{2,0},{3,7},{4,6},{5,1},{6,4},{7,3},{8,10},{9,13},{10,... | collective-permute-start | bytes 2727944 | tf_op jit(solution)/shard_map/ppermute | solution.py:328
  215.9 5.2 %collective-permute-start.26 = (bf16[768,768]{1,0:T(8,128)(2,1)}, bf16[768,768]{1,0:T(8,128)(2,1)S(1)}, u32[]{:S(2)}, u32[]{:S(2)}) collective-permute-start(bf16[768,768]{1,0:T(8,128)(2,1)} %get-tuple-element.272), channel_id=1, source_target_pairs={{0,1},{1,0},{2,3},{3,2},{4,5},{5,4},{6,7},{7,6},{8,9},{9,8},{10,11... | collective-permute-start | bytes 3538952 | tf_op jit(solution)/shard_map/ppermute | solution.py:328
  218.4 19.7 %collective-permute-start.29 = (bf16[768,768]{1,0:T(8,128)(2,1)}, bf16[768,768]{1,0:T(8,128)(2,1)S(1)}, u32[]{:S(2)}, u32[]{:S(2)}) collective-permute-start(bf16[768,768]{1,0:T(8,128)(2,1)} %get-tuple-element.282), channel_id=1, source_target_pairs={{0,1},{1,0},{2,3},{3,2},{4,5},{5,4},{6,7},{7,6},{8,9},{9,8},{10,11... | collective-permute-start | bytes 3538952 | tf_op jit(solution)/shard_map/ppermute | solution.py:328
  218.7 1.6 copy-start.19
  218.7 2.4 copy-start.13
  221.4 16.8 %collective-permute-start.28 = (bf16[768,768]{1,0:T(8,128)(2,1)S(1)}, bf16[768,768]{1,0:T(8,128)(2,1)S(1)}, u32[]{:S(2)}, u32[]{:S(2)}) collective-permute-start(bf16[768,768]{1,0:T(8,128)(2,1)S(1)} %add_convert_fusion), channel_id=1, source_target_pairs={{0,4},{1,3},{2,6},{3,1},{4,0},{5,7},{6,2},{7,5},{8,12},{9,11},{10,... | collective-permute-start | bytes 3538952 | tf_op jit(solution)/shard_map/ppermute | solution.py:328
  222.6 15.6 %collective-permute-start.31 = (bf16[112,768]{1,0:T(8,128)(2,1)}, bf16[112,768]{1,0:T(8,128)(2,1)S(1)}, u32[]{:S(2)}, u32[]{:S(2)}) collective-permute-start(bf16[112,768]{1,0:T(8,128)(2,1)} %pad_maximum_fusion.13), channel_id=1, source_target_pairs={{0,16},{1,17},{2,18},{3,19},{4,20},{5,21},{6,22},{7,23},{8,24},{9,... | collective-permute-start | bytes 516104 | tf_op jit(solution)/shard_map/ppermute | solution.py:328
  225.5 12.6 %collective-permute-start.30 = (bf16[192,768]{1,0:T(8,128)(2,1)}, bf16[192,768]{1,0:T(8,128)(2,1)}, u32[]{:S(2)}, u32[]{:S(2)}) collective-permute-start(bf16[192,768]{1,0:T(8,128)(2,1)} %get-tuple-element.283), channel_id=1, source_target_pairs={{0,8},{1,9},{2,10},{3,11},{4,12},{5,13},{6,14},{7,15},{8,0},{9,1},... | collective-permute-start | bytes 884744 | tf_op jit(solution)/shard_map/ppermute | solution.py:328
  226.5 12.6 %copy-start.16 = (bf16[768,768]{1,0:T(8,128)(2,1)S(1)}, bf16[768,768]{1,0:T(8,128)(2,1)}, u32[]{:S(2)}) copy-start(bf16[768,768]{1,0:T(8,128)(2,1)} %get-tuple-element.280) | copy-start | bytes 3538948
  240.0 9.6 %collective-permute-start.32 = (bf16[400,768]{1,0:T(8,128)(2,1)S(1)}, bf16[400,768]{1,0:T(8,128)(2,1)S(1)}, u32[]{:S(2)}, u32[]{:S(2)}) collective-permute-start(bf16[400,768]{1,0:T(8,128)(2,1)S(1)} %pad_maximum_fusion.7), channel_id=1, source_target_pairs={{0,2},{1,5},{2,0},{3,7},{4,6},{5,1},{6,4},{7,3},{8,10},{9,13},{10,... | collective-permute-start | bytes 1843208 | tf_op jit(solution)/shard_map/ppermute | solution.py:328
  241.2 8.3 %collective-permute-start.33 = (bf16[96,768]{1,0:T(8,128)(2,1)S(1)}, bf16[96,768]{1,0:T(8,128)(2,1)S(1)}, u32[]{:S(2)}, u32[]{:S(2)}) collective-permute-start(bf16[96,768]{1,0:T(8,128)(2,1)S(1)} %add_convert_fusion.19), channel_id=1, source_target_pairs={{0,16},{1,17},{2,18},{3,19},{4,20},{5,21},{6,22},{7,23},{8,24},{9,... | collective-permute-start | bytes 442376 | tf_op jit(solution)/shard_map/ppermute | solution.py:328
  249.7 3.4 %collective-permute-start.35 = (bf16[16,768]{1,0:T(8,128)(2,1)S(1)}, bf16[16,768]{1,0:T(8,128)(2,1)S(1)}, u32[]{:S(2)}, u32[]{:S(2)}) collective-permute-start(bf16[16,768]{1,0:T(8,128)(2,1)S(1)} %convert_element_type.343), channel_id=1, source_target_pairs={{0,4},{1,3},{2,6},{3,1},{4,0},{5,7},{6,2},{7,5},{8,12},{9,11},{10,... | collective-permute-start | bytes 73736 | tf_op jit(solution)/shard_map/ppermute | solution.py:328
  250.0 8.5 %collective-permute-start.34 = (bf16[192,768]{1,0:T(8,128)(2,1)S(1)}, bf16[192,768]{1,0:T(8,128)(2,1)S(1)}, u32[]{:S(2)}, u32[]{:S(2)}) collective-permute-start(bf16[192,768]{1,0:T(8,128)(2,1)S(1)} %get-tuple-element.296), channel_id=1, source_target_pairs={{0,8},{1,9},{2,10},{3,11},{4,12},{5,13},{6,14},{7,15},{8,0},{9,1},... | collective-permute-start | bytes 884744 | tf_op jit(solution)/shard_map/ppermute | solution.py:328
  253.1 5.4 %collective-permute-start.36 = (bf16[16,768]{1,0:T(8,128)(2,1)S(1)}, bf16[16,768]{1,0:T(8,128)(2,1)S(1)}, u32[]{:S(2)}, u32[]{:S(2)}) collective-permute-start(bf16[16,768]{1,0:T(8,128)(2,1)S(1)} %fusion.2), channel_id=1, source_target_pairs={{0,1},{1,0},{2,3},{3,2},{4,5},{5,4},{6,7},{7,6},{8,9},{9,8},{10,11... | collective-permute-start | bytes 73736 | tf_op jit(solution)/shard_map/ppermute | solution.py:328
  258.6 9.8 %collective-permute-start.37 = (bf16[112,768]{1,0:T(8,128)(2,1)S(1)}, bf16[112,768]{1,0:T(8,128)(2,1)S(1)}, u32[]{:S(2)}, u32[]{:S(2)}) collective-permute-start(bf16[112,768]{1,0:T(8,128)(2,1)S(1)} %pad_maximum_fusion.14), channel_id=1, source_target_pairs={{0,16},{1,17},{2,18},{3,19},{4,20},{5,21},{6,22},{7,23},{8,24},{9,... | collective-permute-start | bytes 516104 | tf_op jit(solution)/shard_map/ppermute | solution.py:328
  261.4 12.6 %copy-start.2 = (f32[578,128]{1,0:T(8,128)S(1)}, f32[578,128]{1,0:T(8,128)}, u32[]{:S(2)}) copy-start(f32[578,128]{1,0:T(8,128)} %refs_4_.1) | copy-start | bytes 887812
  261.4 12.6 %copy-start.3 = (f32[1154,128]{1,0:T(8,128)S(1)}, f32[1154,128]{1,0:T(8,128)}, u32[]{:S(2)}) copy-start(f32[1154,128]{1,0:T(8,128)} %refs_8_.1) | copy-start | bytes 1772548
  261.4 12.6 %copy-start.4 = (f32[1154,128]{1,0:T(8,128)S(1)}, f32[1154,128]{1,0:T(8,128)}, u32[]{:S(2)}) copy-start(f32[1154,128]{1,0:T(8,128)} %refs_9_.1) | copy-start | bytes 1772548
  261.5 12.6 %copy-start.5 = (f32[578,128]{1,0:T(8,128)S(1)}, f32[578,128]{1,0:T(8,128)}, u32[]{:S(2)}) copy-start(f32[578,128]{1,0:T(8,128)} %refs_5_.1) | copy-start | bytes 887812
  261.5 12.6 %copy-start.6 = (f32[578,128]{1,0:T(8,128)S(1)}, f32[578,128]{1,0:T(8,128)}, u32[]{:S(2)}) copy-start(f32[578,128]{1,0:T(8,128)} %refs_6_.1) | copy-start | bytes 887812
  268.5 5.5 %collective-permute-start.38 = (f32[128,128]{1,0:T(8,128)S(1)}, f32[128,128]{1,0:T(8,128)S(1)}, u32[]{:S(2)}, u32[]{:S(2)}) collective-permute-start(f32[128,128]{1,0:T(8,128)S(1)} %get-tuple-element.306), channel_id=1, source_target_pairs={{1,0},{2,1},{3,2},{4,3},{5,4},{6,5},{7,6},{8,7},{9,8},{10,9},{11,1... | collective-permute-start | bytes 196616 | tf_op jit(solution)/shard_map/ppermute | solution.py:1405
  (8 other events, 8.6 us)
